TPU v7x, 512 devices: a whole 4x8x8 slice. The times are simulated.
512 devices in a mesh: frame: 16 (over y, core), tok: 32 (over x, z).
Axes of the slice: x: 4, y: 8, z: 8, core: 2. Of those that a mesh axis runs over, the one named last changes fastest.
Arguments:
- inputs: bfloat16 [16, 24576, 512], P('frame', 'tok'), may hold values from -16 to 16
- kv_weight: bfloat16 [512, 2048], replicated, may hold values from -0.25 to 0.25
- latent_queries: bfloat16 [1024, 1024], P('tok'), may hold values from -21 to 21
- mix_gain: float32 [3072], replicated, may hold values from 0.5 to 2
- mix_weight: bfloat16 [3072, 1024], P(None, 'tok'), may hold values from -0.109375 to 0.109375
- output_queries: bfloat16 [16, 4096, 1024], P('frame', 'tok'), may hold values from -28 to 28
Outputs:
- decoded: float32 [16, 4096, 1024], P('frame', 'tok')
All inputs are finite; a program needn't handle non-finite values.
Results may differ from a plain program's by a relative error of at most 0.035.
Values may be sent and summed in bfloat16 or wider, within the bound.
No kernel may reach another device: no remote copies, remote signals or barrier semaphores. Data moves between devices by JAX's collectives and lax.ppermute only.
A program may use at most 128 MiB of HBM per device.

v0:
```python
import math

import jax
import jax.numpy as jnp
from jax import lax
from jax.experimental import pallas as pl
from jax.experimental.pallas import tpu as pltpu
from jax.sharding import Mesh
from jax.sharding import PartitionSpec as P


HEADS = 8
HEAD_DIM = 128
EXP2_SCALE = math.log2(math.e) / math.sqrt(HEAD_DIM)
FRAME = ("y", "core")
EXTRA = 16
TAIL = 8
VMEM_BYTES = 32 * 1024 * 1024
INTERPRET = False


def shift(block, axis, distance):
    size = lax.axis_size(axis)
    return lax.ppermute(block, axis, [(i, (i + distance) % size) for i in range(size)])


def from_behind(block, axis, distance):
    devices = range(lax.axis_size(axis))
    route = [(i - distance, i) for i in devices if i - distance in devices]
    return lax.ppermute(block, axis, route)


def gather(block, axis):
    copies = jnp.broadcast_to(block[None], (lax.axis_size(axis),) + block.shape)
    return lax.all_to_all(copies, axis, 0, 0, tiled=True)


def partner(block):
    return lax.ppermute(block, "core", [(0, 1), (1, 0)])


def dot_nt(a, b):
    return lax.dot_general(a, b, (((1,), (1,)), ((), ())), preferred_element_type=jnp.float32)


def head_cols(h):
    return slice(h * HEAD_DIM, (h + 1) * HEAD_DIM)


def project_inputs(in_refs, w_ref, kv_ref):
    low = 0
    for in_ref in in_refs:
        rows = in_ref.shape[0]
        kv_ref[low : low + rows, :] = jnp.dot(
            in_ref[...], w_ref[...], preferred_element_type=jnp.float32
        ).astype(jnp.bfloat16)
        low += rows


def pick_queries(core_ref, mine_ref, other_ref, tile_ref):
    step = pl.program_id(0)
    tile = tile_ref.shape[0]
    per_half = mine_ref.shape[0] // tile
    start = pl.multiple_of((step % per_half) * tile, tile)
    is_mine = step // per_half == core_ref[0]

    @pl.when(is_mine)
    def _():
        tile_ref[...] = mine_ref[pl.ds(start, tile), :]

    @pl.when(jnp.logical_not(is_mine))
    def _():
        tile_ref[...] = other_ref[pl.ds(start, tile), :]


def lanes(values, shape):
    lane = lax.broadcasted_iota(jnp.int32, shape, 1)
    result = jnp.broadcast_to(values[-1], shape)
    for k in range(len(values) - 2, -1, -1):
        result = jnp.where(lane == k, values[k], result)
    return result


def near_body(core_ref, mine_ref, other_ref, w_ref, *refs):
    in_refs, (num_ref, stat_ref, kv_ref, q_ref) = refs[:-4], refs[-4:]
    width = mine_ref.shape[1]

    @pl.when(pl.program_id(0) == 0)
    def _():
        project_inputs(in_refs, w_ref, kv_ref)

    pick_queries(core_ref, mine_ref, other_ref, q_ref)
    tile = q_ref.shape[0]
    for h in range(width // HEAD_DIM):
        cols = head_cols(h)
        scores = dot_nt(q_ref[:, cols], kv_ref[:, cols])
        peak = jnp.max(scores, axis=1, keepdims=True)
        weights = jnp.exp2((scores - peak) * EXP2_SCALE)
        den = jnp.sum(weights, axis=1, keepdims=True)
        value_cols = slice(width + h * HEAD_DIM, width + (h + 1) * HEAD_DIM)
        num_ref[:, cols] = jnp.dot(
            weights.astype(jnp.bfloat16), kv_ref[:, value_cols], preferred_element_type=jnp.float32
        )
        stat_ref[:, cols] = lanes([peak, den], (tile, HEAD_DIM))


def far_body(core_ref, mine_ref, other_ref, w_ref, num_ref, stat_ref, *refs):
    in_refs, (out_ref, kv_ref, q_ref) = refs[:-3], refs[-3:]
    width = mine_ref.shape[1]

    @pl.when(pl.program_id(0) == 0)
    def _():
        project_inputs(in_refs, w_ref, kv_ref)

    pick_queries(core_ref, mine_ref, other_ref, q_ref)
    tile = q_ref.shape[0]
    blocks = out_ref.shape[0]
    rows = tile // blocks
    for h in range(width // HEAD_DIM):
        cols = head_cols(h)
        near_peak = stat_ref[:, h * HEAD_DIM : h * HEAD_DIM + 1]
        near_den = stat_ref[:, h * HEAD_DIM + 1 : h * HEAD_DIM + 2]
        scores = dot_nt(q_ref[:, cols], kv_ref[:, cols])
        peak = jnp.maximum(jnp.max(scores, axis=1, keepdims=True), near_peak)
        weights = jnp.exp2((scores - peak) * EXP2_SCALE)
        rescale = jnp.exp2((near_peak - peak) * EXP2_SCALE)
        den = jnp.sum(weights, axis=1, keepdims=True) + rescale * near_den
        value_cols = slice(width + h * HEAD_DIM, width + (h + 1) * HEAD_DIM)
        num = rescale * num_ref[:, cols] + jnp.dot(
            weights.astype(jnp.bfloat16), kv_ref[:, value_cols], preferred_element_type=jnp.float32
        )
        first = peak.astype(jnp.bfloat16).astype(jnp.float32)
        second = (peak - first).astype(jnp.bfloat16).astype(jnp.float32)
        packed = lanes([first, second, peak - first - second, den], (tile, HEAD_DIM)).T
        for b in range(blocks):
            span = slice(b * rows, (b + 1) * rows)
            out_ref[b, :rows, cols] = num[span].astype(jnp.bfloat16)
            out_ref[b, rows:, cols] = packed[:EXTRA, span].astype(jnp.bfloat16)


def attend(core, mine, other, weight, near, far, blocks, tile):
    half, width = mine.shape
    latents = 2 * half
    rows = latents // blocks
    scalar = pl.BlockSpec(memory_space=pltpu.SMEM)

    def whole(block):
        return pl.BlockSpec(block.shape, lambda i: (0, 0))

    tiled = pl.BlockSpec((tile, width), lambda i: (i, 0))
    params = pltpu.CompilerParams(vmem_limit_bytes=VMEM_BYTES)
    common = (core, mine, other, weight)
    common_specs = [scalar, whole(mine), whole(other), whole(weight)]
    num, stat = pl.pallas_call(
        near_body,
        grid=(latents // tile,),
        in_specs=common_specs + [whole(block) for block in near],
        out_specs=(tiled, tiled),
        out_shape=(jax.ShapeDtypeStruct((latents, width), jnp.float32),) * 2,
        scratch_shapes=[
            pltpu.VMEM((sum(b.shape[0] for b in near), 2 * width), jnp.bfloat16),
            pltpu.VMEM((tile, width), jnp.bfloat16),
        ],
        compiler_params=params,
        interpret=INTERPRET,
        name="attend_near",
    )(*common, *near)
    return pl.pallas_call(
        far_body,
        grid=(latents // tile,),
        in_specs=common_specs + [tiled, tiled] + [whole(block) for block in far],
        out_specs=pl.BlockSpec((tile // rows, rows + EXTRA, width), lambda i: (i, 0, 0)),
        out_shape=jax.ShapeDtypeStruct((blocks, rows + EXTRA, width), jnp.bfloat16),
        scratch_shapes=[
            pltpu.VMEM((sum(b.shape[0] for b in far), 2 * width), jnp.bfloat16),
            pltpu.VMEM((tile, width), jnp.bfloat16),
        ],
        compiler_params=params,
        interpret=INTERPRET,
        name="attend_far",
    )(*common, num, stat, *far)


def combine_body(part_ref, query_ref, out_ref):
    blocks, height, width = part_ref.shape
    rows = height - EXTRA
    groups = out_ref.shape[0]
    peaks = []
    dens = []
    for b in range(blocks):
        extra = part_ref[b, rows:, :].astype(jnp.float32)
        peaks.append(extra[0:1] + extra[1:2] + extra[2:3])
        dens.append(extra[3:4])
    top = peaks[0]
    for peak in peaks[1:]:
        top = jnp.maximum(top, peak)
    scales = [jnp.exp2((peak - top) * EXP2_SCALE) for peak in peaks]
    den = scales[0] * dens[0]
    for scale, part in zip(scales[1:], dens[1:]):
        den = den + scale * part
    pad = jnp.zeros((HEAD_DIM - blocks - 1, width), jnp.float32)
    table = jnp.concatenate(scales + [den, pad], axis=0)
    for h in range(width // HEAD_DIM):
        cols = head_cols(h)
        turned = table[:, cols].T
        total = jnp.zeros((rows, HEAD_DIM), jnp.float32)
        for b in range(blocks):
            total = total + part_ref[b, :rows, cols].astype(jnp.float32) * turned[:, b : b + 1]
        latents = (total / turned[:, blocks : blocks + 1]).astype(jnp.bfloat16)
        for g in range(groups):
            out_ref[g, :rows, cols] = latents
    for g in range(groups):
        out_ref[g, rows:, :] = query_ref[:, g * width : (g + 1) * width]


def whole_spec(block):
    return pl.BlockSpec(block.shape, lambda i: (0,) * len(block.shape))


def combine(parts, queries, groups):
    _, height, width = parts.shape
    rows = height - EXTRA
    return pl.pallas_call(
        combine_body,
        grid=(1,),
        in_specs=[whole_spec(parts), whole_spec(queries)],
        out_specs=pl.BlockSpec((groups, rows + queries.shape[0], width), lambda i: (0, 0, 0)),
        out_shape=jax.ShapeDtypeStruct((groups, rows + queries.shape[0], width), jnp.bfloat16),
        compiler_params=pltpu.CompilerParams(vmem_limit_bytes=VMEM_BYTES // 2),
        interpret=INTERPRET,
        name="combine",
    )(parts, queries)


def turn(column):
    return jnp.broadcast_to(column, (column.shape[0], HEAD_DIM)).T


def products_body(core_ref, rows_ref, gain_ref, mine_ref, other_ref, own_ref, one_ref, two_ref):
    groups, _, width = rows_ref.shape
    full = groups * width
    half = mine_ref.shape[1]
    count = own_ref.shape[0] - TAIL
    squares = jnp.zeros((count, 1), jnp.float32)
    for g in range(groups):
        block = rows_ref[g, :count].astype(jnp.float32)
        squares = squares + jnp.sum(block * block, axis=1, keepdims=True)
    tail = turn(squares)[:TAIL]
    outs = (own_ref, one_ref, two_ref)
    for out_ref in outs:
        for h in range(width // HEAD_DIM):
            out_ref[count:, head_cols(h)] = tail

    def multiply(halves):
        for t, out_ref in enumerate(outs):
            total = jnp.zeros((count, width), jnp.float32)
            for g in range(groups):
                low = t * full + g * width
                block = rows_ref[g, :count].astype(jnp.float32) * gain_ref[:, low : low + width]
                part_ref = halves[low // half]
                at = low % half
                total = total + dot_nt(block.astype(jnp.bfloat16), part_ref[:, at : at + width])
            out_ref[:count, :] = total

    @pl.when(core_ref[0] == 0)
    def _():
        multiply((mine_ref, other_ref))

    @pl.when(core_ref[0] != 0)
    def _():
        multiply((other_ref, mine_ref))


def products(core, window, count, gain, mine, other):
    groups, _, width = window.shape
    return pl.pallas_call(
        products_body,
        grid=(1,),
        in_specs=[
            pl.BlockSpec(memory_space=pltpu.SMEM),
            pl.BlockSpec((groups, count, width), lambda i: (0, 0, 0)),
            pl.BlockSpec(gain.shape, lambda i: (0, 0)),
            pl.BlockSpec(mine.shape, lambda i: (0, 0)),
            pl.BlockSpec(other.shape, lambda i: (0, 0)),
        ],
        out_specs=(pl.BlockSpec((count + TAIL, width), lambda i: (0, 0)),) * 3,
        out_shape=(jax.ShapeDtypeStruct((count + TAIL, width), jnp.float32),) * 3,
        compiler_params=pltpu.CompilerParams(vmem_limit_bytes=VMEM_BYTES),
        interpret=INTERPRET,
        name="products",
    )(core, window, gain, mine, other)


def finish_body(own_ref, one_ref, two_ref, out_ref, *, features):
    members, count, width = out_ref.shape
    squares = own_ref[count:, :] + one_ref[count:, :] + two_ref[count:, :]
    inverse = lax.rsqrt(squares / features + 1e-06)
    for h in range(width // HEAD_DIM):
        cols = head_cols(h)
        pad = jnp.zeros((HEAD_DIM - TAIL, HEAD_DIM), jnp.float32)
        column = jnp.concatenate([inverse[:, cols], pad], axis=0).T[:, :1]
        product = own_ref[:count, cols] + one_ref[:count, cols] + two_ref[:count, cols]
        value = product * column
        mixed = (0.5 * value * (1.0 + lax.erf(value * math.sqrt(0.5)))).astype(jnp.bfloat16)
        for m in range(members):
            out_ref[m, :, cols] = mixed


def finish(own, one, two, members, features):
    height, width = own.shape
    return pl.pallas_call(
        lambda *refs: finish_body(*refs, features=features),
        grid=(1,),
        in_specs=[whole_spec(own), whole_spec(one), whole_spec(two)],
        out_specs=pl.BlockSpec((members, height - TAIL, width), lambda i: (0, 0, 0)),
        out_shape=jax.ShapeDtypeStruct((members, height - TAIL, width), jnp.bfloat16),
        compiler_params=pltpu.CompilerParams(vmem_limit_bytes=VMEM_BYTES // 2),
        interpret=INTERPRET,
        name="finish",
    )(own, one, two)


def decode_body(q_ref, mixed_ref, out_ref):
    groups, _, width = q_ref.shape
    for g in range(groups):
        for h in range(width // HEAD_DIM):
            cols = head_cols(h)
            scores = dot_nt(q_ref[g, :, cols], mixed_ref[:, cols])
            peak = jnp.max(scores, axis=1, keepdims=True)
            weights = jnp.exp2((scores - peak) * EXP2_SCALE)
            den = jnp.sum(weights, axis=1, keepdims=True)
            num = jnp.dot(
                weights.astype(jnp.bfloat16), mixed_ref[:, cols], preferred_element_type=jnp.float32
            )
            out_ref[g, :, cols] = num / den


def decode(window, count, mixed):
    groups, height, width = window.shape
    rows = height - count
    step = 2
    return pl.pallas_call(
        decode_body,
        grid=(groups // step,),
        in_specs=[
            pl.BlockSpec((step, rows, width), lambda i: (i, 1, 0)),
            pl.BlockSpec(mixed.shape, lambda i: (0, 0)),
        ],
        out_specs=pl.BlockSpec((step, rows, width), lambda i: (i, 0, 0)),
        out_shape=jax.ShapeDtypeStruct((groups, rows, width), jnp.float32),
        compiler_params=pltpu.CompilerParams(vmem_limit_bytes=VMEM_BYTES),
        interpret=INTERPRET,
        name="decode",
    )(window, mixed)


def local(inputs, kv_weight, latent_queries, mix_gain, mix_weight, output_queries):
    groups = lax.axis_size("x")
    members = lax.axis_size("z")
    place = lax.axis_index("x")
    core_index = lax.axis_index("core")
    core = core_index.reshape(1).astype(jnp.int32)
    latent_width = HEADS * HEAD_DIM
    width = latent_width // groups

    mine = inputs[0]
    half = mine.shape[0] // 2
    above = shift(mine, "x", -1)
    below = shift(mine, "x", 1)

    mix_t = mix_weight.T
    mix_half = mix_t.shape[1] // 2
    mix_mine = lax.dynamic_slice_in_dim(mix_t, core_index * mix_half, mix_half, axis=1)
    mix_mine = gather(mix_mine, "z").reshape(members * mix_t.shape[0], mix_half)
    mix_other = partner(mix_mine)

    rows = latent_queries.shape[0] // 2
    asked = lax.dynamic_slice_in_dim(latent_queries, core_index * rows, rows, axis=0)
    asked = jnp.stack([asked[:, g * width : (g + 1) * width] for g in range(groups)], axis=0)
    asked = jnp.broadcast_to(asked[:, None], (groups, members, rows, width))
    asked = asked.reshape(groups * members, rows, width)
    asked = lax.all_to_all(asked, ("x", "z"), 0, 0, tiled=True)
    asked = asked.reshape(groups * members * rows, width)
    asked_other = partner(asked)

    far_low = shift(above[:half], "x", -1)
    far_high = shift(below[half:], "x", 1)
    weight = jnp.concatenate(
        [
            lax.dynamic_slice_in_dim(kv_weight, place * width, width, axis=1),
            lax.dynamic_slice_in_dim(kv_weight, latent_width + place * width, width, axis=1),
        ],
        axis=1,
    )
    latents = groups * members * rows * 2
    parts = attend(
        core,
        asked,
        asked_other,
        weight,
        (mine, above, below),
        (far_low, far_high),
        members,
        latents // 4,
    )
    parts = lax.all_to_all(parts, "z", 0, 0, tiled=True)
    count = latents // members
    window = lax.all_to_all(combine(parts, output_queries[0], groups), "x", 0, 0, tiled=True)
    own, one, two = products(core, window, count, mix_gain[None], mix_mine, mix_other)
    one = from_behind(one, FRAME, 1)
    two = from_behind(two, FRAME, 2)
    mixed = finish(own, one, two, members, 3 * latent_width)
    mixed = lax.all_to_all(mixed, "z", 0, 0, tiled=True).reshape(latents, width)

    decoded = decode(window, count, mixed)
    decoded = lax.all_to_all(decoded, "x", 0, 0, tiled=True)
    return jnp.concatenate([decoded[g] for g in range(groups)], axis=1)[None]


def solution(mesh):
    grid = Mesh(mesh.devices.reshape(8, 2, 4, 8), ("y", "core", "x", "z"))
    tok = ("x", "z")
    return jax.shard_map(
        local,
        mesh=grid,
        in_specs=(P(FRAME, tok, None), P(), P(tok, None), P(), P(None, tok), P(FRAME, tok, None)),
        out_specs=P(FRAME, tok, None),
        check_vma=False,
    )
```

profile of v0, /device:TPU:32, one launch (start us, length us, event | category | flops | bytes accessed | tf_op | source)
XLA Modules:
  0.0 172.0 jit_solution(11280147044280884721)
XLA Ops:
  1.5 13.2 %all-to-all-start = ((bf16[32,16,256]{2,1,0:T(8,128)(2,1)}), bf16[32,16,256]{2,1,0:T(8,128)(2,1)S(1)}, u32[]{:S(2)}, u32[]{:S(2)}) async-start(bf16[32,16,256]{2,1,0:T(8,128)(2,1)} %bitcast.5), calls=%async_computation | async-start | bytes 524288 | tf_op jit(solution)/shard_map/all_to_all | solution.py:382
  14.7 12.4 %all-to-all-done = bf16[32,16,256]{2,1,0:T(8,128)(2,1)S(1)} async-done(((bf16[32,16,256]{2,1,0:T(8,128)(2,1)}), bf16[32,16,256]{2,1,0:T(8,128)(2,1)S(1)}, u32[]{:S(2)}, u32[]{:S(2)}) %all-to-all-start) | async-done | bytes 262176 | tf_op jit(solution)/shard_map/all_to_all | solution.py:382
  28.1 3.5 %all-to-all-start.3 = ((bf16[8,32,1536]{2,1,0:T(8,128)(2,1)}), bf16[8,32,1536]{2,1,0:T(8,128)(2,1)S(1)}, u32[]{:S(2)}, u32[]{:S(2)}) async-start(bf16[8,32,1536]{2,1,0:T(8,128)(2,1)} %broadcast_in_dim.20), calls=%async_computation.3 | async-start | bytes 1572864 | tf_op jit(solution)/shard_map/all_to_all | solution.py:35
  31.6 3.1 %collective-permute-start.1 = (bf16[768,512]{1,0:T(8,128)(2,1)}, bf16[768,512]{1,0:T(8,128)(2,1)S(1)}, u32[]{:S(2)}, u32[]{:S(2)}) collective-permute-start(bf16[768,512]{1,0:T(8,128)(2,1)} %bitcast.7.refs_0_), channel_id=1, source_target_pairs={{0,24},{8,0},{16,8},{24,16},{1,25},{9,1},{17,9},{25,17},{2,26},{10... | collective-permute-start | bytes 2359304 | tf_op jit(solution)/shard_map/ppermute | solution.py:24
  34.7 2.8 %collective-permute-start.2 = (bf16[768,512]{1,0:T(8,128)(2,1)}, bf16[768,512]{1,0:T(8,128)(2,1)S(1)}, u32[]{:S(2)}, u32[]{:S(2)}) collective-permute-start(bf16[768,512]{1,0:T(8,128)(2,1)} %bitcast.7.refs_0_), channel_id=1, source_target_pairs={{0,8},{8,16},{16,24},{24,0},{1,9},{9,17},{17,25},{25,1},{2,10},{10... | collective-permute-start | bytes 2359304 | tf_op jit(solution)/shard_map/ppermute | solution.py:24
  37.5 13.6 %collective-permute-done.1.refs_1_ = bf16[768,512]{1,0:T(8,128)(2,1)S(1)} collective-permute-done((bf16[768,512]{1,0:T(8,128)(2,1)}, bf16[768,512]{1,0:T(8,128)(2,1)S(1)}, u32[]{:S(2)}, u32[]{:S(2)}) %collective-permute-start.1) | collective-permute-done | bytes 786464 | tf_op jit(solution)/shard_map/ppermute | solution.py:24
  51.9 4.3 %collective-permute-start.3 = (bf16[384,512]{1,0:T(8,128)(2,1)}, bf16[384,512]{1,0:T(8,128)(2,1)S(1)}, u32[]{:S(2)}, u32[]{:S(2)}) collective-permute-start(bf16[384,512]{1,0:T(8,128)(2,1)} %slice.40), channel_id=1, source_target_pairs={{0,24},{8,0},{16,8},{24,16},{1,25},{9,1},{17,9},{25,17},{2,26},{10... | collective-permute-start | bytes 1179656 | tf_op jit(solution)/shard_map/ppermute | solution.py:24
  57.0 1.9 %collective-permute-start.4 = (bf16[384,512]{1,0:T(8,128)(2,1)}, bf16[384,512]{1,0:T(8,128)(2,1)}, u32[]{:S(2)}, u32[]{:S(2)}) collective-permute-start(bf16[384,512]{1,0:T(8,128)(2,1)} %slice.41), channel_id=1, source_target_pairs={{0,8},{8,16},{16,24},{24,0},{1,9},{9,17},{17,25},{25,1},{2,10},{10... | collective-permute-start | bytes 1179656 | tf_op jit(solution)/shard_map/ppermute | solution.py:24
  58.9 1.9 %collective-permute-start = (bf16[512,256]{1,0:T(8,128)(2,1)S(1)}, bf16[512,256]{1,0:T(8,128)(2,1)S(1)}, u32[]{:S(2)}, u32[]{:S(2)}) collective-permute-start(bf16[512,256]{1,0:T(8,128)(2,1)S(1)} %bitcast.30), channel_id=1, source_target_pairs={{0,32},{32,0},{1,33},{33,1},{2,34},{34,2},{3,35},{35,3},{4,36},{36... | collective-permute-start | bytes 786440 | tf_op jit(solution)/shard_map/ppermute | solution.py:39
  62.4 10.9 %attend_near.1 = (f32[1024,256]{1,0:T(8,128)S(1)}, f32[1024,256]{1,0:T(8,128)S(1)}) custom-call(s32[1]{0:T(128)} %bitcast.core_ref, bf16[512,256]{1,0:T(8,128)(2,1)S(1)} %bitcast.31, bf16[512,256]{1,0:T(8,128)(2,1)S(1)} %collective-permute-done.other_ref, bf16[512,512]{1,0:T(8,128)(2,1)S(1)} %pad_maximum_fusion.w_ref, bf16[768,512]{1,0:T(8,128)(2,1)} %bitcast.7.refs_0_, ...), custom_call_target="tpu_custom_call" | custom-call | tf_op jit(solution)/shard_map/attend_near/pallas_call | solution.py:154
  73.3 7.5 %attend_far.1 = bf16[8,144,256]{2,1,0:T(8,128)(2,1)} custom-call(s32[1]{0:T(128)} %bitcast.core_ref, bf16[512,256]{1,0:T(8,128)(2,1)S(1)} %bitcast.32, bf16[512,256]{1,0:T(8,128)(2,1)S(1)} %collective-permute-done.other_ref, bf16[512,512]{1,0:T(8,128)(2,1)S(1)} %pad_maximum_fusion.w_ref, f32[1024,256]{1,0:T(8,128)S(1)} %get-tuple-element.10.num_ref, ...), custom_call_target="tpu_custom_call" | custom-call | tf_op jit(solution)/shard_map/attend_far/pallas_call | solution.py:168
  80.8 7.0 %all-to-all-start.1 = ((bf16[8,144,256]{2,1,0:T(8,128)(2,1)}), bf16[8,144,256]{2,1,0:T(8,128)(2,1)S(1)}, u32[]{:S(2)}, u32[]{:S(2)}) async-start(bf16[8,144,256]{2,1,0:T(8,128)(2,1)} %attend_far.1), calls=%async_computation.1 | async-start | bytes 1179648 | tf_op jit(solution)/shard_map/all_to_all | solution.py:406
  87.8 1.9 %collective-permute-start.5 = (bf16[256,1536]{1,0:T(8,128)(2,1)S(1)}, bf16[256,1536]{1,0:T(8,128)(2,1)S(1)}, u32[]{:S(2)}, u32[]{:S(2)}) collective-permute-start(bf16[256,1536]{1,0:T(8,128)(2,1)S(1)} %bitcast.28), channel_id=1, source_target_pairs={{0,32},{32,0},{1,33},{33,1},{2,34},{34,2},{3,35},{35,3},{4,36},{36... | collective-permute-start | bytes 2359304 | tf_op jit(solution)/shard_map/ppermute | solution.py:39
  89.7 17.3 %all-to-all-done.1.part_ref = bf16[8,144,256]{2,1,0:T(8,128)(2,1)S(1)} async-done(((bf16[8,144,256]{2,1,0:T(8,128)(2,1)}), bf16[8,144,256]{2,1,0:T(8,128)(2,1)S(1)}, u32[]{:S(2)}, u32[]{:S(2)}) %all-to-all-start.1) | async-done | bytes 589856 | tf_op jit(solution)/shard_map/all_to_all | solution.py:406
  108.0 1.4 combine.1
  109.4 4.5 %all-to-all-start.2 = ((bf16[4,256,256]{2,1,0:T(8,128)(2,1)}), bf16[4,256,256]{2,1,0:T(8,128)(2,1)S(1)}, u32[]{:S(2)}, u32[]{:S(2)}) async-start(bf16[4,256,256]{2,1,0:T(8,128)(2,1)} %combine.1), calls=%async_computation.2 | async-start | bytes 1048576 | tf_op jit(solution)/shard_map/all_to_all | solution.py:408
  113.9 9.7 %all-to-all-done.2.rows_ref.q_ref = bf16[4,256,256]{2,1,0:T(8,128)(2,1)S(1)} async-done(((bf16[4,256,256]{2,1,0:T(8,128)(2,1)}), bf16[4,256,256]{2,1,0:T(8,128)(2,1)S(1)}, u32[]{:S(2)}, u32[]{:S(2)}) %all-to-all-start.2) | async-done | bytes 524320 | tf_op jit(solution)/shard_map/all_to_all | solution.py:408
  124.4 1.9 %collective-permute-start.6 = (f32[136,256]{1,0:T(8,128)S(1)}, f32[136,256]{1,0:T(8,128)S(1)}, u32[]{:S(2)}, u32[]{:S(2)}) collective-permute-start(f32[136,256]{1,0:T(8,128)S(1)} %get-tuple-element.13), channel_id=1, source_target_pairs={{0,32},{32,64},{64,96},{96,128},{128,160},{160,192},{192,224},{224... | collective-permute-start | bytes 417800 | tf_op jit(solution)/shard_map/ppermute | solution.py:30
  126.3 2.6 %collective-permute-start.7 = (f32[136,256]{1,0:T(8,128)S(1)}, f32[136,256]{1,0:T(8,128)S(1)}, u32[]{:S(2)}, u32[]{:S(2)}) collective-permute-start(f32[136,256]{1,0:T(8,128)S(1)} %get-tuple-element.14), channel_id=1, source_target_pairs={{0,64},{32,96},{64,128},{96,160},{128,192},{160,224},{192,256},{22... | collective-permute-start | bytes 417800 | tf_op jit(solution)/shard_map/ppermute | solution.py:30
  128.9 3.1 %collective-permute-done.6.refs_1_ = f32[136,256]{1,0:T(8,128)S(1)} collective-permute-done((f32[136,256]{1,0:T(8,128)S(1)}, f32[136,256]{1,0:T(8,128)S(1)}, u32[]{:S(2)}, u32[]{:S(2)}) %collective-permute-start.6) | collective-permute-done | bytes 139296 | tf_op jit(solution)/shard_map/ppermute | solution.py:30
  131.9 3.8 %collective-permute-done.7.refs_2_ = f32[136,256]{1,0:T(8,128)S(1)} collective-permute-done((f32[136,256]{1,0:T(8,128)S(1)}, f32[136,256]{1,0:T(8,128)S(1)}, u32[]{:S(2)}, u32[]{:S(2)}) %collective-permute-start.7) | collective-permute-done | bytes 139296 | tf_op jit(solution)/shard_map/ppermute | solution.py:30
  136.0 20.3 %all_to_all.30 = bf16[8,128,256]{2,1,0:T(8,128)(2,1)S(1)} all-to-all(bf16[8,128,256]{2,1,0:T(8,128)(2,1)S(1)} %finish.1), channel_id=1, replica_groups=mesh['y'=8,'core'=2,'x'=4,'z'=8] {'z'}, dimensions={0} | all-to-all | bytes 1048576 | tf_op jit(solution)/shard_map/all_to_all | solution.py:413
  156.2 3.2 %decode.1 = f32[4,128,256]{2,1,0:T(8,128)S(1)} custom-call(bf16[4,256,256]{2,1,0:T(8,128)(2,1)S(1)} %all-to-all-done.2.rows_ref.q_ref, bf16[1024,256]{1,0:T(8,128)(2,1)S(1)} %bitcast.33), custom_call_target="tpu_custom_call" | custom-call | tf_op jit(solution)/shard_map/decode/pallas_call | solution.py:342
  159.4 11.7 %all_to_all.31 = f32[4,128,256]{2,1,0:T(8,128)S(1)} all-to-all(f32[4,128,256]{2,1,0:T(8,128)S(1)} %decode.1), channel_id=1, replica_groups=mesh['y'=8,'core'=2,'x'=4,'z'=8] {'x'}, dimensions={0} | all-to-all | bytes 1048576 | tf_op jit(solution)/shard_map/all_to_all | solution.py:416
  (25 shorter events, 8.4 us)
Async XLA Ops:
  0.0 14.7 %copy-start = (bf16[3072,32]{0,1:T(8,128)(2,1)S(1)}, bf16[3072,32]{0,1:T(8,128)(2,1)}, u32[]{:S(2)}) copy-start(bf16[3072,32]{0,1:T(8,128)(2,1)} %param.10) | copy-start | bytes 589828
  1.5 25.6 %all-to-all-start = ((bf16[32,16,256]{2,1,0:T(8,128)(2,1)}), bf16[32,16,256]{2,1,0:T(8,128)(2,1)S(1)}, u32[]{:S(2)}, u32[]{:S(2)}) async-start(bf16[32,16,256]{2,1,0:T(8,128)(2,1)} %bitcast.5), calls=%async_computation | async-start | bytes 524288 | tf_op jit(solution)/shard_map/all_to_all | solution.py:382
  28.1 52.7 %all-to-all-start.3 = ((bf16[8,32,1536]{2,1,0:T(8,128)(2,1)}), bf16[8,32,1536]{2,1,0:T(8,128)(2,1)S(1)}, u32[]{:S(2)}, u32[]{:S(2)}) async-start(bf16[8,32,1536]{2,1,0:T(8,128)(2,1)} %broadcast_in_dim.20), calls=%async_computation.3 | async-start | bytes 1572864 | tf_op jit(solution)/shard_map/all_to_all | solution.py:35
  31.6 19.5 %collective-permute-start.1 = (bf16[768,512]{1,0:T(8,128)(2,1)}, bf16[768,512]{1,0:T(8,128)(2,1)S(1)}, u32[]{:S(2)}, u32[]{:S(2)}) collective-permute-start(bf16[768,512]{1,0:T(8,128)(2,1)} %bitcast.7.refs_0_), channel_id=1, source_target_pairs={{0,24},{8,0},{16,8},{24,16},{1,25},{9,1},{17,9},{25,17},{2,26},{10... | collective-permute-start | bytes 2359304 | tf_op jit(solution)/shard_map/ppermute | solution.py:24
  34.7 21.5 %collective-permute-start.2 = (bf16[768,512]{1,0:T(8,128)(2,1)}, bf16[768,512]{1,0:T(8,128)(2,1)S(1)}, u32[]{:S(2)}, u32[]{:S(2)}) collective-permute-start(bf16[768,512]{1,0:T(8,128)(2,1)} %bitcast.7.refs_0_), channel_id=1, source_target_pairs={{0,8},{8,16},{16,24},{24,0},{1,9},{9,17},{17,25},{25,1},{2,10},{10... | collective-permute-start | bytes 2359304 | tf_op jit(solution)/shard_map/ppermute | solution.py:24
  51.9 21.3 %collective-permute-start.3 = (bf16[384,512]{1,0:T(8,128)(2,1)}, bf16[384,512]{1,0:T(8,128)(2,1)S(1)}, u32[]{:S(2)}, u32[]{:S(2)}) collective-permute-start(bf16[384,512]{1,0:T(8,128)(2,1)} %slice.40), channel_id=1, source_target_pairs={{0,24},{8,0},{16,8},{24,16},{1,25},{9,1},{17,9},{25,17},{2,26},{10... | collective-permute-start | bytes 1179656 | tf_op jit(solution)/shard_map/ppermute | solution.py:24
  57.0 16.2 %collective-permute-start.4 = (bf16[384,512]{1,0:T(8,128)(2,1)}, bf16[384,512]{1,0:T(8,128)(2,1)}, u32[]{:S(2)}, u32[]{:S(2)}) collective-permute-start(bf16[384,512]{1,0:T(8,128)(2,1)} %slice.41), channel_id=1, source_target_pairs={{0,8},{8,16},{16,24},{24,0},{1,9},{9,17},{17,25},{25,1},{2,10},{10... | collective-permute-start | bytes 1179656 | tf_op jit(solution)/shard_map/ppermute | solution.py:24
  58.9 3.4 %collective-permute-start = (bf16[512,256]{1,0:T(8,128)(2,1)S(1)}, bf16[512,256]{1,0:T(8,128)(2,1)S(1)}, u32[]{:S(2)}, u32[]{:S(2)}) collective-permute-start(bf16[512,256]{1,0:T(8,128)(2,1)S(1)} %bitcast.30), channel_id=1, source_target_pairs={{0,32},{32,0},{1,33},{33,1},{2,34},{34,2},{3,35},{35,3},{4,36},{36... | collective-permute-start | bytes 786440 | tf_op jit(solution)/shard_map/ppermute | solution.py:39
  80.7 42.8 %copy-start.2 = (f32[3072]{0:T(1024)S(1)}, f32[3072]{0:T(1024)}, u32[]{:S(2)}) copy-start(f32[3072]{0:T(1024)} %param.9) | copy-start | bytes 36868
  80.8 26.3 %all-to-all-start.1 = ((bf16[8,144,256]{2,1,0:T(8,128)(2,1)}), bf16[8,144,256]{2,1,0:T(8,128)(2,1)S(1)}, u32[]{:S(2)}, u32[]{:S(2)}) async-start(bf16[8,144,256]{2,1,0:T(8,128)(2,1)} %attend_far.1), calls=%async_computation.1 | async-start | bytes 1179648 | tf_op jit(solution)/shard_map/all_to_all | solution.py:406
  87.8 26.1 %collective-permute-start.5 = (bf16[256,1536]{1,0:T(8,128)(2,1)S(1)}, bf16[256,1536]{1,0:T(8,128)(2,1)S(1)}, u32[]{:S(2)}, u32[]{:S(2)}) collective-permute-start(bf16[256,1536]{1,0:T(8,128)(2,1)S(1)} %bitcast.28), channel_id=1, source_target_pairs={{0,32},{32,0},{1,33},{33,1},{2,34},{34,2},{3,35},{35,3},{4,36},{36... | collective-permute-start | bytes 2359304 | tf_op jit(solution)/shard_map/ppermute | solution.py:39
  107.0 1.0 copy-start.1
  109.4 14.2 %all-to-all-start.2 = ((bf16[4,256,256]{2,1,0:T(8,128)(2,1)}), bf16[4,256,256]{2,1,0:T(8,128)(2,1)S(1)}, u32[]{:S(2)}, u32[]{:S(2)}) async-start(bf16[4,256,256]{2,1,0:T(8,128)(2,1)} %combine.1), calls=%async_computation.2 | async-start | bytes 1048576 | tf_op jit(solution)/shard_map/all_to_all | solution.py:408
  124.4 7.6 %collective-permute-start.6 = (f32[136,256]{1,0:T(8,128)S(1)}, f32[136,256]{1,0:T(8,128)S(1)}, u32[]{:S(2)}, u32[]{:S(2)}) collective-permute-start(f32[136,256]{1,0:T(8,128)S(1)} %get-tuple-element.13), channel_id=1, source_target_pairs={{0,32},{32,64},{64,96},{96,128},{128,160},{160,192},{192,224},{224... | collective-permute-start | bytes 417800 | tf_op jit(solution)/shard_map/ppermute | solution.py:30
  126.3 9.5 %collective-permute-start.7 = (f32[136,256]{1,0:T(8,128)S(1)}, f32[136,256]{1,0:T(8,128)S(1)}, u32[]{:S(2)}, u32[]{:S(2)}) collective-permute-start(f32[136,256]{1,0:T(8,128)S(1)} %get-tuple-element.14), channel_id=1, source_target_pairs={{0,64},{32,96},{64,128},{96,160},{128,192},{160,224},{192,256},{22... | collective-permute-start | bytes 417800 | tf_op jit(solution)/shard_map/ppermute | solution.py:30
where the time goes:
time: 173 us; the launch traced here: 172 us
  waiting for transfers between devices  60.3 us (35%)
  starting transfers between devices  48.6 us (28%)
  blocking collectives  31.9 us (18%)
  Pallas kernels  23.9 us (14%)
  local copies, waits for them, and re-layouts  6.11 us (4%)
    all_to_all x1, blocking collectives, local(): mixed = lax.all_to_all(mixed, 'z', 0, 0, tiled=True).reshape(latents, width)  20.3 us
    all_to_all x1, waiting for transfers between devices, local(): parts = lax.all_to_all(parts, 'z', 0, 0, tiled=True)  17.3 us
    ppermute x4, waiting for transfers between devices, shift(): lax.ppermute(block, axis, [(i, (i + distance) % size) for i in range(size)])  13.6 us
    all_to_all x1, starting transfers between devices, local(): asked = lax.all_to_all(asked, ('x', 'z'), 0, 0, tiled=True)  13.2 us
    all_to_all x1, waiting for transfers between devices, local(): asked = lax.all_to_all(asked, ('x', 'z'), 0, 0, tiled=True)  12.4 us
    ppermute x4, starting transfers between devices, shift(): lax.ppermute(block, axis, [(i, (i + distance) % size) for i in range(size)])  12 us
    all_to_all x1, blocking collectives, local(): decoded = lax.all_to_all(decoded, 'x', 0, 0, tiled=True)  11.7 us
    pallas_call x1, Pallas kernels, attend(): pl.pallas_call(near_body, grid=(latents // tile,), in_specs=common_specs...  10.9 us
  transfers between devices with their start and end apart: 12, of which 7 were waited for; matrix products, arithmetic and copies ran while one was open for 2% of the time, Pallas kernels for 11%

commit v1 on v0

v1 whole, which is shorter than its diff:
```python
import math

import jax
import jax.numpy as jnp
from jax import lax
from jax.experimental import pallas as pl
from jax.experimental.pallas import tpu as pltpu
from jax.sharding import Mesh
from jax.sharding import PartitionSpec as P


HEADS = 8
HEAD_DIM = 128
EXP2_SCALE = math.log2(math.e) / math.sqrt(HEAD_DIM)
FRAME = ("y", "core")
EXTRA = 16
TAIL = 8
XORS = (4, 2, 1)
MASKS = (0, 4, 2, 6, 1, 5, 3, 7)
VMEM_BYTES = 32 * 1024 * 1024
INTERPRET = False


def shift(block, axis, distance):
    size = lax.axis_size(axis)
    return lax.ppermute(block, axis, [(i, (i + distance) % size) for i in range(size)])


def from_behind(block, axis, distance):
    devices = range(lax.axis_size(axis))
    route = [(i - distance, i) for i in devices if i - distance in devices]
    return lax.ppermute(block, axis, route)


def across(block, axis, mask):
    return lax.ppermute(block, axis, [(i, i ^ mask) for i in range(lax.axis_size(axis))])


def partner(block):
    return lax.ppermute(block, "core", [(0, 1), (1, 0)])


def dot_nt(a, b):
    return lax.dot_general(a, b, (((1,), (1,)), ((), ())), preferred_element_type=jnp.float32)


def whole_spec(block):
    return pl.BlockSpec(block.shape, lambda i: (0,) * len(block.shape))


def head_cols(h):
    return slice(h * HEAD_DIM, (h + 1) * HEAD_DIM)


def project_inputs(in_refs, w_ref, kv_ref):
    low = 0
    for in_ref in in_refs:
        rows = in_ref.shape[0]
        kv_ref[low : low + rows, :] = jnp.dot(
            in_ref[...], w_ref[...], preferred_element_type=jnp.float32
        ).astype(jnp.bfloat16)
        low += rows


def pick_queries(core_ref, mine_ref, other_ref, tile_ref):
    step = pl.program_id(0)
    tile = tile_ref.shape[0]
    per_half = mine_ref.shape[0] // tile
    start = pl.multiple_of((step % per_half) * tile, tile)
    is_mine = step // per_half == core_ref[0]

    @pl.when(is_mine)
    def _():
        tile_ref[...] = mine_ref[pl.ds(start, tile), :]

    @pl.when(jnp.logical_not(is_mine))
    def _():
        tile_ref[...] = other_ref[pl.ds(start, tile), :]


def lanes(values, shape):
    lane = lax.broadcasted_iota(jnp.int32, shape, 1)
    result = jnp.broadcast_to(values[-1], shape)
    for k in range(len(values) - 2, -1, -1):
        result = jnp.where(lane == k, values[k], result)
    return result


def attend_body(core_ref, mine_ref, other_ref, w_ref, *refs):
    in_refs, (out_ref, kv_ref, q_ref) = refs[:-3], refs[-3:]
    width = mine_ref.shape[1]

    @pl.when(pl.program_id(0) == 0)
    def _():
        project_inputs(in_refs, w_ref, kv_ref)

    pick_queries(core_ref, mine_ref, other_ref, q_ref)
    tile = q_ref.shape[0]
    blocks = out_ref.shape[0]
    rows = tile // blocks
    for h in range(width // HEAD_DIM):
        cols = head_cols(h)
        scores = dot_nt(q_ref[:, cols], kv_ref[:, cols])
        peak = jnp.max(scores, axis=1, keepdims=True)
        weights = jnp.exp2((scores - peak) * EXP2_SCALE)
        den = jnp.sum(weights, axis=1, keepdims=True)
        value_cols = slice(width + h * HEAD_DIM, width + (h + 1) * HEAD_DIM)
        num = jnp.dot(
            weights.astype(jnp.bfloat16), kv_ref[:, value_cols], preferred_element_type=jnp.float32
        )
        first = peak.astype(jnp.bfloat16).astype(jnp.float32)
        second = (peak - first).astype(jnp.bfloat16).astype(jnp.float32)
        packed = lanes([first, second, peak - first - second, den], (tile, HEAD_DIM)).T
        for b in range(blocks):
            span = slice(b * rows, (b + 1) * rows)
            out_ref[b, :rows, cols] = num[span].astype(jnp.bfloat16)
            out_ref[b, rows:, cols] = packed[:EXTRA, span].astype(jnp.bfloat16)


def attend(core, mine, other, weight, inputs, blocks, tile):
    half, width = mine.shape
    latents = 2 * half
    rows = latents // blocks
    return pl.pallas_call(
        attend_body,
        grid=(latents // tile,),
        in_specs=[pl.BlockSpec(memory_space=pltpu.SMEM)]
        + [whole_spec(block) for block in (mine, other, weight) + inputs],
        out_specs=pl.BlockSpec((tile // rows, rows + EXTRA, width), lambda i: (i, 0, 0)),
        out_shape=jax.ShapeDtypeStruct((blocks, rows + EXTRA, width), jnp.bfloat16),
        scratch_shapes=[
            pltpu.VMEM((sum(b.shape[0] for b in inputs), 2 * width), jnp.bfloat16),
            pltpu.VMEM((tile, width), jnp.bfloat16),
        ],
        compiler_params=pltpu.CompilerParams(vmem_limit_bytes=VMEM_BYTES),
        interpret=INTERPRET,
        name="attend",
    )(core, mine, other, weight, *inputs)


def order_body(place_ref, first_ref, second_ref, out_ref):
    rows = out_ref.shape[0] // len(MASKS)
    half = len(MASKS) // 2
    for j, mask in enumerate(MASKS):
        part_ref = (first_ref, second_ref)[j // half]
        low = (j % half) * rows
        at = pl.multiple_of((place_ref[0] ^ mask) * rows, rows)
        out_ref[pl.ds(at, rows), :] = part_ref[low : low + rows, :]


def order(place, first, second):
    shape = (2 * first.shape[0], first.shape[1])
    return pl.pallas_call(
        order_body,
        grid=(1,),
        in_specs=[pl.BlockSpec(memory_space=pltpu.SMEM), whole_spec(first), whole_spec(second)],
        out_specs=pl.BlockSpec(shape, lambda i: (0, 0)),
        out_shape=jax.ShapeDtypeStruct(shape, first.dtype),
        compiler_params=pltpu.CompilerParams(vmem_limit_bytes=VMEM_BYTES // 2),
        interpret=INTERPRET,
        name="order",
    )(place, first, second)


def combine_body(part_ref, out_ref):
    blocks, height, width = part_ref.shape
    rows = height - EXTRA
    groups = out_ref.shape[0]
    peaks = []
    dens = []
    for b in range(blocks):
        extra = part_ref[b, rows:, :].astype(jnp.float32)
        peaks.append(extra[0:1] + extra[1:2] + extra[2:3])
        dens.append(extra[3:4])
    top = peaks[0]
    for peak in peaks[1:]:
        top = jnp.maximum(top, peak)
    scales = [jnp.exp2((peak - top) * EXP2_SCALE) for peak in peaks]
    den = scales[0] * dens[0]
    for scale, part in zip(scales[1:], dens[1:]):
        den = den + scale * part
    pad = jnp.zeros((HEAD_DIM - blocks - 1, width), jnp.float32)
    table = jnp.concatenate(scales + [den, pad], axis=0)
    for h in range(width // HEAD_DIM):
        cols = head_cols(h)
        turned = table[:, cols].T
        total = jnp.zeros((rows, HEAD_DIM), jnp.float32)
        for b in range(blocks):
            total = total + part_ref[b, :rows, cols].astype(jnp.float32) * turned[:, b : b + 1]
        latents = (total / turned[:, blocks : blocks + 1]).astype(jnp.bfloat16)
        for g in range(groups):
            out_ref[g, :, cols] = latents


def combine(parts, groups):
    _, height, width = parts.shape
    rows = height - EXTRA
    return pl.pallas_call(
        combine_body,
        grid=(1,),
        in_specs=[whole_spec(parts)],
        out_specs=pl.BlockSpec((groups, rows, width), lambda i: (0, 0, 0)),
        out_shape=jax.ShapeDtypeStruct((groups, rows, width), jnp.bfloat16),
        compiler_params=pltpu.CompilerParams(vmem_limit_bytes=VMEM_BYTES // 2),
        interpret=INTERPRET,
        name="combine",
    )(parts)


def turn(column):
    return jnp.broadcast_to(column, (column.shape[0], HEAD_DIM)).T


def products_body(core_ref, rows_ref, gain_ref, mine_ref, other_ref, own_ref, one_ref, two_ref):
    groups, _, width = rows_ref.shape
    full = groups * width
    half = mine_ref.shape[1]
    count = own_ref.shape[0] - TAIL
    squares = jnp.zeros((count, 1), jnp.float32)
    for g in range(groups):
        block = rows_ref[g].astype(jnp.float32)
        squares = squares + jnp.sum(block * block, axis=1, keepdims=True)
    tail = turn(squares)[:TAIL]
    outs = (own_ref, one_ref, two_ref)
    for out_ref in outs:
        for h in range(width // HEAD_DIM):
            out_ref[count:, head_cols(h)] = tail

    def multiply(halves):
        for t, out_ref in enumerate(outs):
            total = jnp.zeros((count, width), jnp.float32)
            for g in range(groups):
                low = t * full + g * width
                block = rows_ref[g].astype(jnp.float32) * gain_ref[:, low : low + width]
                part_ref = halves[low // half]
                at = low % half
                total = total + dot_nt(block.astype(jnp.bfloat16), part_ref[:, at : at + width])
            out_ref[:count, :] = total

    @pl.when(core_ref[0] == 0)
    def _():
        multiply((mine_ref, other_ref))

    @pl.when(core_ref[0] != 0)
    def _():
        multiply((other_ref, mine_ref))


def products(core, window, gain, mine, other):
    _, count, width = window.shape
    return pl.pallas_call(
        products_body,
        grid=(1,),
        in_specs=[
            pl.BlockSpec(memory_space=pltpu.SMEM),
        ]
        + [whole_spec(block) for block in (window, gain, mine, other)],
        out_specs=(pl.BlockSpec((count + TAIL, width), lambda i: (0, 0)),) * 3,
        out_shape=(jax.ShapeDtypeStruct((count + TAIL, width), jnp.float32),) * 3,
        compiler_params=pltpu.CompilerParams(vmem_limit_bytes=VMEM_BYTES),
        interpret=INTERPRET,
        name="products",
    )(core, window, gain, mine, other)


def finish_body(own_ref, one_ref, two_ref, out_ref, *, features):
    members, count, width = out_ref.shape
    squares = own_ref[count:, :] + one_ref[count:, :] + two_ref[count:, :]
    inverse = lax.rsqrt(squares / features + 1e-06)
    for h in range(width // HEAD_DIM):
        cols = head_cols(h)
        pad = jnp.zeros((HEAD_DIM - TAIL, HEAD_DIM), jnp.float32)
        column = jnp.concatenate([inverse[:, cols], pad], axis=0).T[:, :1]
        product = own_ref[:count, cols] + one_ref[:count, cols] + two_ref[:count, cols]
        value = product * column
        mixed = (0.5 * value * (1.0 + lax.erf(value * math.sqrt(0.5)))).astype(jnp.bfloat16)
        for m in range(members):
            out_ref[m, :, cols] = mixed


def finish(own, one, two, members, features):
    height, width = own.shape
    return pl.pallas_call(
        lambda *refs: finish_body(*refs, features=features),
        grid=(1,),
        in_specs=[whole_spec(own), whole_spec(one), whole_spec(two)],
        out_specs=pl.BlockSpec((members, height - TAIL, width), lambda i: (0, 0, 0)),
        out_shape=jax.ShapeDtypeStruct((members, height - TAIL, width), jnp.bfloat16),
        compiler_params=pltpu.CompilerParams(vmem_limit_bytes=VMEM_BYTES // 2),
        interpret=INTERPRET,
        name="finish",
    )(own, one, two)


def decode_body(place_ref, mixed_ref, *refs):
    query_refs, out_ref = refs[:-1], refs[-1]
    groups, rows, width = out_ref.shape
    pair = 2
    for k in range(0, groups, pair):
        for h in range(width // HEAD_DIM):
            cols = head_cols(h)
            queries = jnp.concatenate([ref[:, cols] for ref in query_refs[k : k + pair]], axis=0)
            scores = dot_nt(queries, mixed_ref[:, cols])
            peak = jnp.max(scores, axis=1, keepdims=True)
            weights = jnp.exp2((scores - peak) * EXP2_SCALE)
            den = jnp.sum(weights, axis=1, keepdims=True)
            result = jnp.dot(
                weights.astype(jnp.bfloat16), mixed_ref[:, cols], preferred_element_type=jnp.float32
            )
            result = result / den
            for p in range(pair):
                at = (place_ref[0] + groups - k - p) % groups
                out_ref[at, :, cols] = result[p * rows : (p + 1) * rows]


def decode(place, mixed, queries):
    rows, width = queries[0].shape
    shape = (len(queries), rows, width)
    return pl.pallas_call(
        decode_body,
        grid=(1,),
        in_specs=[pl.BlockSpec(memory_space=pltpu.SMEM)]
        + [whole_spec(block) for block in (mixed,) + queries],
        out_specs=pl.BlockSpec(shape, lambda i: (0, 0, 0)),
        out_shape=jax.ShapeDtypeStruct(shape, jnp.float32),
        compiler_params=pltpu.CompilerParams(vmem_limit_bytes=VMEM_BYTES),
        interpret=INTERPRET,
        name="decode",
    )(place, mixed, *queries)


def scalar(index):
    return index.reshape(1).astype(jnp.int32)


def join(first, second):
    return jnp.concatenate([first, second], axis=0)


def all_to_all(block, axis):
    return lax.all_to_all(block, axis, 0, 0, tiled=True)


def local(inputs, kv_weight, latent_queries, mix_gain, mix_weight, output_queries):
    groups = lax.axis_size("x")
    members = lax.axis_size("z")
    place = lax.axis_index("x")
    core_index = lax.axis_index("core")
    core = scalar(core_index)
    latent_width = HEADS * HEAD_DIM
    width = latent_width // groups

    mine = inputs[0]
    half = mine.shape[0] // 2
    above = shift(mine, "x", -1)
    below = shift(mine, "x", 1)

    mix_t = mix_weight.T
    mix_half = mix_t.shape[1] // 2
    held = lax.dynamic_slice_in_dim(mix_t, core_index * mix_half, mix_half, axis=1)
    for mask in XORS[:-1]:
        held = join(held, across(held, "z", mask))
    brought = across(held, "z", XORS[-1])

    rows = latent_queries.shape[0] // 2
    asked = lax.dynamic_slice_in_dim(latent_queries, core_index * rows, rows, axis=0)
    asked = jnp.stack([asked[:, g * width : (g + 1) * width] for g in range(groups)], axis=0)
    asked = jnp.broadcast_to(asked[:, None], (groups, members, rows, width))
    asked = asked.reshape(groups * members, rows, width)
    asked = all_to_all(asked, ("x", "z"))
    asked = asked.reshape(groups * members * rows, width)
    asked_other = partner(asked)

    far_low = above[:half]
    far_low = shift(far_low, "x", -1)
    far_high = below[half:]
    far_high = shift(far_high, "x", 1)
    weight = jnp.concatenate(
        [
            lax.dynamic_slice_in_dim(kv_weight, place * width, width, axis=1),
            lax.dynamic_slice_in_dim(kv_weight, latent_width + place * width, width, axis=1),
        ],
        axis=1,
    )
    latents = groups * members * rows * 2
    parts = attend(
        core,
        asked,
        asked_other,
        weight,
        (mine, above, below, far_low, far_high),
        members,
        latents // 4,
    )
    parts = all_to_all(parts, "z")

    queries = []
    for k in range(groups):
        to = (place + k) % groups
        sent = lax.dynamic_slice_in_dim(output_queries[0], to * width, width, axis=1)
        queries.append(shift(sent, "x", k) if k else sent)
    mix_mine = order(scalar(lax.axis_index("z")), held, brought)
    mix_other = partner(mix_mine)

    window = all_to_all(combine(parts, groups), "x")
    own, one, two = products(core, window, mix_gain[None], mix_mine, mix_other)
    one = from_behind(one, FRAME, 1)
    two = from_behind(two, FRAME, 2)
    mixed = finish(own, one, two, members, 3 * latent_width)
    mixed = all_to_all(mixed, "z").reshape(latents, width)

    decoded = decode(scalar(place), mixed, tuple(queries))
    decoded = all_to_all(decoded, "x")
    return jnp.concatenate([decoded[g] for g in range(groups)], axis=1)[None]


def solution(mesh):
    grid = Mesh(mesh.devices.reshape(8, 2, 4, 8), ("y", "core", "x", "z"))
    tok = ("x", "z")
    return jax.shard_map(
        local,
        mesh=grid,
        in_specs=(P(FRAME, tok, None), P(), P(tok, None), P(), P(None, tok), P(FRAME, tok, None)),
        out_specs=P(FRAME, tok, None),
        check_vma=False,
    )
```

time: 173 us -> 161 us (0.931)
  the two profiles are of different devices: /device:TPU:32 before, /device:TPU:16 now
where the time goes in v1:
time: 161 us; the launch traced here: 160 us
  starting transfers between devices  74.9 us (47%)
  waiting for transfers between devices  50.7 us (31%)
  Pallas kernels  18 us (11%)
  blocking collectives  12.4 us (8%)
  local copies, waits for them, and re-layouts  2.73 us (2%)
    all_to_all x4, starting transfers between devices, all_to_all(): return lax.all_to_all(block, axis, 0, 0, tiled=True)  26.4 us
    ppermute x7, starting transfers between devices, shift(): lax.ppermute(block, axis, [(i, (i + distance) % size) for i in range(size)])  22.2 us
    ppermute x3, waiting for transfers between devices, across(): lax.ppermute(block, axis, [(i, i ^ mask) for i in range(lax.axis_size(axi...  19.2 us
    all_to_all x4, waiting for transfers between devices, all_to_all(): return lax.all_to_all(block, axis, 0, 0, tiled=True)  17.5 us
    ppermute x3, starting transfers between devices, across(): lax.ppermute(block, axis, [(i, i ^ mask) for i in range(lax.axis_size(axi...  17 us
    pallas_call x1, Pallas kernels, attend(): pl.pallas_call(attend_body, grid=(latents // tile,), in_specs=[pl.BlockSp...  12.8 us
    all_to_all x1, blocking collectives, all_to_all(): return lax.all_to_all(block, axis, 0, 0, tiled=True)  12.4 us
    ppermute x7, waiting for transfers between devices, shift(): lax.ppermute(block, axis, [(i, (i + distance) % size) for i in range(size)])  9.54 us
  transfers between devices with their start and end apart: 18, of which 10 were waited for; matrix products, arithmetic and copies ran while one was open for 2% of the time, Pallas kernels for 9%

profile of v1, /device:TPU:16, one launch (start us, length us, event | category | flops | bytes accessed | tf_op | source)
XLA Modules:
  0.0 160.0 jit_solution(14592816071831343189)
XLA Ops:
  0.0 4.8 %collective-permute-start.1 = (bf16[768,512]{1,0:T(8,128)(2,1)}, bf16[768,512]{1,0:T(8,128)(2,1)S(1)}, u32[]{:S(2)}, u32[]{:S(2)}) collective-permute-start(bf16[768,512]{1,0:T(8,128)(2,1)} %bitcast.39), channel_id=1, source_target_pairs={{0,24},{8,0},{16,8},{24,16},{1,25},{9,1},{17,9},{25,17},{2,26},{10... | collective-permute-start | bytes 2359304 | tf_op jit(solution)/shard_map/ppermute | solution.py:26
  4.8 1.9 %collective-permute-start.2 = (bf16[768,512]{1,0:T(8,128)(2,1)}, bf16[768,512]{1,0:T(8,128)(2,1)S(1)}, u32[]{:S(2)}, u32[]{:S(2)}) collective-permute-start(bf16[768,512]{1,0:T(8,128)(2,1)} %bitcast.40), channel_id=1, source_target_pairs={{0,8},{8,16},{16,24},{24,0},{1,9},{9,17},{17,25},{25,1},{2,10},{10... | collective-permute-start | bytes 2359304 | tf_op jit(solution)/shard_map/ppermute | solution.py:26
  8.2 13.4 %all-to-all-start = ((bf16[32,16,256]{2,1,0:T(8,128)(2,1)}), bf16[32,16,256]{2,1,0:T(8,128)(2,1)S(1)}, u32[]{:S(2)}, u32[]{:S(2)}) async-start(bf16[32,16,256]{2,1,0:T(8,128)(2,1)} %bitcast.6), calls=%async_computation | async-start | bytes 524288 | tf_op jit(solution)/shard_map/all_to_all | solution.py:341
  21.6 7.7 %collective-permute-start.5 = (bf16[32,1536]{1,0:T(8,128)(2,1)S(1)}, bf16[32,1536]{1,0:T(8,128)(2,1)S(1)}, u32[]{:S(2)}, u32[]{:S(2)}) collective-permute-start(bf16[32,1536]{1,0:T(8,128)(2,1)S(1)} %dynamic-slice_bitcast_fusion), channel_id=1, source_target_pairs={{0,4},{1,5},{2,6},{3,7},{4,0},{5,1},{6,2},{7,3},{8,12},{9,13},{10,... | collective-permute-start | bytes 294920 | tf_op jit(solution)/shard_map/ppermute | solution.py:36
  29.4 4.5 %all-to-all-done = bf16[32,16,256]{2,1,0:T(8,128)(2,1)S(1)} async-done(((bf16[32,16,256]{2,1,0:T(8,128)(2,1)}), bf16[32,16,256]{2,1,0:T(8,128)(2,1)S(1)}, u32[]{:S(2)}, u32[]{:S(2)}) %all-to-all-start) | async-done | bytes 262176 | tf_op jit(solution)/shard_map/all_to_all | solution.py:341
  35.9 4.6 %collective-permute-start.3 = (bf16[384,512]{1,0:T(8,128)(2,1)S(1)}, bf16[384,512]{1,0:T(8,128)(2,1)S(1)}, u32[]{:S(2)}, u32[]{:S(2)}) collective-permute-start(bf16[384,512]{1,0:T(8,128)(2,1)S(1)} %slice.40), channel_id=1, source_target_pairs={{0,24},{8,0},{16,8},{24,16},{1,25},{9,1},{17,9},{25,17},{2,26},{10... | collective-permute-start | bytes 1179656 | tf_op jit(solution)/shard_map/ppermute | solution.py:26
  42.5 5.3 %collective-permute-start.6 = (bf16[64,1536]{1,0:T(8,128)(2,1)S(1)}, bf16[64,1536]{1,0:T(8,128)(2,1)S(1)}, u32[]{:S(2)}, u32[]{:S(2)}) collective-permute-start(bf16[64,1536]{1,0:T(8,128)(2,1)S(1)} %pad_maximum_fusion.2), channel_id=1, source_target_pairs={{0,2},{1,3},{2,0},{3,1},{4,6},{5,7},{6,4},{7,5},{8,10},{9,11},{10,... | collective-permute-start | bytes 589832 | tf_op jit(solution)/shard_map/ppermute | solution.py:36
  49.5 5.4 %collective-permute-done.4.refs_4_ = bf16[384,512]{1,0:T(8,128)(2,1)S(1)} collective-permute-done((bf16[384,512]{1,0:T(8,128)(2,1)S(1)}, bf16[384,512]{1,0:T(8,128)(2,1)S(1)}, u32[]{:S(2)}, u32[]{:S(2)}) %collective-permute-start.4) | collective-permute-done | bytes 393248 | tf_op jit(solution)/shard_map/ppermute | solution.py:26
  54.9 12.8 %attend.1 = bf16[8,144,256]{2,1,0:T(8,128)(2,1)} custom-call(s32[1]{0:T(128)} %bitcast.1.core_ref, bf16[512,256]{1,0:T(8,128)(2,1)S(1)} %bitcast.38, bf16[512,256]{1,0:T(8,128)(2,1)S(1)} %collective-permute-done.other_ref, bf16[512,512]{1,0:T(8,128)(2,1)S(1)} %pad_maximum_fusion.w_ref, bf16[768,512]{1,0:T(8,128)(2,1)S(1)} %bitcast.41, ...), custom_call_target="tpu_custom_call" | custom-call | tf_op jit(solution)/shard_map/attend/pallas_call | solution.py:124
  67.7 3.9 %all-to-all-start.1 = ((bf16[8,144,256]{2,1,0:T(8,128)(2,1)}), bf16[8,144,256]{2,1,0:T(8,128)(2,1)S(1)}, u32[]{:S(2)}, u32[]{:S(2)}) async-start(bf16[8,144,256]{2,1,0:T(8,128)(2,1)} %attend.1), calls=%async_computation.1 | async-start | bytes 1179648 | tf_op jit(solution)/shard_map/all_to_all | solution.py:341
  71.7 3.9 %collective-permute-start.7 = (bf16[128,1536]{1,0:T(8,128)(2,1)S(1)}, bf16[128,1536]{1,0:T(8,128)(2,1)S(1)}, u32[]{:S(2)}, u32[]{:S(2)}) collective-permute-start(bf16[128,1536]{1,0:T(8,128)(2,1)S(1)} %pad_maximum_fusion.1.first_ref), channel_id=1, source_target_pairs={{0,1},{1,0},{2,3},{3,2},{4,5},{5,4},{6,7},{7,6},{8,9},{9,8},{10,11... | collective-permute-start | bytes 1179656 | tf_op jit(solution)/shard_map/ppermute | solution.py:36
  75.6 19.2 %collective-permute-done.7.second_ref = bf16[128,1536]{1,0:T(8,128)(2,1)S(1)} collective-permute-done((bf16[128,1536]{1,0:T(8,128)(2,1)S(1)}, bf16[128,1536]{1,0:T(8,128)(2,1)S(1)}, u32[]{:S(2)}, u32[]{:S(2)}) %collective-permute-start.7) | collective-permute-done | bytes 393248 | tf_op jit(solution)/shard_map/ppermute | solution.py:36
  98.1 3.4 %all-to-all-start.2 = ((bf16[4,128,256]{2,1,0:T(8,128)(2,1)}), bf16[4,128,256]{2,1,0:T(8,128)(2,1)S(1)}, u32[]{:S(2)}, u32[]{:S(2)}) async-start(bf16[4,128,256]{2,1,0:T(8,128)(2,1)} %combine.1), calls=%async_computation.2 | async-start | bytes 524288 | tf_op jit(solution)/shard_map/all_to_all | solution.py:341
  101.6 7.6 %all-to-all-done.2.rows_ref = bf16[4,128,256]{2,1,0:T(8,128)(2,1)S(1)} async-done(((bf16[4,128,256]{2,1,0:T(8,128)(2,1)}), bf16[4,128,256]{2,1,0:T(8,128)(2,1)S(1)}, u32[]{:S(2)}, u32[]{:S(2)}) %all-to-all-start.2) | async-done | bytes 262176 | tf_op jit(solution)/shard_map/all_to_all | solution.py:341
  109.9 3.5 %collective-permute-start.10 = (f32[136,256]{1,0:T(8,128)S(1)}, f32[136,256]{1,0:T(8,128)S(1)}, u32[]{:S(2)}, u32[]{:S(2)}) collective-permute-start(f32[136,256]{1,0:T(8,128)S(1)} %get-tuple-element.10), channel_id=1, source_target_pairs={{0,64},{32,96},{64,128},{96,160},{128,192},{160,224},{192,256},{22... | collective-permute-start | bytes 417800 | tf_op jit(solution)/shard_map/ppermute | solution.py:32
  117.1 2.7 %collective-permute-done.9.refs_1_ = f32[136,256]{1,0:T(8,128)S(1)} collective-permute-done((f32[136,256]{1,0:T(8,128)S(1)}, f32[136,256]{1,0:T(8,128)S(1)}, u32[]{:S(2)}, u32[]{:S(2)}) %collective-permute-start.9) | collective-permute-done | bytes 139296 | tf_op jit(solution)/shard_map/ppermute | solution.py:32
  120.8 5.7 %all-to-all-start.3 = ((bf16[8,128,256]{2,1,0:T(8,128)(2,1)}), bf16[8,128,256]{2,1,0:T(8,128)(2,1)S(1)}, u32[]{:S(2)}, u32[]{:S(2)}) async-start(bf16[8,128,256]{2,1,0:T(8,128)(2,1)} %finish.1), calls=%async_computation.3 | async-start | bytes 1048576 | tf_op jit(solution)/shard_map/all_to_all | solution.py:341
  126.6 2.5 %collective-permute-start.11 = (bf16[128,256]{1,0:T(8,128)(2,1)S(1)}, bf16[128,256]{1,0:T(8,128)(2,1)S(1)}, u32[]{:S(2)}, u32[]{:S(2)}) collective-permute-start(bf16[128,256]{1,0:T(8,128)(2,1)S(1)} %get-tuple-element.18), channel_id=1, source_target_pairs={{0,8},{8,16},{16,24},{24,0},{1,9},{9,17},{17,25},{25,1},{2,10},{10... | collective-permute-start | bytes 196616 | tf_op jit(solution)/shard_map/ppermute | solution.py:26
  129.1 4.0 %collective-permute-start.12 = (bf16[128,256]{1,0:T(8,128)(2,1)S(1)}, bf16[128,256]{1,0:T(8,128)(2,1)S(1)}, u32[]{:S(2)}, u32[]{:S(2)}) collective-permute-start(bf16[128,256]{1,0:T(8,128)(2,1)S(1)} %get-tuple-element.20), channel_id=1, source_target_pairs={{0,16},{8,24},{16,0},{24,8},{1,17},{9,25},{17,1},{25,9},{2,18},{10... | collective-permute-start | bytes 196616 | tf_op jit(solution)/shard_map/ppermute | solution.py:26
  133.1 2.5 %collective-permute-start.13 = (bf16[128,256]{1,0:T(8,128)(2,1)S(1)}, bf16[128,256]{1,0:T(8,128)(2,1)S(1)}, u32[]{:S(2)}, u32[]{:S(2)}) collective-permute-start(bf16[128,256]{1,0:T(8,128)(2,1)S(1)} %get-tuple-element.17), channel_id=1, source_target_pairs={{0,24},{8,0},{16,8},{24,16},{1,25},{9,1},{17,9},{25,17},{2,26},{10... | collective-permute-start | bytes 196616 | tf_op jit(solution)/shard_map/ppermute | solution.py:26
  136.8 2.5 %collective-permute-done.13.refs_3_ = bf16[128,256]{1,0:T(8,128)(2,1)S(1)} collective-permute-done((bf16[128,256]{1,0:T(8,128)(2,1)S(1)}, bf16[128,256]{1,0:T(8,128)(2,1)S(1)}, u32[]{:S(2)}, u32[]{:S(2)}) %collective-permute-start.13) | collective-permute-done | bytes 65568 | tf_op jit(solution)/shard_map/ppermute | solution.py:26
  139.2 5.4 %all-to-all-done.3 = bf16[8,128,256]{2,1,0:T(8,128)(2,1)S(1)} async-done(((bf16[8,128,256]{2,1,0:T(8,128)(2,1)}), bf16[8,128,256]{2,1,0:T(8,128)(2,1)S(1)}, u32[]{:S(2)}, u32[]{:S(2)}) %all-to-all-start.3) | async-done | bytes 524320 | tf_op jit(solution)/shard_map/all_to_all | solution.py:341
  144.7 2.0 %decode.1 = f32[4,128,256]{2,1,0:T(8,128)S(1)} custom-call(s32[1]{0:T(128)} %bitcast.place_ref, bf16[1024,256]{1,0:T(8,128)(2,1)S(1)} %bitcast.36, bf16[128,256]{1,0:T(8,128)(2,1)S(1)} %get-tuple-element.19.refs_0_, bf16[128,256]{1,0:T(8,128)(2,1)S(1)} %collective-permute-done.11.refs_1_, bf16[128,256]{1,0:T(8,128)(2,1)S(1)} %collective-permute-done.12.refs_2_, ...), custom_call_target="tpu_custom_call" | custom-call | tf_op jit(solution)/shard_map/decode/pallas_call | solution.py:319
  146.7 12.4 %all_to_all.25 = f32[4,128,256]{2,1,0:T(8,128)S(1)} all-to-all(f32[4,128,256]{2,1,0:T(8,128)S(1)} %decode.1), channel_id=1, replica_groups=mesh['y'=8,'core'=2,'x'=4,'z'=8] {'x'}, dimensions={0} | all-to-all | bytes 1048576 | tf_op jit(solution)/shard_map/all_to_all | solution.py:341
  (40 shorter events, 17.9 us)
Async XLA Ops:
  0.0 21.6 %copy-start = (bf16[3072,32]{0,1:T(8,128)(2,1)S(1)}, bf16[3072,32]{0,1:T(8,128)(2,1)}, u32[]{:S(2)}) copy-start(bf16[3072,32]{0,1:T(8,128)(2,1)} %param.10) | copy-start | bytes 589828
  0.0 35.8 %collective-permute-start.1 = (bf16[768,512]{1,0:T(8,128)(2,1)}, bf16[768,512]{1,0:T(8,128)(2,1)S(1)}, u32[]{:S(2)}, u32[]{:S(2)}) collective-permute-start(bf16[768,512]{1,0:T(8,128)(2,1)} %bitcast.39), channel_id=1, source_target_pairs={{0,24},{8,0},{16,8},{24,16},{1,25},{9,1},{17,9},{25,17},{2,26},{10... | collective-permute-start | bytes 2359304 | tf_op jit(solution)/shard_map/ppermute | solution.py:26
  4.8 35.7 %collective-permute-start.2 = (bf16[768,512]{1,0:T(8,128)(2,1)}, bf16[768,512]{1,0:T(8,128)(2,1)S(1)}, u32[]{:S(2)}, u32[]{:S(2)}) collective-permute-start(bf16[768,512]{1,0:T(8,128)(2,1)} %bitcast.40), channel_id=1, source_target_pairs={{0,8},{8,16},{16,24},{24,0},{1,9},{9,17},{17,25},{25,1},{2,10},{10... | collective-permute-start | bytes 2359304 | tf_op jit(solution)/shard_map/ppermute | solution.py:26
  8.2 25.7 %all-to-all-start = ((bf16[32,16,256]{2,1,0:T(8,128)(2,1)}), bf16[32,16,256]{2,1,0:T(8,128)(2,1)S(1)}, u32[]{:S(2)}, u32[]{:S(2)}) async-start(bf16[32,16,256]{2,1,0:T(8,128)(2,1)} %bitcast.6), calls=%async_computation | async-start | bytes 524288 | tf_op jit(solution)/shard_map/all_to_all | solution.py:341
  21.6 33.3 %copy-start.1 = (bf16[1,768,512]{2,1,0:T(8,128)(2,1)S(1)}, bf16[1,768,512]{2,1,0:T(8,128)(2,1)}, u32[]{:S(2)}) copy-start(bf16[1,768,512]{2,1,0:T(8,128)(2,1)} %param.6) | copy-start | bytes 2359300
  21.6 20.8 %collective-permute-start.5 = (bf16[32,1536]{1,0:T(8,128)(2,1)S(1)}, bf16[32,1536]{1,0:T(8,128)(2,1)S(1)}, u32[]{:S(2)}, u32[]{:S(2)}) collective-permute-start(bf16[32,1536]{1,0:T(8,128)(2,1)S(1)} %dynamic-slice_bitcast_fusion), channel_id=1, source_target_pairs={{0,4},{1,5},{2,6},{3,7},{4,0},{5,1},{6,2},{7,3},{8,12},{9,13},{10,... | collective-permute-start | bytes 294920 | tf_op jit(solution)/shard_map/ppermute | solution.py:36
  33.9 15.1 %collective-permute-start = (bf16[512,256]{1,0:T(8,128)(2,1)S(1)}, bf16[512,256]{1,0:T(8,128)(2,1)S(1)}, u32[]{:S(2)}, u32[]{:S(2)}) collective-permute-start(bf16[512,256]{1,0:T(8,128)(2,1)S(1)} %bitcast.37), channel_id=1, source_target_pairs={{0,32},{32,0},{1,33},{33,1},{2,34},{34,2},{3,35},{35,3},{4,36},{36... | collective-permute-start | bytes 786440 | tf_op jit(solution)/shard_map/ppermute | solution.py:40
  35.9 13.7 %collective-permute-start.3 = (bf16[384,512]{1,0:T(8,128)(2,1)S(1)}, bf16[384,512]{1,0:T(8,128)(2,1)S(1)}, u32[]{:S(2)}, u32[]{:S(2)}) collective-permute-start(bf16[384,512]{1,0:T(8,128)(2,1)S(1)} %slice.40), channel_id=1, source_target_pairs={{0,24},{8,0},{16,8},{24,16},{1,25},{9,1},{17,9},{25,17},{2,26},{10... | collective-permute-start | bytes 1179656 | tf_op jit(solution)/shard_map/ppermute | solution.py:26
  40.6 14.3 %collective-permute-start.4 = (bf16[384,512]{1,0:T(8,128)(2,1)S(1)}, bf16[384,512]{1,0:T(8,128)(2,1)S(1)}, u32[]{:S(2)}, u32[]{:S(2)}) collective-permute-start(bf16[384,512]{1,0:T(8,128)(2,1)S(1)} %slice.41), channel_id=1, source_target_pairs={{0,8},{8,16},{16,24},{24,0},{1,9},{9,17},{17,25},{25,1},{2,10},{10... | collective-permute-start | bytes 1179656 | tf_op jit(solution)/shard_map/ppermute | solution.py:26
  42.5 29.1 %collective-permute-start.6 = (bf16[64,1536]{1,0:T(8,128)(2,1)S(1)}, bf16[64,1536]{1,0:T(8,128)(2,1)S(1)}, u32[]{:S(2)}, u32[]{:S(2)}) collective-permute-start(bf16[64,1536]{1,0:T(8,128)(2,1)S(1)} %pad_maximum_fusion.2), channel_id=1, source_target_pairs={{0,2},{1,3},{2,0},{3,1},{4,6},{5,7},{6,4},{7,5},{8,10},{9,11},{10,... | collective-permute-start | bytes 589832 | tf_op jit(solution)/shard_map/ppermute | solution.py:36
  67.7 29.1 %all-to-all-start.1 = ((bf16[8,144,256]{2,1,0:T(8,128)(2,1)}), bf16[8,144,256]{2,1,0:T(8,128)(2,1)S(1)}, u32[]{:S(2)}, u32[]{:S(2)}) async-start(bf16[8,144,256]{2,1,0:T(8,128)(2,1)} %attend.1), calls=%async_computation.1 | async-start | bytes 1179648 | tf_op jit(solution)/shard_map/all_to_all | solution.py:341
  71.6 37.5 %copy-start.2 = (f32[3072]{0:T(1024)S(1)}, f32[3072]{0:T(1024)}, u32[]{:S(2)}) copy-start(f32[3072]{0:T(1024)} %param.9) | copy-start | bytes 36868
  71.7 23.2 %collective-permute-start.7 = (bf16[128,1536]{1,0:T(8,128)(2,1)S(1)}, bf16[128,1536]{1,0:T(8,128)(2,1)S(1)}, u32[]{:S(2)}, u32[]{:S(2)}) collective-permute-start(bf16[128,1536]{1,0:T(8,128)(2,1)S(1)} %pad_maximum_fusion.1.first_ref), channel_id=1, source_target_pairs={{0,1},{1,0},{2,3},{3,2},{4,5},{5,4},{6,7},{7,6},{8,9},{9,8},{10,11... | collective-permute-start | bytes 1179656 | tf_op jit(solution)/shard_map/ppermute | solution.py:36
  94.9 6.7 %collective-permute-start.8 = (bf16[256,1536]{1,0:T(8,128)(2,1)S(1)}, bf16[256,1536]{1,0:T(8,128)(2,1)S(1)}, u32[]{:S(2)}, u32[]{:S(2)}) collective-permute-start(bf16[256,1536]{1,0:T(8,128)(2,1)S(1)} %order.1.mine_ref), channel_id=1, source_target_pairs={{0,32},{32,0},{1,33},{33,1},{2,34},{34,2},{3,35},{35,3},{4,36},{36... | collective-permute-start | bytes 2359304 | tf_op jit(solution)/shard_map/ppermute | solution.py:40
  98.1 11.0 %all-to-all-start.2 = ((bf16[4,128,256]{2,1,0:T(8,128)(2,1)}), bf16[4,128,256]{2,1,0:T(8,128)(2,1)S(1)}, u32[]{:S(2)}, u32[]{:S(2)}) async-start(bf16[4,128,256]{2,1,0:T(8,128)(2,1)} %combine.1), calls=%async_computation.2 | async-start | bytes 524288 | tf_op jit(solution)/shard_map/all_to_all | solution.py:341
  101.6 25.0 %copy-start.3 = (bf16[1,128,1024]{2,1,0:T(8,128)(2,1)S(1)}, bf16[1,128,1024]{2,1,0:T(8,128)(2,1)}, u32[]{:S(2)}) copy-start(bf16[1,128,1024]{2,1,0:T(8,128)(2,1)} %param.11) | copy-start | bytes 786436
  109.9 7.1 %collective-permute-start.10 = (f32[136,256]{1,0:T(8,128)S(1)}, f32[136,256]{1,0:T(8,128)S(1)}, u32[]{:S(2)}, u32[]{:S(2)}) collective-permute-start(f32[136,256]{1,0:T(8,128)S(1)} %get-tuple-element.10), channel_id=1, source_target_pairs={{0,64},{32,96},{64,128},{96,160},{128,192},{160,224},{192,256},{22... | collective-permute-start | bytes 417800 | tf_op jit(solution)/shard_map/ppermute | solution.py:32
  113.4 6.4 %collective-permute-start.9 = (f32[136,256]{1,0:T(8,128)S(1)}, f32[136,256]{1,0:T(8,128)S(1)}, u32[]{:S(2)}, u32[]{:S(2)}) collective-permute-start(f32[136,256]{1,0:T(8,128)S(1)} %get-tuple-element.9), channel_id=1, source_target_pairs={{0,32},{32,64},{64,96},{96,128},{128,160},{160,192},{192,224},{224... | collective-permute-start | bytes 417800 | tf_op jit(solution)/shard_map/ppermute | solution.py:32
  120.8 23.9 %all-to-all-start.3 = ((bf16[8,128,256]{2,1,0:T(8,128)(2,1)}), bf16[8,128,256]{2,1,0:T(8,128)(2,1)S(1)}, u32[]{:S(2)}, u32[]{:S(2)}) async-start(bf16[8,128,256]{2,1,0:T(8,128)(2,1)} %finish.1), calls=%async_computation.3 | async-start | bytes 1048576 | tf_op jit(solution)/shard_map/all_to_all | solution.py:341
  126.6 9.0 %collective-permute-start.11 = (bf16[128,256]{1,0:T(8,128)(2,1)S(1)}, bf16[128,256]{1,0:T(8,128)(2,1)S(1)}, u32[]{:S(2)}, u32[]{:S(2)}) collective-permute-start(bf16[128,256]{1,0:T(8,128)(2,1)S(1)} %get-tuple-element.18), channel_id=1, source_target_pairs={{0,8},{8,16},{16,24},{24,0},{1,9},{9,17},{17,25},{25,1},{2,10},{10... | collective-permute-start | bytes 196616 | tf_op jit(solution)/shard_map/ppermute | solution.py:26
  129.1 7.7 %collective-permute-start.12 = (bf16[128,256]{1,0:T(8,128)(2,1)S(1)}, bf16[128,256]{1,0:T(8,128)(2,1)S(1)}, u32[]{:S(2)}, u32[]{:S(2)}) collective-permute-start(bf16[128,256]{1,0:T(8,128)(2,1)S(1)} %get-tuple-element.20), channel_id=1, source_target_pairs={{0,16},{8,24},{16,0},{24,8},{1,17},{9,25},{17,1},{25,9},{2,18},{10... | collective-permute-start | bytes 196616 | tf_op jit(solution)/shard_map/ppermute | solution.py:26
  133.1 6.2 %collective-permute-start.13 = (bf16[128,256]{1,0:T(8,128)(2,1)S(1)}, bf16[128,256]{1,0:T(8,128)(2,1)S(1)}, u32[]{:S(2)}, u32[]{:S(2)}) collective-permute-start(bf16[128,256]{1,0:T(8,128)(2,1)S(1)} %get-tuple-element.17), channel_id=1, source_target_pairs={{0,24},{8,0},{16,8},{24,16},{1,25},{9,1},{17,9},{25,17},{2,26},{10... | collective-permute-start | bytes 196616 | tf_op jit(solution)/shard_map/ppermute | solution.py:26

commit v2 on v1

--- a/solution.py
+++ b/solution.py
@@ -13,11 +13,9 @@
 HEAD_DIM = 128
 EXP2_SCALE = math.log2(math.e) / math.sqrt(HEAD_DIM)
 FRAME = ("y", "core")
-EXTRA = 16
+EXTRA = 8
 TAIL = 8
-XORS = (4, 2, 1)
-MASKS = (0, 4, 2, 6, 1, 5, 3, 7)
-VMEM_BYTES = 32 * 1024 * 1024
+VMEM_BYTES = 20 * 1024 * 1024
 INTERPRET = False
 
 
@@ -32,10 +30,6 @@
     return lax.ppermute(block, axis, route)
 
 
-def across(block, axis, mask):
-    return lax.ppermute(block, axis, [(i, i ^ mask) for i in range(lax.axis_size(axis))])
-
-
 def partner(block):
     return lax.ppermute(block, "core", [(0, 1), (1, 0)])
 
@@ -52,22 +46,26 @@
     return slice(h * HEAD_DIM, (h + 1) * HEAD_DIM)
 
 
-def project_inputs(in_refs, w_ref, kv_ref):
+def project_inputs(in_refs, w_refs, kv_ref):
     low = 0
     for in_ref in in_refs:
         rows = in_ref.shape[0]
-        kv_ref[low : low + rows, :] = jnp.dot(
-            in_ref[...], w_ref[...], preferred_element_type=jnp.float32
-        ).astype(jnp.bfloat16)
+        left = 0
+        for w_ref in w_refs:
+            width = w_ref.shape[1]
+            kv_ref[low : low + rows, left : left + width] = jnp.dot(
+                in_ref[...], w_ref[...], preferred_element_type=jnp.float32
+            ).astype(jnp.bfloat16)
+            left += width
         low += rows
 
 
-def pick_queries(core_ref, mine_ref, other_ref, tile_ref):
+def pick_queries(spot_ref, mine_ref, other_ref, tile_ref):
     step = pl.program_id(0)
     tile = tile_ref.shape[0]
     per_half = mine_ref.shape[0] // tile
     start = pl.multiple_of((step % per_half) * tile, tile)
-    is_mine = step // per_half == core_ref[0]
+    is_mine = step // per_half == spot_ref[0]
 
     @pl.when(is_mine)
     def _():
@@ -86,15 +84,15 @@
     return result
 
 
-def attend_body(core_ref, mine_ref, other_ref, w_ref, *refs):
+def attend_body(spot_ref, mine_ref, other_ref, key_ref, value_ref, *refs):
     in_refs, (out_ref, kv_ref, q_ref) = refs[:-3], refs[-3:]
     width = mine_ref.shape[1]
 
     @pl.when(pl.program_id(0) == 0)
     def _():
-        project_inputs(in_refs, w_ref, kv_ref)
-
-    pick_queries(core_ref, mine_ref, other_ref, q_ref)
+        project_inputs(in_refs, (key_ref, value_ref), kv_ref)
+
+    pick_queries(spot_ref, mine_ref, other_ref, q_ref)
     tile = q_ref.shape[0]
     blocks = out_ref.shape[0]
     rows = tile // blocks
@@ -117,49 +115,38 @@
             out_ref[b, rows:, cols] = packed[:EXTRA, span].astype(jnp.bfloat16)
 
 
-def attend(core, mine, other, weight, inputs, blocks, tile):
+def attend(spot, mine, other, kv_weight, inputs, groups, blocks, tile):
     half, width = mine.shape
     latents = 2 * half
     rows = latents // blocks
+
+    def still(block):
+        return pl.BlockSpec(block.shape, lambda i, spot_ref: (0, 0))
+
+    if not INTERPRET:
+        kv_weight = pltpu.with_memory_space_constraint(kv_weight, pltpu.HBM)
+    depth = kv_weight.shape[0]
+    keys = pl.BlockSpec((depth, width), lambda i, spot_ref: (0, spot_ref[1]))
+    values = pl.BlockSpec((depth, width), lambda i, spot_ref: (0, groups + spot_ref[1]))
     return pl.pallas_call(
         attend_body,
-        grid=(latents // tile,),
-        in_specs=[pl.BlockSpec(memory_space=pltpu.SMEM)]
-        + [whole_spec(block) for block in (mine, other, weight) + inputs],
-        out_specs=pl.BlockSpec((tile // rows, rows + EXTRA, width), lambda i: (i, 0, 0)),
+        grid_spec=pltpu.PrefetchScalarGridSpec(
+            num_scalar_prefetch=1,
+            grid=(latents // tile,),
+            in_specs=[still(mine), still(other), keys, values] + [still(b) for b in inputs],
+            out_specs=pl.BlockSpec(
+                (tile // rows, rows + EXTRA, width), lambda i, spot_ref: (i, 0, 0)
+            ),
+            scratch_shapes=[
+                pltpu.VMEM((sum(b.shape[0] for b in inputs), 2 * width), jnp.bfloat16),
+                pltpu.VMEM((tile, width), jnp.bfloat16),
+            ],
+        ),
         out_shape=jax.ShapeDtypeStruct((blocks, rows + EXTRA, width), jnp.bfloat16),
-        scratch_shapes=[
-            pltpu.VMEM((sum(b.shape[0] for b in inputs), 2 * width), jnp.bfloat16),
-            pltpu.VMEM((tile, width), jnp.bfloat16),
-        ],
         compiler_params=pltpu.CompilerParams(vmem_limit_bytes=VMEM_BYTES),
         interpret=INTERPRET,
         name="attend",
-    )(core, mine, other, weight, *inputs)
-
-
-def order_body(place_ref, first_ref, second_ref, out_ref):
-    rows = out_ref.shape[0] // len(MASKS)
-    half = len(MASKS) // 2
-    for j, mask in enumerate(MASKS):
-        part_ref = (first_ref, second_ref)[j // half]
-        low = (j % half) * rows
-        at = pl.multiple_of((place_ref[0] ^ mask) * rows, rows)
-        out_ref[pl.ds(at, rows), :] = part_ref[low : low + rows, :]
-
-
-def order(place, first, second):
-    shape = (2 * first.shape[0], first.shape[1])
-    return pl.pallas_call(
-        order_body,
-        grid=(1,),
-        in_specs=[pl.BlockSpec(memory_space=pltpu.SMEM), whole_spec(first), whole_spec(second)],
-        out_specs=pl.BlockSpec(shape, lambda i: (0, 0)),
-        out_shape=jax.ShapeDtypeStruct(shape, first.dtype),
-        compiler_params=pltpu.CompilerParams(vmem_limit_bytes=VMEM_BYTES // 2),
-        interpret=INTERPRET,
-        name="order",
-    )(place, first, second)
+    )(spot, mine, other, kv_weight, kv_weight, *inputs)
 
 
 def combine_body(part_ref, out_ref):
@@ -292,14 +279,13 @@
     )(own, one, two)
 
 
-def decode_body(place_ref, mixed_ref, *refs):
-    query_refs, out_ref = refs[:-1], refs[-1]
+def decode_body(place_ref, mixed_ref, query_ref, out_ref):
     groups, rows, width = out_ref.shape
     pair = 2
     for k in range(0, groups, pair):
         for h in range(width // HEAD_DIM):
             cols = head_cols(h)
-            queries = jnp.concatenate([ref[:, cols] for ref in query_refs[k : k + pair]], axis=0)
+            queries = query_ref[k * rows : (k + pair) * rows, cols]
             scores = dot_nt(queries, mixed_ref[:, cols])
             peak = jnp.max(scores, axis=1, keepdims=True)
             weights = jnp.exp2((scores - peak) * EXP2_SCALE)
@@ -313,28 +299,31 @@
                 out_ref[at, :, cols] = result[p * rows : (p + 1) * rows]
 
 
-def decode(place, mixed, queries):
-    rows, width = queries[0].shape
-    shape = (len(queries), rows, width)
+def decode(place, mixed, queries, groups):
+    count, width = queries.shape
+    shape = (groups, count // groups, width)
     return pl.pallas_call(
         decode_body,
         grid=(1,),
-        in_specs=[pl.BlockSpec(memory_space=pltpu.SMEM)]
-        + [whole_spec(block) for block in (mixed,) + queries],
+        in_specs=[
+            pl.BlockSpec(memory_space=pltpu.SMEM),
+            whole_spec(mixed),
+            whole_spec(queries),
+        ],
         out_specs=pl.BlockSpec(shape, lambda i: (0, 0, 0)),
         out_shape=jax.ShapeDtypeStruct(shape, jnp.float32),
         compiler_params=pltpu.CompilerParams(vmem_limit_bytes=VMEM_BYTES),
         interpret=INTERPRET,
         name="decode",
-    )(place, mixed, *queries)
+    )(place, mixed, queries)
 
 
 def scalar(index):
     return index.reshape(1).astype(jnp.int32)
 
 
-def join(first, second):
-    return jnp.concatenate([first, second], axis=0)
+def join(*blocks):
+    return jnp.concatenate(blocks, axis=0)
 
 
 def all_to_all(block, axis):
@@ -357,10 +346,11 @@
 
     mix_t = mix_weight.T
     mix_half = mix_t.shape[1] // 2
-    held = lax.dynamic_slice_in_dim(mix_t, core_index * mix_half, mix_half, axis=1)
-    for mask in XORS[:-1]:
-        held = join(held, across(held, "z", mask))
-    brought = across(held, "z", XORS[-1])
+    mix_mine = lax.dynamic_slice_in_dim(mix_t, core_index * mix_half, mix_half, axis=1)
+    mix_mine = jnp.broadcast_to(mix_mine[None], (members,) + mix_mine.shape)
+    mix_mine = all_to_all(mix_mine, "z")
+    mix_mine = mix_mine.reshape(members * mix_t.shape[0], mix_half)
+    mix_other = partner(mix_mine)
 
     rows = latent_queries.shape[0] // 2
     asked = lax.dynamic_slice_in_dim(latent_queries, core_index * rows, rows, axis=0)
@@ -375,20 +365,14 @@
     far_low = shift(far_low, "x", -1)
     far_high = below[half:]
     far_high = shift(far_high, "x", 1)
-    weight = jnp.concatenate(
-        [
-            lax.dynamic_slice_in_dim(kv_weight, place * width, width, axis=1),
-            lax.dynamic_slice_in_dim(kv_weight, latent_width + place * width, width, axis=1),
-        ],
-        axis=1,
-    )
     latents = groups * members * rows * 2
     parts = attend(
-        core,
+        jnp.stack([core_index, place]).astype(jnp.int32),
         asked,
         asked_other,
-        weight,
+        kv_weight,
         (mine, above, below, far_low, far_high),
+        groups,
         members,
         latents // 4,
     )
@@ -399,8 +383,7 @@
         to = (place + k) % groups
         sent = lax.dynamic_slice_in_dim(output_queries[0], to * width, width, axis=1)
         queries.append(shift(sent, "x", k) if k else sent)
-    mix_mine = order(scalar(lax.axis_index("z")), held, brought)
-    mix_other = partner(mix_mine)
+    sent = lax.optimization_barrier(join(*queries[1:]))
 
     window = all_to_all(combine(parts, groups), "x")
     own, one, two = products(core, window, mix_gain[None], mix_mine, mix_other)
@@ -408,8 +391,9 @@
     two = from_behind(two, FRAME, 2)
     mixed = finish(own, one, two, members, 3 * latent_width)
     mixed = all_to_all(mixed, "z").reshape(latents, width)
-
-    decoded = decode(scalar(place), mixed, tuple(queries))
+    queries = join(queries[0], sent)
+
+    decoded = decode(scalar(place), mixed, queries, groups)
     decoded = all_to_all(decoded, "x")
     return jnp.concatenate([decoded[g] for g in range(groups)], axis=1)[None]
 

time: 161 us -> 166 us (1.031)
  the two profiles are of different devices: /device:TPU:16 before, /device:TPU:32 now
where the time goes in v2:
time: 166 us; the launch traced here: 165 us
  waiting for transfers between devices  68 us (41%)
  starting transfers between devices  59.4 us (36%)
  Pallas kernels  20 us (12%)
  blocking collectives  12.3 us (7%)
  local copies, waits for them, and re-layouts  4.13 us (2%)
    all_to_all x5, waiting for transfers between devices, all_to_all(): return lax.all_to_all(block, axis, 0, 0, tiled=True)  35.1 us
    all_to_all x5, starting transfers between devices, all_to_all(): return lax.all_to_all(block, axis, 0, 0, tiled=True)  30.6 us
    ppermute x7, waiting for transfers between devices, shift(): lax.ppermute(block, axis, [(i, (i + distance) % size) for i in range(size)])  24.6 us
    ppermute x7, starting transfers between devices, shift(): lax.ppermute(block, axis, [(i, (i + distance) % size) for i in range(size)])  20.4 us
    pallas_call x1, Pallas kernels, attend(): pl.pallas_call(attend_body, grid_spec=pltpu.PrefetchScalarGridSpec(num_sc...  14.8 us
    all_to_all x1, blocking collectives, all_to_all(): return lax.all_to_all(block, axis, 0, 0, tiled=True)  12.3 us
    ppermute x2, waiting for transfers between devices, from_behind(): return lax.ppermute(block, axis, route)  6.87 us
    ppermute x2, starting transfers between devices, from_behind(): return lax.ppermute(block, axis, route)  4.51 us
  transfers between devices with their start and end apart: 16, of which 11 were waited for; matrix products, arithmetic and copies ran while one was open for 1% of the time, Pallas kernels for 10%

profile of v2, /device:TPU:32, one launch (start us, length us, event | category | flops | bytes accessed | tf_op | source)
XLA Modules:
  0.0 165.1 jit_solution(16280519447898390103)
XLA Ops:
  1.5 13.2 %all-to-all-start = ((bf16[32,16,256]{2,1,0:T(8,128)(2,1)}), bf16[32,16,256]{2,1,0:T(8,128)(2,1)S(1)}, u32[]{:S(2)}, u32[]{:S(2)}) async-start(bf16[32,16,256]{2,1,0:T(8,128)(2,1)} %bitcast.6), calls=%async_computation | async-start | bytes 524288 | tf_op jit(solution)/shard_map/all_to_all | solution.py:330
  14.7 12.4 %all-to-all-done = bf16[32,16,256]{2,1,0:T(8,128)(2,1)S(1)} async-done(((bf16[32,16,256]{2,1,0:T(8,128)(2,1)}), bf16[32,16,256]{2,1,0:T(8,128)(2,1)S(1)}, u32[]{:S(2)}, u32[]{:S(2)}) %all-to-all-start) | async-done | bytes 262176 | tf_op jit(solution)/shard_map/all_to_all | solution.py:330
  28.1 3.5 %all-to-all-start.3 = ((bf16[8,32,1536]{2,1,0:T(8,128)(2,1)}), bf16[8,32,1536]{2,1,0:T(8,128)(2,1)S(1)}, u32[]{:S(2)}, u32[]{:S(2)}) async-start(bf16[8,32,1536]{2,1,0:T(8,128)(2,1)} %broadcast_in_dim.20), calls=%async_computation.3 | async-start | bytes 1572864 | tf_op jit(solution)/shard_map/all_to_all | solution.py:330
  31.6 3.1 %collective-permute-start.1 = (bf16[768,512]{1,0:T(8,128)(2,1)}, bf16[768,512]{1,0:T(8,128)(2,1)S(1)}, u32[]{:S(2)}, u32[]{:S(2)}) collective-permute-start(bf16[768,512]{1,0:T(8,128)(2,1)} %bitcast.8.refs_0_), channel_id=1, source_target_pairs={{0,24},{8,0},{16,8},{24,16},{1,25},{9,1},{17,9},{25,17},{2,26},{10... | collective-permute-start | bytes 2359304 | tf_op jit(solution)/shard_map/ppermute | solution.py:24
  34.7 2.8 %collective-permute-start.2 = (bf16[768,512]{1,0:T(8,128)(2,1)}, bf16[768,512]{1,0:T(8,128)(2,1)S(1)}, u32[]{:S(2)}, u32[]{:S(2)}) collective-permute-start(bf16[768,512]{1,0:T(8,128)(2,1)} %bitcast.8.refs_0_), channel_id=1, source_target_pairs={{0,8},{8,16},{16,24},{24,0},{1,9},{9,17},{17,25},{25,1},{2,10},{10... | collective-permute-start | bytes 2359304 | tf_op jit(solution)/shard_map/ppermute | solution.py:24
  37.5 13.6 %collective-permute-done.1.refs_1_ = bf16[768,512]{1,0:T(8,128)(2,1)S(1)} collective-permute-done((bf16[768,512]{1,0:T(8,128)(2,1)}, bf16[768,512]{1,0:T(8,128)(2,1)S(1)}, u32[]{:S(2)}, u32[]{:S(2)}) %collective-permute-start.1) | collective-permute-done | bytes 786464 | tf_op jit(solution)/shard_map/ppermute | solution.py:24
  51.9 4.3 %collective-permute-start.3 = (bf16[384,512]{1,0:T(8,128)(2,1)}, bf16[384,512]{1,0:T(8,128)(2,1)S(1)}, u32[]{:S(2)}, u32[]{:S(2)}) collective-permute-start(bf16[384,512]{1,0:T(8,128)(2,1)} %slice.40), channel_id=1, source_target_pairs={{0,24},{8,0},{16,8},{24,16},{1,25},{9,1},{17,9},{25,17},{2,26},{10... | collective-permute-start | bytes 1179656 | tf_op jit(solution)/shard_map/ppermute | solution.py:24
  62.4 5.9 %collective-permute-done.4.refs_4_ = bf16[384,512]{1,0:T(8,128)(2,1)} collective-permute-done((bf16[384,512]{1,0:T(8,128)(2,1)}, bf16[384,512]{1,0:T(8,128)(2,1)}, u32[]{:S(2)}, u32[]{:S(2)}) %collective-permute-start.4) | collective-permute-done | bytes 393248 | tf_op jit(solution)/shard_map/ppermute | solution.py:24
  68.2 14.8 %attend.1 = bf16[8,136,256]{2,1,0:T(8,128)(2,1)} custom-call(s32[2]{0:T(128)S(1)} %pad_add_fusion.spot_ref, bf16[512,256]{1,0:T(8,128)(2,1)S(1)} %bitcast.40, bf16[512,256]{1,0:T(8,128)(2,1)S(1)} %collective-permute-done.other_ref, bf16[512,2048]{1,0:T(8,128)(2,1)} %value_ref.1, bf16[512,2048]{1,0:T(8,128)(2,1)} %value_ref.1, ...), custom_call_target="tpu_custom_call" | custom-call | tf_op jit(solution)/shard_map/attend/pallas_call | solution.py:131
  83.1 7.0 %all-to-all-start.1 = ((bf16[8,136,256]{2,1,0:T(8,128)(2,1)}), bf16[8,136,256]{2,1,0:T(8,128)(2,1)S(1)}, u32[]{:S(2)}, u32[]{:S(2)}) async-start(bf16[8,136,256]{2,1,0:T(8,128)(2,1)} %attend.1), calls=%async_computation.1 | async-start | bytes 1114112 | tf_op jit(solution)/shard_map/all_to_all | solution.py:330
  92.0 12.0 %all-to-all-done.1.part_ref = bf16[8,136,256]{2,1,0:T(8,128)(2,1)S(1)} async-done(((bf16[8,136,256]{2,1,0:T(8,128)(2,1)}), bf16[8,136,256]{2,1,0:T(8,128)(2,1)S(1)}, u32[]{:S(2)}, u32[]{:S(2)}) %all-to-all-start.1) | async-done | bytes 557088 | tf_op jit(solution)/shard_map/all_to_all | solution.py:330
  105.3 3.4 %all-to-all-start.2 = ((bf16[4,128,256]{2,1,0:T(8,128)(2,1)}), bf16[4,128,256]{2,1,0:T(8,128)(2,1)S(1)}, u32[]{:S(2)}, u32[]{:S(2)}) async-start(bf16[4,128,256]{2,1,0:T(8,128)(2,1)} %combine.1), calls=%async_computation.2 | async-start | bytes 524288 | tf_op jit(solution)/shard_map/all_to_all | solution.py:330
  108.7 6.6 %all-to-all-done.2.rows_ref = bf16[4,128,256]{2,1,0:T(8,128)(2,1)S(1)} async-done(((bf16[4,128,256]{2,1,0:T(8,128)(2,1)}), bf16[4,128,256]{2,1,0:T(8,128)(2,1)S(1)}, u32[]{:S(2)}, u32[]{:S(2)}) %all-to-all-start.2) | async-done | bytes 262176 | tf_op jit(solution)/shard_map/all_to_all | solution.py:330
  118.1 2.6 %collective-permute-start.7 = (f32[136,256]{1,0:T(8,128)S(1)}, f32[136,256]{1,0:T(8,128)S(1)}, u32[]{:S(2)}, u32[]{:S(2)}) collective-permute-start(f32[136,256]{1,0:T(8,128)S(1)} %get-tuple-element.10), channel_id=1, source_target_pairs={{0,64},{32,96},{64,128},{96,160},{128,192},{160,224},{192,256},{22... | collective-permute-start | bytes 417800 | tf_op jit(solution)/shard_map/ppermute | solution.py:30
  120.7 3.1 %collective-permute-done.6.refs_1_ = f32[136,256]{1,0:T(8,128)S(1)} collective-permute-done((f32[136,256]{1,0:T(8,128)S(1)}, f32[136,256]{1,0:T(8,128)S(1)}, u32[]{:S(2)}, u32[]{:S(2)}) %collective-permute-start.6) | collective-permute-done | bytes 139296 | tf_op jit(solution)/shard_map/ppermute | solution.py:30
  123.7 3.8 %collective-permute-done.7.refs_2_ = f32[136,256]{1,0:T(8,128)S(1)} collective-permute-done((f32[136,256]{1,0:T(8,128)S(1)}, f32[136,256]{1,0:T(8,128)S(1)}, u32[]{:S(2)}, u32[]{:S(2)}) %collective-permute-start.7) | collective-permute-done | bytes 139296 | tf_op jit(solution)/shard_map/ppermute | solution.py:30
  128.6 3.5 %all-to-all-start.4 = ((bf16[8,128,256]{2,1,0:T(8,128)(2,1)}), bf16[8,128,256]{2,1,0:T(8,128)(2,1)S(1)}, u32[]{:S(2)}, u32[]{:S(2)}) async-start(bf16[8,128,256]{2,1,0:T(8,128)(2,1)} %finish.1), calls=%async_computation.4 | async-start | bytes 1048576 | tf_op jit(solution)/shard_map/all_to_all | solution.py:330
  132.2 3.1 %collective-permute-start.10 = (bf16[128,256]{1,0:T(8,128)(2,1)S(1)}, bf16[128,256]{1,0:T(8,128)(2,1)S(1)}, u32[]{:S(2)}, u32[]{:S(2)}) collective-permute-start(bf16[128,256]{1,0:T(8,128)(2,1)S(1)} %get-tuple-element.17), channel_id=1, source_target_pairs={{0,24},{8,0},{16,8},{24,16},{1,25},{9,1},{17,9},{25,17},{2,26},{10... | collective-permute-start | bytes 196616 | tf_op jit(solution)/shard_map/ppermute | solution.py:24
  135.3 2.8 %collective-permute-start.8 = (bf16[128,256]{1,0:T(8,128)(2,1)S(1)}, bf16[128,256]{1,0:T(8,128)(2,1)S(1)}, u32[]{:S(2)}, u32[]{:S(2)}) collective-permute-start(bf16[128,256]{1,0:T(8,128)(2,1)S(1)} %get-tuple-element.16), channel_id=1, source_target_pairs={{0,8},{8,16},{16,24},{24,0},{1,9},{9,17},{17,25},{25,1},{2,10},{10... | collective-permute-start | bytes 196616 | tf_op jit(solution)/shard_map/ppermute | solution.py:24
  138.0 2.5 %collective-permute-start.9 = (bf16[128,256]{1,0:T(8,128)(2,1)S(1)}, bf16[128,256]{1,0:T(8,128)(2,1)S(1)}, u32[]{:S(2)}, u32[]{:S(2)}) collective-permute-start(bf16[128,256]{1,0:T(8,128)(2,1)S(1)} %get-tuple-element.18), channel_id=1, source_target_pairs={{0,16},{8,24},{16,0},{24,8},{1,17},{9,25},{17,1},{25,9},{2,18},{10... | collective-permute-start | bytes 196616 | tf_op jit(solution)/shard_map/ppermute | solution.py:24
  140.6 2.0 %collective-permute-done.8 = bf16[128,256]{1,0:T(8,128)(2,1)S(1)} collective-permute-done((bf16[128,256]{1,0:T(8,128)(2,1)S(1)}, bf16[128,256]{1,0:T(8,128)(2,1)S(1)}, u32[]{:S(2)}, u32[]{:S(2)}) %collective-permute-start.8) | collective-permute-done | bytes 65568 | tf_op jit(solution)/shard_map/ppermute | solution.py:24
  142.6 3.1 %collective-permute-done.9 = bf16[128,256]{1,0:T(8,128)(2,1)S(1)} collective-permute-done((bf16[128,256]{1,0:T(8,128)(2,1)S(1)}, bf16[128,256]{1,0:T(8,128)(2,1)S(1)}, u32[]{:S(2)}, u32[]{:S(2)}) %collective-permute-start.9) | collective-permute-done | bytes 65568 | tf_op jit(solution)/shard_map/ppermute | solution.py:24
  145.8 4.1 %all-to-all-done.4 = bf16[8,128,256]{2,1,0:T(8,128)(2,1)S(1)} async-done(((bf16[8,128,256]{2,1,0:T(8,128)(2,1)}), bf16[8,128,256]{2,1,0:T(8,128)(2,1)S(1)}, u32[]{:S(2)}, u32[]{:S(2)}) %all-to-all-start.4) | async-done | bytes 524320 | tf_op jit(solution)/shard_map/all_to_all | solution.py:330
  151.9 12.3 %all_to_all.30 = f32[4,128,256]{2,1,0:T(8,128)S(1)} all-to-all(f32[4,128,256]{2,1,0:T(8,128)S(1)} %decode.1), channel_id=1, replica_groups=mesh['y'=8,'core'=2,'x'=4,'z'=8] {'x'}, dimensions={0} | all-to-all | bytes 1048576 | tf_op jit(solution)/shard_map/all_to_all | solution.py:330
  (33 shorter events, 19.3 us)
Async XLA Ops:
  0.0 14.7 %copy-start = (bf16[3072,32]{0,1:T(8,128)(2,1)S(1)}, bf16[3072,32]{0,1:T(8,128)(2,1)}, u32[]{:S(2)}) copy-start(bf16[3072,32]{0,1:T(8,128)(2,1)} %param.10) | copy-start | bytes 589828
  1.5 25.6 %all-to-all-start = ((bf16[32,16,256]{2,1,0:T(8,128)(2,1)}), bf16[32,16,256]{2,1,0:T(8,128)(2,1)S(1)}, u32[]{:S(2)}, u32[]{:S(2)}) async-start(bf16[32,16,256]{2,1,0:T(8,128)(2,1)} %bitcast.6), calls=%async_computation | async-start | bytes 524288 | tf_op jit(solution)/shard_map/all_to_all | solution.py:330
  28.1 55.0 %all-to-all-start.3 = ((bf16[8,32,1536]{2,1,0:T(8,128)(2,1)}), bf16[8,32,1536]{2,1,0:T(8,128)(2,1)S(1)}, u32[]{:S(2)}, u32[]{:S(2)}) async-start(bf16[8,32,1536]{2,1,0:T(8,128)(2,1)} %broadcast_in_dim.20), calls=%async_computation.3 | async-start | bytes 1572864 | tf_op jit(solution)/shard_map/all_to_all | solution.py:330
  31.6 19.5 %collective-permute-start.1 = (bf16[768,512]{1,0:T(8,128)(2,1)}, bf16[768,512]{1,0:T(8,128)(2,1)S(1)}, u32[]{:S(2)}, u32[]{:S(2)}) collective-permute-start(bf16[768,512]{1,0:T(8,128)(2,1)} %bitcast.8.refs_0_), channel_id=1, source_target_pairs={{0,24},{8,0},{16,8},{24,16},{1,25},{9,1},{17,9},{25,17},{2,26},{10... | collective-permute-start | bytes 2359304 | tf_op jit(solution)/shard_map/ppermute | solution.py:24
  34.7 21.5 %collective-permute-start.2 = (bf16[768,512]{1,0:T(8,128)(2,1)}, bf16[768,512]{1,0:T(8,128)(2,1)S(1)}, u32[]{:S(2)}, u32[]{:S(2)}) collective-permute-start(bf16[768,512]{1,0:T(8,128)(2,1)} %bitcast.8.refs_0_), channel_id=1, source_target_pairs={{0,8},{8,16},{16,24},{24,0},{1,9},{9,17},{17,25},{25,1},{2,10},{10... | collective-permute-start | bytes 2359304 | tf_op jit(solution)/shard_map/ppermute | solution.py:24
  51.9 10.5 %collective-permute-start.3 = (bf16[384,512]{1,0:T(8,128)(2,1)}, bf16[384,512]{1,0:T(8,128)(2,1)S(1)}, u32[]{:S(2)}, u32[]{:S(2)}) collective-permute-start(bf16[384,512]{1,0:T(8,128)(2,1)} %slice.40), channel_id=1, source_target_pairs={{0,24},{8,0},{16,8},{24,16},{1,25},{9,1},{17,9},{25,17},{2,26},{10... | collective-permute-start | bytes 1179656 | tf_op jit(solution)/shard_map/ppermute | solution.py:24
  57.0 11.2 %collective-permute-start.4 = (bf16[384,512]{1,0:T(8,128)(2,1)}, bf16[384,512]{1,0:T(8,128)(2,1)}, u32[]{:S(2)}, u32[]{:S(2)}) collective-permute-start(bf16[384,512]{1,0:T(8,128)(2,1)} %slice.41), channel_id=1, source_target_pairs={{0,8},{8,16},{16,24},{24,0},{1,9},{9,17},{17,25},{25,1},{2,10},{10... | collective-permute-start | bytes 1179656 | tf_op jit(solution)/shard_map/ppermute | solution.py:24
  58.9 3.4 %collective-permute-start = (bf16[512,256]{1,0:T(8,128)(2,1)S(1)}, bf16[512,256]{1,0:T(8,128)(2,1)S(1)}, u32[]{:S(2)}, u32[]{:S(2)}) collective-permute-start(bf16[512,256]{1,0:T(8,128)(2,1)S(1)} %bitcast.39), channel_id=1, source_target_pairs={{0,32},{32,0},{1,33},{33,1},{2,34},{34,2},{3,35},{35,3},{4,36},{36... | collective-permute-start | bytes 786440 | tf_op jit(solution)/shard_map/ppermute | solution.py:34
  83.1 32.3 %copy-start.1 = (f32[3072]{0:T(1024)S(1)}, f32[3072]{0:T(1024)}, u32[]{:S(2)}) copy-start(f32[3072]{0:T(1024)} %param.9) | copy-start | bytes 36868
  83.1 20.9 %all-to-all-start.1 = ((bf16[8,136,256]{2,1,0:T(8,128)(2,1)}), bf16[8,136,256]{2,1,0:T(8,128)(2,1)S(1)}, u32[]{:S(2)}, u32[]{:S(2)}) async-start(bf16[8,136,256]{2,1,0:T(8,128)(2,1)} %attend.1), calls=%async_computation.1 | async-start | bytes 1114112 | tf_op jit(solution)/shard_map/all_to_all | solution.py:330
  90.1 18.6 %collective-permute-start.5 = (bf16[256,1536]{1,0:T(8,128)(2,1)S(1)}, bf16[256,1536]{1,0:T(8,128)(2,1)S(1)}, u32[]{:S(2)}, u32[]{:S(2)}) collective-permute-start(bf16[256,1536]{1,0:T(8,128)(2,1)S(1)} %bitcast.36), channel_id=1, source_target_pairs={{0,32},{32,0},{1,33},{33,1},{2,34},{34,2},{3,35},{35,3},{4,36},{36... | collective-permute-start | bytes 2359304 | tf_op jit(solution)/shard_map/ppermute | solution.py:34
  105.3 10.1 %all-to-all-start.2 = ((bf16[4,128,256]{2,1,0:T(8,128)(2,1)}), bf16[4,128,256]{2,1,0:T(8,128)(2,1)S(1)}, u32[]{:S(2)}, u32[]{:S(2)}) async-start(bf16[4,128,256]{2,1,0:T(8,128)(2,1)} %combine.1), calls=%async_computation.2 | async-start | bytes 524288 | tf_op jit(solution)/shard_map/all_to_all | solution.py:330
  108.7 23.4 %copy-start.2 = (bf16[1,128,1024]{2,1,0:T(8,128)(2,1)S(1)}, bf16[1,128,1024]{2,1,0:T(8,128)(2,1)}, u32[]{:S(2)}) copy-start(bf16[1,128,1024]{2,1,0:T(8,128)(2,1)} %param.11) | copy-start | bytes 786436
  116.2 7.6 %collective-permute-start.6 = (f32[136,256]{1,0:T(8,128)S(1)}, f32[136,256]{1,0:T(8,128)S(1)}, u32[]{:S(2)}, u32[]{:S(2)}) collective-permute-start(f32[136,256]{1,0:T(8,128)S(1)} %get-tuple-element.9), channel_id=1, source_target_pairs={{0,32},{32,64},{64,96},{96,128},{128,160},{160,192},{192,224},{224... | collective-permute-start | bytes 417800 | tf_op jit(solution)/shard_map/ppermute | solution.py:30
  118.1 9.5 %collective-permute-start.7 = (f32[136,256]{1,0:T(8,128)S(1)}, f32[136,256]{1,0:T(8,128)S(1)}, u32[]{:S(2)}, u32[]{:S(2)}) collective-permute-start(f32[136,256]{1,0:T(8,128)S(1)} %get-tuple-element.10), channel_id=1, source_target_pairs={{0,64},{32,96},{64,128},{96,160},{128,192},{160,224},{192,256},{22... | collective-permute-start | bytes 417800 | tf_op jit(solution)/shard_map/ppermute | solution.py:30
  128.6 21.3 %all-to-all-start.4 = ((bf16[8,128,256]{2,1,0:T(8,128)(2,1)}), bf16[8,128,256]{2,1,0:T(8,128)(2,1)S(1)}, u32[]{:S(2)}, u32[]{:S(2)}) async-start(bf16[8,128,256]{2,1,0:T(8,128)(2,1)} %finish.1), calls=%async_computation.4 | async-start | bytes 1048576 | tf_op jit(solution)/shard_map/all_to_all | solution.py:330
  132.2 8.4 %collective-permute-start.10 = (bf16[128,256]{1,0:T(8,128)(2,1)S(1)}, bf16[128,256]{1,0:T(8,128)(2,1)S(1)}, u32[]{:S(2)}, u32[]{:S(2)}) collective-permute-start(bf16[128,256]{1,0:T(8,128)(2,1)S(1)} %get-tuple-element.17), channel_id=1, source_target_pairs={{0,24},{8,0},{16,8},{24,16},{1,25},{9,1},{17,9},{25,17},{2,26},{10... | collective-permute-start | bytes 196616 | tf_op jit(solution)/shard_map/ppermute | solution.py:24
  135.3 7.4 %collective-permute-start.8 = (bf16[128,256]{1,0:T(8,128)(2,1)S(1)}, bf16[128,256]{1,0:T(8,128)(2,1)S(1)}, u32[]{:S(2)}, u32[]{:S(2)}) collective-permute-start(bf16[128,256]{1,0:T(8,128)(2,1)S(1)} %get-tuple-element.16), channel_id=1, source_target_pairs={{0,8},{8,16},{16,24},{24,0},{1,9},{9,17},{17,25},{25,1},{2,10},{10... | collective-permute-start | bytes 196616 | tf_op jit(solution)/shard_map/ppermute | solution.py:24
  138.0 7.7 %collective-permute-start.9 = (bf16[128,256]{1,0:T(8,128)(2,1)S(1)}, bf16[128,256]{1,0:T(8,128)(2,1)S(1)}, u32[]{:S(2)}, u32[]{:S(2)}) collective-permute-start(bf16[128,256]{1,0:T(8,128)(2,1)S(1)} %get-tuple-element.18), channel_id=1, source_target_pairs={{0,16},{8,24},{16,0},{24,8},{1,17},{9,25},{17,1},{25,9},{2,18},{10... | collective-permute-start | bytes 196616 | tf_op jit(solution)/shard_map/ppermute | solution.py:24

commit v3 on v2

--- a/solution.py
+++ b/solution.py
@@ -15,6 +15,8 @@
 FRAME = ("y", "core")
 EXTRA = 8
 TAIL = 8
+XORS = (4, 2, 1)
+MASKS = (0, 4, 2, 6, 1, 5, 3, 7)
 VMEM_BYTES = 20 * 1024 * 1024
 INTERPRET = False
 
@@ -28,6 +30,10 @@
     devices = range(lax.axis_size(axis))
     route = [(i - distance, i) for i in devices if i - distance in devices]
     return lax.ppermute(block, axis, route)
+
+
+def across(block, axis, mask):
+    return lax.ppermute(block, axis, [(i, i ^ mask) for i in range(lax.axis_size(axis))])
 
 
 def partner(block):
@@ -147,6 +153,30 @@
         interpret=INTERPRET,
         name="attend",
     )(spot, mine, other, kv_weight, kv_weight, *inputs)
+
+
+def order_body(place_ref, first_ref, second_ref, out_ref):
+    rows = out_ref.shape[0] // len(MASKS)
+    half = len(MASKS) // 2
+    for j, mask in enumerate(MASKS):
+        part_ref = (first_ref, second_ref)[j // half]
+        low = (j % half) * rows
+        at = pl.multiple_of((place_ref[0] ^ mask) * rows, rows)
+        out_ref[pl.ds(at, rows), :] = part_ref[low : low + rows, :]
+
+
+def order(place, first, second):
+    shape = (2 * first.shape[0], first.shape[1])
+    return pl.pallas_call(
+        order_body,
+        grid=(1,),
+        in_specs=[pl.BlockSpec(memory_space=pltpu.SMEM), whole_spec(first), whole_spec(second)],
+        out_specs=pl.BlockSpec(shape, lambda i: (0, 0)),
+        out_shape=jax.ShapeDtypeStruct(shape, first.dtype),
+        compiler_params=pltpu.CompilerParams(vmem_limit_bytes=VMEM_BYTES // 2),
+        interpret=INTERPRET,
+        name="order",
+    )(place, first, second)
 
 
 def combine_body(part_ref, out_ref):
@@ -279,13 +309,14 @@
     )(own, one, two)
 
 
-def decode_body(place_ref, mixed_ref, query_ref, out_ref):
+def decode_body(place_ref, mixed_ref, *refs):
+    query_refs, out_ref = refs[:-1], refs[-1]
     groups, rows, width = out_ref.shape
     pair = 2
     for k in range(0, groups, pair):
         for h in range(width // HEAD_DIM):
             cols = head_cols(h)
-            queries = query_ref[k * rows : (k + pair) * rows, cols]
+            queries = jnp.concatenate([ref[:, cols] for ref in query_refs[k : k + pair]], axis=0)
             scores = dot_nt(queries, mixed_ref[:, cols])
             peak = jnp.max(scores, axis=1, keepdims=True)
             weights = jnp.exp2((scores - peak) * EXP2_SCALE)
@@ -299,31 +330,28 @@
                 out_ref[at, :, cols] = result[p * rows : (p + 1) * rows]
 
 
-def decode(place, mixed, queries, groups):
-    count, width = queries.shape
-    shape = (groups, count // groups, width)
+def decode(place, mixed, queries):
+    rows, width = queries[0].shape
+    shape = (len(queries), rows, width)
     return pl.pallas_call(
         decode_body,
         grid=(1,),
-        in_specs=[
-            pl.BlockSpec(memory_space=pltpu.SMEM),
-            whole_spec(mixed),
-            whole_spec(queries),
-        ],
+        in_specs=[pl.BlockSpec(memory_space=pltpu.SMEM)]
+        + [whole_spec(block) for block in (mixed,) + queries],
         out_specs=pl.BlockSpec(shape, lambda i: (0, 0, 0)),
         out_shape=jax.ShapeDtypeStruct(shape, jnp.float32),
         compiler_params=pltpu.CompilerParams(vmem_limit_bytes=VMEM_BYTES),
         interpret=INTERPRET,
         name="decode",
-    )(place, mixed, queries)
+    )(place, mixed, *queries)
 
 
 def scalar(index):
     return index.reshape(1).astype(jnp.int32)
 
 
-def join(*blocks):
-    return jnp.concatenate(blocks, axis=0)
+def join(first, second):
+    return jnp.concatenate([first, second], axis=0)
 
 
 def all_to_all(block, axis):
@@ -346,11 +374,10 @@
 
     mix_t = mix_weight.T
     mix_half = mix_t.shape[1] // 2
-    mix_mine = lax.dynamic_slice_in_dim(mix_t, core_index * mix_half, mix_half, axis=1)
-    mix_mine = jnp.broadcast_to(mix_mine[None], (members,) + mix_mine.shape)
-    mix_mine = all_to_all(mix_mine, "z")
-    mix_mine = mix_mine.reshape(members * mix_t.shape[0], mix_half)
-    mix_other = partner(mix_mine)
+    held = lax.dynamic_slice_in_dim(mix_t, core_index * mix_half, mix_half, axis=1)
+    for mask in XORS[:-1]:
+        held = join(held, across(held, "z", mask))
+    brought = across(held, "z", XORS[-1])
 
     rows = latent_queries.shape[0] // 2
     asked = lax.dynamic_slice_in_dim(latent_queries, core_index * rows, rows, axis=0)
@@ -383,7 +410,8 @@
         to = (place + k) % groups
         sent = lax.dynamic_slice_in_dim(output_queries[0], to * width, width, axis=1)
         queries.append(shift(sent, "x", k) if k else sent)
-    sent = lax.optimization_barrier(join(*queries[1:]))
+    mix_mine = order(scalar(lax.axis_index("z")), held, brought)
+    mix_other = partner(mix_mine)
 
     window = all_to_all(combine(parts, groups), "x")
     own, one, two = products(core, window, mix_gain[None], mix_mine, mix_other)
@@ -391,9 +419,8 @@
     two = from_behind(two, FRAME, 2)
     mixed = finish(own, one, two, members, 3 * latent_width)
     mixed = all_to_all(mixed, "z").reshape(latents, width)
-    queries = join(queries[0], sent)
-
-    decoded = decode(scalar(place), mixed, queries, groups)
+
+    decoded = decode(scalar(place), mixed, tuple(queries))
     decoded = all_to_all(decoded, "x")
     return jnp.concatenate([decoded[g] for g in range(groups)], axis=1)[None]
 

time: 166 us -> 148 us (0.89)
  the two profiles are of different devices: /device:TPU:32 before, /device:TPU:16 now
where the time goes in v3:
time: 148 us; the launch traced here: 147 us
  starting transfers between devices  68.3 us (46%)
  waiting for transfers between devices  40.1 us (27%)
  Pallas kernels  20.9 us (14%)
  blocking collectives  12.4 us (8%)
  local copies, waits for them, and re-layouts  3.16 us (2%)
  other arithmetic  1.9 us (1%)
    all_to_all x4, waiting for transfers between devices, all_to_all(): return lax.all_to_all(block, axis, 0, 0, tiled=True)  31.3 us
    ppermute x7, starting transfers between devices, shift(): lax.ppermute(block, axis, [(i, (i + distance) % size) for i in range(size)])  22.2 us
    all_to_all x4, starting transfers between devices, all_to_all(): return lax.all_to_all(block, axis, 0, 0, tiled=True)  19.4 us
    ppermute x3, starting transfers between devices, across(): lax.ppermute(block, axis, [(i, i ^ mask) for i in range(lax.axis_size(axi...  17.4 us
    pallas_call x1, Pallas kernels, attend(): pl.pallas_call(attend_body, grid_spec=pltpu.PrefetchScalarGridSpec(num_sc...  14.7 us
    all_to_all x1, blocking collectives, all_to_all(): return lax.all_to_all(block, axis, 0, 0, tiled=True)  12.4 us
    ppermute x2, starting transfers between devices, from_behind(): return lax.ppermute(block, axis, route)  5.4 us
    ppermute x2, waiting for transfers between devices, from_behind(): return lax.ppermute(block, axis, route)  4.45 us
  transfers between devices with their start and end apart: 18, of which 9 were waited for; matrix products, arithmetic and copies ran while one was open for 3% of the time, Pallas kernels for 12%

profile of v3, /device:TPU:16, one launch (start us, length us, event | category | flops | bytes accessed | tf_op | source)
XLA Modules:
  0.0 147.1 jit_solution(12419821960951328132)
XLA Ops:
  0.0 4.8 %collective-permute-start.1 = (bf16[768,512]{1,0:T(8,128)(2,1)}, bf16[768,512]{1,0:T(8,128)(2,1)S(1)}, u32[]{:S(2)}, u32[]{:S(2)}) collective-permute-start(bf16[768,512]{1,0:T(8,128)(2,1)} %bitcast.39), channel_id=1, source_target_pairs={{0,24},{8,0},{16,8},{24,16},{1,25},{9,1},{17,9},{25,17},{2,26},{10... | collective-permute-start | bytes 2359304 | tf_op jit(solution)/shard_map/ppermute | solution.py:26
  6.8 10.9 %collective-permute-start.5 = (bf16[32,1536]{1,0:T(8,128)(2,1)S(1)}, bf16[32,1536]{1,0:T(8,128)(2,1)S(1)}, u32[]{:S(2)}, u32[]{:S(2)}) collective-permute-start(bf16[32,1536]{1,0:T(8,128)(2,1)S(1)} %dynamic-slice_bitcast_fusion), channel_id=1, source_target_pairs={{0,4},{1,5},{2,6},{3,7},{4,0},{5,1},{6,2},{7,3},{8,12},{9,13},{10,... | collective-permute-start | bytes 294920 | tf_op jit(solution)/shard_map/ppermute | solution.py:36
  19.2 7.6 %all-to-all-start = ((bf16[32,16,256]{2,1,0:T(8,128)(2,1)}), bf16[32,16,256]{2,1,0:T(8,128)(2,1)S(1)}, u32[]{:S(2)}, u32[]{:S(2)}) async-start(bf16[32,16,256]{2,1,0:T(8,128)(2,1)} %bitcast.6), calls=%async_computation | async-start | bytes 524288 | tf_op jit(solution)/shard_map/all_to_all | solution.py:358
  26.9 4.6 %collective-permute-start.6 = (bf16[64,1536]{1,0:T(8,128)(2,1)S(1)}, bf16[64,1536]{1,0:T(8,128)(2,1)}, u32[]{:S(2)}, u32[]{:S(2)}) collective-permute-start(bf16[64,1536]{1,0:T(8,128)(2,1)S(1)} %pad_maximum_fusion.1), channel_id=1, source_target_pairs={{0,2},{1,3},{2,0},{3,1},{4,6},{5,7},{6,4},{7,5},{8,10},{9,11},{10,... | collective-permute-start | bytes 589832 | tf_op jit(solution)/shard_map/ppermute | solution.py:36
  32.2 4.6 %collective-permute-start.3 = (bf16[384,512]{1,0:T(8,128)(2,1)}, bf16[384,512]{1,0:T(8,128)(2,1)}, u32[]{:S(2)}, u32[]{:S(2)}) collective-permute-start(bf16[384,512]{1,0:T(8,128)(2,1)} %slice.40), channel_id=1, source_target_pairs={{0,24},{8,0},{16,8},{24,16},{1,25},{9,1},{17,9},{25,17},{2,26},{10... | collective-permute-start | bytes 1179656 | tf_op jit(solution)/shard_map/ppermute | solution.py:26
  39.6 4.9 %all-to-all-done = bf16[32,16,256]{2,1,0:T(8,128)(2,1)S(1)} async-done(((bf16[32,16,256]{2,1,0:T(8,128)(2,1)}), bf16[32,16,256]{2,1,0:T(8,128)(2,1)S(1)}, u32[]{:S(2)}, u32[]{:S(2)}) %all-to-all-start) | async-done | bytes 262176 | tf_op jit(solution)/shard_map/all_to_all | solution.py:358
  47.4 1.9 %collective-permute-start.7 = (bf16[128,1536]{1,0:T(8,128)(2,1)S(1)}, bf16[128,1536]{1,0:T(8,128)(2,1)}, u32[]{:S(2)}, u32[]{:S(2)}) collective-permute-start(bf16[128,1536]{1,0:T(8,128)(2,1)S(1)} %pad_maximum_fusion.first_ref), channel_id=1, source_target_pairs={{0,1},{1,0},{2,3},{3,2},{4,5},{5,4},{6,7},{7,6},{8,9},{9,8},{10,11... | collective-permute-start | bytes 1179656 | tf_op jit(solution)/shard_map/ppermute | solution.py:36
  50.1 14.7 %attend.1 = bf16[8,136,256]{2,1,0:T(8,128)(2,1)} custom-call(s32[2]{0:T(128)S(1)} %pad_add_fusion.spot_ref, bf16[512,256]{1,0:T(8,128)(2,1)S(1)} %bitcast.38, bf16[512,256]{1,0:T(8,128)(2,1)S(1)} %collective-permute-done.other_ref, bf16[512,2048]{1,0:T(8,128)(2,1)} %value_ref.1, bf16[512,2048]{1,0:T(8,128)(2,1)} %value_ref.1, bf16[768,512]{1,0:T(8,128)(2,1)S(1)} %bitcast.41, ...), custom_call_target="tpu_custom_call" | custom-call | tf_op jit(solution)/shard_map/attend/pallas_call | solution.py:137
  64.8 4.9 %all-to-all-start.1 = ((bf16[8,136,256]{2,1,0:T(8,128)(2,1)}), bf16[8,136,256]{2,1,0:T(8,128)(2,1)S(1)}, u32[]{:S(2)}, u32[]{:S(2)}) async-start(bf16[8,136,256]{2,1,0:T(8,128)(2,1)} %attend.1), calls=%async_computation.1 | async-start | bytes 1114112 | tf_op jit(solution)/shard_map/all_to_all | solution.py:358
  70.8 1.9 %collective-permute-start.8 = (bf16[256,1536]{1,0:T(8,128)(2,1)S(1)}, bf16[256,1536]{1,0:T(8,128)(2,1)S(1)}, u32[]{:S(2)}, u32[]{:S(2)}) collective-permute-start(bf16[256,1536]{1,0:T(8,128)(2,1)S(1)} %order.1.mine_ref), channel_id=1, source_target_pairs={{0,32},{32,0},{1,33},{33,1},{2,34},{34,2},{3,35},{35,3},{4,36},{36... | collective-permute-start | bytes 2359304 | tf_op jit(solution)/shard_map/ppermute | solution.py:40
  72.7 14.2 %all-to-all-done.1.part_ref = bf16[8,136,256]{2,1,0:T(8,128)(2,1)S(1)} async-done(((bf16[8,136,256]{2,1,0:T(8,128)(2,1)}), bf16[8,136,256]{2,1,0:T(8,128)(2,1)S(1)}, u32[]{:S(2)}, u32[]{:S(2)}) %all-to-all-start.1) | async-done | bytes 557088 | tf_op jit(solution)/shard_map/all_to_all | solution.py:358
  88.2 3.4 %all-to-all-start.2 = ((bf16[4,128,256]{2,1,0:T(8,128)(2,1)}), bf16[4,128,256]{2,1,0:T(8,128)(2,1)S(1)}, u32[]{:S(2)}, u32[]{:S(2)}) async-start(bf16[4,128,256]{2,1,0:T(8,128)(2,1)} %combine.1), calls=%async_computation.2 | async-start | bytes 524288 | tf_op jit(solution)/shard_map/all_to_all | solution.py:358
  91.6 6.6 %all-to-all-done.2.rows_ref = bf16[4,128,256]{2,1,0:T(8,128)(2,1)S(1)} async-done(((bf16[4,128,256]{2,1,0:T(8,128)(2,1)}), bf16[4,128,256]{2,1,0:T(8,128)(2,1)S(1)}, u32[]{:S(2)}, u32[]{:S(2)}) %all-to-all-start.2) | async-done | bytes 262176 | tf_op jit(solution)/shard_map/all_to_all | solution.py:358
  99.1 3.5 %collective-permute-start.10 = (f32[136,256]{1,0:T(8,128)S(1)}, f32[136,256]{1,0:T(8,128)S(1)}, u32[]{:S(2)}, u32[]{:S(2)}) collective-permute-start(f32[136,256]{1,0:T(8,128)S(1)} %get-tuple-element.10), channel_id=1, source_target_pairs={{0,64},{32,96},{64,128},{96,160},{128,192},{160,224},{192,256},{22... | collective-permute-start | bytes 417800 | tf_op jit(solution)/shard_map/ppermute | solution.py:32
  102.6 1.9 %collective-permute-start.9 = (f32[136,256]{1,0:T(8,128)S(1)}, f32[136,256]{1,0:T(8,128)S(1)}, u32[]{:S(2)}, u32[]{:S(2)}) collective-permute-start(f32[136,256]{1,0:T(8,128)S(1)} %get-tuple-element.9), channel_id=1, source_target_pairs={{0,32},{32,64},{64,96},{96,128},{128,160},{160,192},{192,224},{224... | collective-permute-start | bytes 417800 | tf_op jit(solution)/shard_map/ppermute | solution.py:32
  106.0 2.9 %collective-permute-done.9.refs_1_ = f32[136,256]{1,0:T(8,128)S(1)} collective-permute-done((f32[136,256]{1,0:T(8,128)S(1)}, f32[136,256]{1,0:T(8,128)S(1)}, u32[]{:S(2)}, u32[]{:S(2)}) %collective-permute-start.9) | collective-permute-done | bytes 139296 | tf_op jit(solution)/shard_map/ppermute | solution.py:32
  110.0 3.5 %all-to-all-start.3 = ((bf16[8,128,256]{2,1,0:T(8,128)(2,1)}), bf16[8,128,256]{2,1,0:T(8,128)(2,1)S(1)}, u32[]{:S(2)}, u32[]{:S(2)}) async-start(bf16[8,128,256]{2,1,0:T(8,128)(2,1)} %finish.1), calls=%async_computation.3 | async-start | bytes 1048576 | tf_op jit(solution)/shard_map/all_to_all | solution.py:358
  113.6 2.5 %collective-permute-start.11 = (bf16[128,256]{1,0:T(8,128)(2,1)S(1)}, bf16[128,256]{1,0:T(8,128)(2,1)S(1)}, u32[]{:S(2)}, u32[]{:S(2)}) collective-permute-start(bf16[128,256]{1,0:T(8,128)(2,1)S(1)} %get-tuple-element.16), channel_id=1, source_target_pairs={{0,8},{8,16},{16,24},{24,0},{1,9},{9,17},{17,25},{25,1},{2,10},{10... | collective-permute-start | bytes 196616 | tf_op jit(solution)/shard_map/ppermute | solution.py:26
  116.1 4.0 %collective-permute-start.12 = (bf16[128,256]{1,0:T(8,128)(2,1)S(1)}, bf16[128,256]{1,0:T(8,128)(2,1)S(1)}, u32[]{:S(2)}, u32[]{:S(2)}) collective-permute-start(bf16[128,256]{1,0:T(8,128)(2,1)S(1)} %get-tuple-element.18), channel_id=1, source_target_pairs={{0,16},{8,24},{16,0},{24,8},{1,17},{9,25},{17,1},{25,9},{2,18},{10... | collective-permute-start | bytes 196616 | tf_op jit(solution)/shard_map/ppermute | solution.py:26
  120.0 2.5 %collective-permute-start.13 = (bf16[128,256]{1,0:T(8,128)(2,1)S(1)}, bf16[128,256]{1,0:T(8,128)(2,1)S(1)}, u32[]{:S(2)}, u32[]{:S(2)}) collective-permute-start(bf16[128,256]{1,0:T(8,128)(2,1)S(1)} %get-tuple-element.15), channel_id=1, source_target_pairs={{0,24},{8,0},{16,8},{24,16},{1,25},{9,1},{17,9},{25,17},{2,26},{10... | collective-permute-start | bytes 196616 | tf_op jit(solution)/shard_map/ppermute | solution.py:26
  123.7 2.5 %collective-permute-done.13.refs_3_ = bf16[128,256]{1,0:T(8,128)(2,1)S(1)} collective-permute-done((bf16[128,256]{1,0:T(8,128)(2,1)S(1)}, bf16[128,256]{1,0:T(8,128)(2,1)S(1)}, u32[]{:S(2)}, u32[]{:S(2)}) %collective-permute-start.13) | collective-permute-done | bytes 65568 | tf_op jit(solution)/shard_map/ppermute | solution.py:26
  126.2 5.6 %all-to-all-done.3 = bf16[8,128,256]{2,1,0:T(8,128)(2,1)S(1)} async-done(((bf16[8,128,256]{2,1,0:T(8,128)(2,1)}), bf16[8,128,256]{2,1,0:T(8,128)(2,1)S(1)}, u32[]{:S(2)}, u32[]{:S(2)}) %all-to-all-start.3) | async-done | bytes 524320 | tf_op jit(solution)/shard_map/all_to_all | solution.py:358
  131.8 2.0 %decode.1 = f32[4,128,256]{2,1,0:T(8,128)S(1)} custom-call(s32[1]{0:T(128)} %bitcast.place_ref, bf16[1024,256]{1,0:T(8,128)(2,1)S(1)} %bitcast.36, bf16[128,256]{1,0:T(8,128)(2,1)S(1)} %get-tuple-element.17.refs_0_, bf16[128,256]{1,0:T(8,128)(2,1)S(1)} %collective-permute-done.11.refs_1_, bf16[128,256]{1,0:T(8,128)(2,1)S(1)} %collective-permute-done.12.refs_2_, ...), custom_call_target="tpu_custom_call" | custom-call | tf_op jit(solution)/shard_map/decode/pallas_call | solution.py:336
  133.8 12.4 %all_to_all.25 = f32[4,128,256]{2,1,0:T(8,128)S(1)} all-to-all(f32[4,128,256]{2,1,0:T(8,128)S(1)} %decode.1), channel_id=1, replica_groups=mesh['y'=8,'core'=2,'x'=4,'z'=8] {'x'}, dimensions={0} | all-to-all | bytes 1048576 | tf_op jit(solution)/shard_map/all_to_all | solution.py:358
  (39 shorter events, 18.3 us)
Async XLA Ops:
  0.0 6.7 %copy-start = (bf16[3072,32]{0,1:T(8,128)(2,1)S(1)}, bf16[3072,32]{0,1:T(8,128)(2,1)}, u32[]{:S(2)}) copy-start(bf16[3072,32]{0,1:T(8,128)(2,1)} %param.10) | copy-start | bytes 589828
  0.0 50.1 %copy-start.1 = (bf16[1,768,512]{2,1,0:T(8,128)(2,1)S(1)}, bf16[1,768,512]{2,1,0:T(8,128)(2,1)}, u32[]{:S(2)}) copy-start(bf16[1,768,512]{2,1,0:T(8,128)(2,1)} %param.6) | copy-start | bytes 2359300
  0.0 31.5 %collective-permute-start.1 = (bf16[768,512]{1,0:T(8,128)(2,1)}, bf16[768,512]{1,0:T(8,128)(2,1)S(1)}, u32[]{:S(2)}, u32[]{:S(2)}) collective-permute-start(bf16[768,512]{1,0:T(8,128)(2,1)} %bitcast.39), channel_id=1, source_target_pairs={{0,24},{8,0},{16,8},{24,16},{1,25},{9,1},{17,9},{25,17},{2,26},{10... | collective-permute-start | bytes 2359304 | tf_op jit(solution)/shard_map/ppermute | solution.py:26
  4.8 32.1 %collective-permute-start.2 = (bf16[768,512]{1,0:T(8,128)(2,1)}, bf16[768,512]{1,0:T(8,128)(2,1)S(1)}, u32[]{:S(2)}, u32[]{:S(2)}) collective-permute-start(bf16[768,512]{1,0:T(8,128)(2,1)} %bitcast.40), channel_id=1, source_target_pairs={{0,8},{8,16},{16,24},{24,0},{1,9},{9,17},{17,25},{25,1},{2,10},{10... | collective-permute-start | bytes 2359304 | tf_op jit(solution)/shard_map/ppermute | solution.py:26
  6.8 20.1 %collective-permute-start.5 = (bf16[32,1536]{1,0:T(8,128)(2,1)S(1)}, bf16[32,1536]{1,0:T(8,128)(2,1)S(1)}, u32[]{:S(2)}, u32[]{:S(2)}) collective-permute-start(bf16[32,1536]{1,0:T(8,128)(2,1)S(1)} %dynamic-slice_bitcast_fusion), channel_id=1, source_target_pairs={{0,4},{1,5},{2,6},{3,7},{4,0},{5,1},{6,2},{7,3},{8,12},{9,13},{10,... | collective-permute-start | bytes 294920 | tf_op jit(solution)/shard_map/ppermute | solution.py:36
  19.2 25.3 %all-to-all-start = ((bf16[32,16,256]{2,1,0:T(8,128)(2,1)}), bf16[32,16,256]{2,1,0:T(8,128)(2,1)S(1)}, u32[]{:S(2)}, u32[]{:S(2)}) async-start(bf16[32,16,256]{2,1,0:T(8,128)(2,1)} %bitcast.6), calls=%async_computation | async-start | bytes 524288 | tf_op jit(solution)/shard_map/all_to_all | solution.py:358
  26.9 19.6 %collective-permute-start.6 = (bf16[64,1536]{1,0:T(8,128)(2,1)S(1)}, bf16[64,1536]{1,0:T(8,128)(2,1)}, u32[]{:S(2)}, u32[]{:S(2)}) collective-permute-start(bf16[64,1536]{1,0:T(8,128)(2,1)S(1)} %pad_maximum_fusion.1), channel_id=1, source_target_pairs={{0,2},{1,3},{2,0},{3,1},{4,6},{5,7},{6,4},{7,5},{8,10},{9,11},{10,... | collective-permute-start | bytes 589832 | tf_op jit(solution)/shard_map/ppermute | solution.py:36
  32.2 17.2 %collective-permute-start.3 = (bf16[384,512]{1,0:T(8,128)(2,1)}, bf16[384,512]{1,0:T(8,128)(2,1)}, u32[]{:S(2)}, u32[]{:S(2)}) collective-permute-start(bf16[384,512]{1,0:T(8,128)(2,1)} %slice.40), channel_id=1, source_target_pairs={{0,24},{8,0},{16,8},{24,16},{1,25},{9,1},{17,9},{25,17},{2,26},{10... | collective-permute-start | bytes 1179656 | tf_op jit(solution)/shard_map/ppermute | solution.py:26
  37.7 12.4 %collective-permute-start.4 = (bf16[384,512]{1,0:T(8,128)(2,1)}, bf16[384,512]{1,0:T(8,128)(2,1)}, u32[]{:S(2)}, u32[]{:S(2)}) collective-permute-start(bf16[384,512]{1,0:T(8,128)(2,1)} %slice.41), channel_id=1, source_target_pairs={{0,8},{8,16},{16,24},{24,0},{1,9},{9,17},{17,25},{25,1},{2,10},{10... | collective-permute-start | bytes 1179656 | tf_op jit(solution)/shard_map/ppermute | solution.py:26
  44.5 4.9 %collective-permute-start = (bf16[512,256]{1,0:T(8,128)(2,1)S(1)}, bf16[512,256]{1,0:T(8,128)(2,1)S(1)}, u32[]{:S(2)}, u32[]{:S(2)}) collective-permute-start(bf16[512,256]{1,0:T(8,128)(2,1)S(1)} %bitcast.37), channel_id=1, source_target_pairs={{0,32},{32,0},{1,33},{33,1},{2,34},{34,2},{3,35},{35,3},{4,36},{36... | collective-permute-start | bytes 786440 | tf_op jit(solution)/shard_map/ppermute | solution.py:40
  47.4 22.3 %collective-permute-start.7 = (bf16[128,1536]{1,0:T(8,128)(2,1)S(1)}, bf16[128,1536]{1,0:T(8,128)(2,1)}, u32[]{:S(2)}, u32[]{:S(2)}) collective-permute-start(bf16[128,1536]{1,0:T(8,128)(2,1)S(1)} %pad_maximum_fusion.first_ref), channel_id=1, source_target_pairs={{0,1},{1,0},{2,3},{3,2},{4,5},{5,4},{6,7},{7,6},{8,9},{9,8},{10,11... | collective-permute-start | bytes 1179656 | tf_op jit(solution)/shard_map/ppermute | solution.py:36
  64.8 33.5 %copy-start.2 = (f32[3072]{0:T(1024)S(1)}, f32[3072]{0:T(1024)}, u32[]{:S(2)}) copy-start(f32[3072]{0:T(1024)} %param.9) | copy-start | bytes 36868
  64.8 22.1 %all-to-all-start.1 = ((bf16[8,136,256]{2,1,0:T(8,128)(2,1)}), bf16[8,136,256]{2,1,0:T(8,128)(2,1)S(1)}, u32[]{:S(2)}, u32[]{:S(2)}) async-start(bf16[8,136,256]{2,1,0:T(8,128)(2,1)} %attend.1), calls=%async_computation.1 | async-start | bytes 1114112 | tf_op jit(solution)/shard_map/all_to_all | solution.py:358
  70.8 20.9 %collective-permute-start.8 = (bf16[256,1536]{1,0:T(8,128)(2,1)S(1)}, bf16[256,1536]{1,0:T(8,128)(2,1)S(1)}, u32[]{:S(2)}, u32[]{:S(2)}) collective-permute-start(bf16[256,1536]{1,0:T(8,128)(2,1)S(1)} %order.1.mine_ref), channel_id=1, source_target_pairs={{0,32},{32,0},{1,33},{33,1},{2,34},{34,2},{3,35},{35,3},{4,36},{36... | collective-permute-start | bytes 2359304 | tf_op jit(solution)/shard_map/ppermute | solution.py:40
  88.2 10.1 %all-to-all-start.2 = ((bf16[4,128,256]{2,1,0:T(8,128)(2,1)}), bf16[4,128,256]{2,1,0:T(8,128)(2,1)S(1)}, u32[]{:S(2)}, u32[]{:S(2)}) async-start(bf16[4,128,256]{2,1,0:T(8,128)(2,1)} %combine.1), calls=%async_computation.2 | async-start | bytes 524288 | tf_op jit(solution)/shard_map/all_to_all | solution.py:358
  91.6 21.9 %copy-start.3 = (bf16[1,128,1024]{2,1,0:T(8,128)(2,1)S(1)}, bf16[1,128,1024]{2,1,0:T(8,128)(2,1)}, u32[]{:S(2)}) copy-start(bf16[1,128,1024]{2,1,0:T(8,128)(2,1)} %param.11) | copy-start | bytes 786436
  99.1 6.9 %collective-permute-start.10 = (f32[136,256]{1,0:T(8,128)S(1)}, f32[136,256]{1,0:T(8,128)S(1)}, u32[]{:S(2)}, u32[]{:S(2)}) collective-permute-start(f32[136,256]{1,0:T(8,128)S(1)} %get-tuple-element.10), channel_id=1, source_target_pairs={{0,64},{32,96},{64,128},{96,160},{128,192},{160,224},{192,256},{22... | collective-permute-start | bytes 417800 | tf_op jit(solution)/shard_map/ppermute | solution.py:32
  102.6 6.4 %collective-permute-start.9 = (f32[136,256]{1,0:T(8,128)S(1)}, f32[136,256]{1,0:T(8,128)S(1)}, u32[]{:S(2)}, u32[]{:S(2)}) collective-permute-start(f32[136,256]{1,0:T(8,128)S(1)} %get-tuple-element.9), channel_id=1, source_target_pairs={{0,32},{32,64},{64,96},{96,128},{128,160},{160,192},{192,224},{224... | collective-permute-start | bytes 417800 | tf_op jit(solution)/shard_map/ppermute | solution.py:32
  110.0 21.8 %all-to-all-start.3 = ((bf16[8,128,256]{2,1,0:T(8,128)(2,1)}), bf16[8,128,256]{2,1,0:T(8,128)(2,1)S(1)}, u32[]{:S(2)}, u32[]{:S(2)}) async-start(bf16[8,128,256]{2,1,0:T(8,128)(2,1)} %finish.1), calls=%async_computation.3 | async-start | bytes 1048576 | tf_op jit(solution)/shard_map/all_to_all | solution.py:358
  113.6 9.0 %collective-permute-start.11 = (bf16[128,256]{1,0:T(8,128)(2,1)S(1)}, bf16[128,256]{1,0:T(8,128)(2,1)S(1)}, u32[]{:S(2)}, u32[]{:S(2)}) collective-permute-start(bf16[128,256]{1,0:T(8,128)(2,1)S(1)} %get-tuple-element.16), channel_id=1, source_target_pairs={{0,8},{8,16},{16,24},{24,0},{1,9},{9,17},{17,25},{25,1},{2,10},{10... | collective-permute-start | bytes 196616 | tf_op jit(solution)/shard_map/ppermute | solution.py:26
  116.1 7.7 %collective-permute-start.12 = (bf16[128,256]{1,0:T(8,128)(2,1)S(1)}, bf16[128,256]{1,0:T(8,128)(2,1)S(1)}, u32[]{:S(2)}, u32[]{:S(2)}) collective-permute-start(bf16[128,256]{1,0:T(8,128)(2,1)S(1)} %get-tuple-element.18), channel_id=1, source_target_pairs={{0,16},{8,24},{16,0},{24,8},{1,17},{9,25},{17,1},{25,9},{2,18},{10... | collective-permute-start | bytes 196616 | tf_op jit(solution)/shard_map/ppermute | solution.py:26
  120.0 6.2 %collective-permute-start.13 = (bf16[128,256]{1,0:T(8,128)(2,1)S(1)}, bf16[128,256]{1,0:T(8,128)(2,1)S(1)}, u32[]{:S(2)}, u32[]{:S(2)}) collective-permute-start(bf16[128,256]{1,0:T(8,128)(2,1)S(1)} %get-tuple-element.15), channel_id=1, source_target_pairs={{0,24},{8,0},{16,8},{24,16},{1,25},{9,1},{17,9},{25,17},{2,26},{10... | collective-permute-start | bytes 196616 | tf_op jit(solution)/shard_map/ppermute | solution.py:26

commit v4 on v3

--- a/solution.py
+++ b/solution.py
@@ -14,6 +14,7 @@
 EXP2_SCALE = math.log2(math.e) / math.sqrt(HEAD_DIM)
 FRAME = ("y", "core")
 EXTRA = 8
+CHUNK = 768
 TAIL = 8
 XORS = (4, 2, 1)
 MASKS = (0, 4, 2, 6, 1, 5, 3, 7)
@@ -30,6 +31,12 @@
     devices = range(lax.axis_size(axis))
     route = [(i - distance, i) for i in devices if i - distance in devices]
     return lax.ppermute(block, axis, route)
+
+
+def skew(block):
+    ys, zs = lax.axis_size("y"), lax.axis_size("z")
+    route = [(y * zs + (z ^ y), y * zs + z) for y in range(ys) for z in range(zs)]
+    return lax.ppermute(block, ("y", "z"), route)
 
 
 def across(block, axis, mask):
@@ -102,16 +109,29 @@
     tile = q_ref.shape[0]
     blocks = out_ref.shape[0]
     rows = tile // blocks
-    for h in range(width // HEAD_DIM):
+    heads = range(width // HEAD_DIM)
+    states = [None for _ in heads]
+    count = kv_ref.shape[0]
+    chunk = CHUNK if count % CHUNK == 0 else count
+    for low in range(0, count, chunk):
+        span = slice(low, low + chunk)
+        for h in heads:
+            scores = dot_nt(q_ref[:, head_cols(h)], kv_ref[span, head_cols(h)])
+            peak = jnp.max(scores, axis=1, keepdims=True)
+            if states[h] is not None:
+                peak = jnp.maximum(peak, states[h][0])
+            weights = jnp.exp2((scores - peak) * EXP2_SCALE)
+            den = jnp.sum(weights, axis=1, keepdims=True)
+            values = kv_ref[span, width + h * HEAD_DIM : width + (h + 1) * HEAD_DIM]
+            num = jnp.dot(weights.astype(jnp.bfloat16), values, preferred_element_type=jnp.float32)
+            if states[h] is not None:
+                rescale = jnp.exp2((states[h][0] - peak) * EXP2_SCALE)
+                den = den + rescale * states[h][1]
+                num = num + rescale * states[h][2]
+            states[h] = (peak, den, num)
+    for h in heads:
         cols = head_cols(h)
-        scores = dot_nt(q_ref[:, cols], kv_ref[:, cols])
-        peak = jnp.max(scores, axis=1, keepdims=True)
-        weights = jnp.exp2((scores - peak) * EXP2_SCALE)
-        den = jnp.sum(weights, axis=1, keepdims=True)
-        value_cols = slice(width + h * HEAD_DIM, width + (h + 1) * HEAD_DIM)
-        num = jnp.dot(
-            weights.astype(jnp.bfloat16), kv_ref[:, value_cols], preferred_element_type=jnp.float32
-        )
+        peak, den, num = states[h]
         first = peak.astype(jnp.bfloat16).astype(jnp.float32)
         second = (peak - first).astype(jnp.bfloat16).astype(jnp.float32)
         packed = lanes([first, second, peak - first - second, den], (tile, HEAD_DIM)).T
@@ -375,9 +395,10 @@
     mix_t = mix_weight.T
     mix_half = mix_t.shape[1] // 2
     held = lax.dynamic_slice_in_dim(mix_t, core_index * mix_half, mix_half, axis=1)
+    held = skew(held)
     for mask in XORS[:-1]:
-        held = join(held, across(held, "z", mask))
-    brought = across(held, "z", XORS[-1])
+        held = join(held, across(held, "y", mask))
+    brought = across(held, "y", XORS[-1])
 
     rows = latent_queries.shape[0] // 2
     asked = lax.dynamic_slice_in_dim(latent_queries, core_index * rows, rows, axis=0)
@@ -401,7 +422,7 @@
         (mine, above, below, far_low, far_high),
         groups,
         members,
-        latents // 4,
+        latents // 2,
     )
     parts = all_to_all(parts, "z")
 
@@ -410,7 +431,7 @@
         to = (place + k) % groups
         sent = lax.dynamic_slice_in_dim(output_queries[0], to * width, width, axis=1)
         queries.append(shift(sent, "x", k) if k else sent)
-    mix_mine = order(scalar(lax.axis_index("z")), held, brought)
+    mix_mine = order(scalar(lax.axis_index("z") ^ lax.axis_index("y")), held, brought)
     mix_other = partner(mix_mine)
 
     window = all_to_all(combine(parts, groups), "x")

time: 148 us -> 157 us (1.061)
  the two profiles are of different devices: /device:TPU:16 before, /device:TPU:48 now
where the time goes in v4:
time: 157 us; the launch traced here: 156 us
  starting transfers between devices  76 us (48%)
  waiting for transfers between devices  42 us (27%)
  Pallas kernels  19.7 us (13%)
  blocking collectives  12.4 us (8%)
  local copies, waits for them, and re-layouts  4.11 us (3%)
    all_to_all x4, waiting for transfers between devices, all_to_all(): return lax.all_to_all(block, axis, 0, 0, tiled=True)  24.1 us
    ppermute x7, starting transfers between devices, shift(): lax.ppermute(block, axis, [(i, (i + distance) % size) for i in range(size)])  22.5 us
    all_to_all x4, starting transfers between devices, all_to_all(): return lax.all_to_all(block, axis, 0, 0, tiled=True)  20.3 us
    pallas_call x1, Pallas kernels, attend(): pl.pallas_call(attend_body, grid_spec=pltpu.PrefetchScalarGridSpec(num_sc...  13.5 us
    ppermute x3, starting transfers between devices, across(): lax.ppermute(block, axis, [(i, i ^ mask) for i in range(lax.axis_size(axi...  13 us
    all_to_all x1, blocking collectives, all_to_all(): return lax.all_to_all(block, axis, 0, 0, tiled=True)  12.4 us
    ppermute x1, starting transfers between devices, skew(): return lax.ppermute(block, ('y', 'z'), route)  10.9 us
    ppermute x7, waiting for transfers between devices, shift(): lax.ppermute(block, axis, [(i, (i + distance) % size) for i in range(size)])  7.83 us
  transfers between devices with their start and end apart: 19, of which 9 were waited for; matrix products, arithmetic and copies ran while one was open for 3% of the time, Pallas kernels for 10%

profile of v4, /device:TPU:48, one launch (start us, length us, event | category | flops | bytes accessed | tf_op | source)
XLA Modules:
  0.0 155.5 jit_solution(12132677707171413433)
XLA Ops:
  0.0 4.8 %collective-permute-start.1 = (bf16[768,512]{1,0:T(8,128)(2,1)}, bf16[768,512]{1,0:T(8,128)(2,1)S(1)}, u32[]{:S(2)}, u32[]{:S(2)}) collective-permute-start(bf16[768,512]{1,0:T(8,128)(2,1)} %bitcast.39), channel_id=1, source_target_pairs={{0,24},{8,0},{16,8},{24,16},{1,25},{9,1},{17,9},{25,17},{2,26},{10... | collective-permute-start | bytes 2359304 | tf_op jit(solution)/shard_map/ppermute | solution.py:27
  6.8 10.9 %collective-permute-start.5 = (bf16[32,1536]{1,0:T(8,128)(2,1)S(1)}, bf16[32,1536]{1,0:T(8,128)(2,1)S(1)}, u32[]{:S(2)}, u32[]{:S(2)}) collective-permute-start(bf16[32,1536]{1,0:T(8,128)(2,1)S(1)} %dynamic-slice_bitcast_fusion), channel_id=1, source_target_pairs={{0,0},{1,1},{2,2},{3,3},{4,4},{5,5},{6,6},{7,7},{65,64},{64,65},{6... | collective-permute-start | bytes 294920 | tf_op jit(solution)/shard_map/ppermute | solution.py:39
  19.2 5.8 %all-to-all-start = ((bf16[32,16,256]{2,1,0:T(8,128)(2,1)}), bf16[32,16,256]{2,1,0:T(8,128)(2,1)S(1)}, u32[]{:S(2)}, u32[]{:S(2)}) async-start(bf16[32,16,256]{2,1,0:T(8,128)(2,1)} %bitcast.6), calls=%async_computation | async-start | bytes 524288 | tf_op jit(solution)/shard_map/all_to_all | solution.py:378
  25.0 4.7 %collective-permute-start.6 = (bf16[32,1536]{1,0:T(8,128)(2,1)S(1)}, bf16[32,1536]{1,0:T(8,128)(2,1)S(1)}, u32[]{:S(2)}, u32[]{:S(2)}) collective-permute-start(bf16[32,1536]{1,0:T(8,128)(2,1)S(1)} %collective-permute-done.5), channel_id=1, source_target_pairs={{0,256},{64,320},{128,384},{192,448},{256,0},{320,64},{384,128},{4... | collective-permute-start | bytes 294920 | tf_op jit(solution)/shard_map/ppermute | solution.py:43
  29.8 5.7 %collective-permute-done.6 = bf16[32,1536]{1,0:T(8,128)(2,1)S(1)} collective-permute-done((bf16[32,1536]{1,0:T(8,128)(2,1)S(1)}, bf16[32,1536]{1,0:T(8,128)(2,1)S(1)}, u32[]{:S(2)}, u32[]{:S(2)}) %collective-permute-start.6) | collective-permute-done | bytes 98336 | tf_op jit(solution)/shard_map/ppermute | solution.py:43
  35.5 5.8 %collective-permute-start.7 = (bf16[64,1536]{1,0:T(8,128)(2,1)S(1)}, bf16[64,1536]{1,0:T(8,128)(2,1)}, u32[]{:S(2)}, u32[]{:S(2)}) collective-permute-start(bf16[64,1536]{1,0:T(8,128)(2,1)S(1)} %pad_maximum_fusion), channel_id=1, source_target_pairs={{0,128},{64,192},{128,0},{192,64},{256,384},{320,448},{384,256},{4... | collective-permute-start | bytes 589832 | tf_op jit(solution)/shard_map/ppermute | solution.py:43
  42.1 4.9 %collective-permute-start.3 = (bf16[384,512]{1,0:T(8,128)(2,1)}, bf16[384,512]{1,0:T(8,128)(2,1)}, u32[]{:S(2)}, u32[]{:S(2)}) collective-permute-start(bf16[384,512]{1,0:T(8,128)(2,1)} %slice.40), channel_id=1, source_target_pairs={{0,24},{8,0},{16,8},{24,16},{1,25},{9,1},{17,9},{25,17},{2,26},{10... | collective-permute-start | bytes 1179656 | tf_op jit(solution)/shard_map/ppermute | solution.py:27
  52.7 2.4 %collective-permute-start.8 = (bf16[128,1536]{1,0:T(8,128)(2,1)S(1)}, bf16[128,1536]{1,0:T(8,128)(2,1)}, u32[]{:S(2)}, u32[]{:S(2)}) collective-permute-start(bf16[128,1536]{1,0:T(8,128)(2,1)S(1)} %constant_dynamic-update-slice_fusion.first_ref), channel_id=1, source_target_pairs={{0,64},{64,0},{128,192},{192,128},{256,320},{320,256},{384,448},{4... | collective-permute-start | bytes 1179656 | tf_op jit(solution)/shard_map/ppermute | solution.py:43
  55.2 4.2 %collective-permute-done.4.refs_4_ = bf16[384,512]{1,0:T(8,128)(2,1)} collective-permute-done((bf16[384,512]{1,0:T(8,128)(2,1)}, bf16[384,512]{1,0:T(8,128)(2,1)}, u32[]{:S(2)}, u32[]{:S(2)}) %collective-permute-start.4) | collective-permute-done | bytes 393248 | tf_op jit(solution)/shard_map/ppermute | solution.py:27
  59.4 13.5 %attend.1 = bf16[8,136,256]{2,1,0:T(8,128)(2,1)} custom-call(s32[2]{0:T(128)S(1)} %pad_add_fusion.spot_ref, bf16[512,256]{1,0:T(8,128)(2,1)S(1)} %bitcast.38, bf16[512,256]{1,0:T(8,128)(2,1)S(1)} %collective-permute-done.other_ref, bf16[512,2048]{1,0:T(8,128)(2,1)} %value_ref.1, bf16[512,2048]{1,0:T(8,128)(2,1)} %value_ref.1, bf16[768,512]{1,0:T(8,128)(2,1)S(1)} %bitcast.41, ...), custom_call_target="tpu_custom_call" | custom-call | tf_op jit(solution)/shard_map/attend/pallas_call | solution.py:157
  72.9 6.5 %all-to-all-start.1 = ((bf16[8,136,256]{2,1,0:T(8,128)(2,1)}), bf16[8,136,256]{2,1,0:T(8,128)(2,1)S(1)}, u32[]{:S(2)}, u32[]{:S(2)}) async-start(bf16[8,136,256]{2,1,0:T(8,128)(2,1)} %attend.1), calls=%async_computation.1 | async-start | bytes 1114112 | tf_op jit(solution)/shard_map/all_to_all | solution.py:378
  82.5 11.7 %all-to-all-done.1.part_ref = bf16[8,136,256]{2,1,0:T(8,128)(2,1)S(1)} async-done(((bf16[8,136,256]{2,1,0:T(8,128)(2,1)}), bf16[8,136,256]{2,1,0:T(8,128)(2,1)S(1)}, u32[]{:S(2)}, u32[]{:S(2)}) %all-to-all-start.1) | async-done | bytes 557088 | tf_op jit(solution)/shard_map/all_to_all | solution.py:378
  95.4 4.5 %all-to-all-start.2 = ((bf16[4,128,256]{2,1,0:T(8,128)(2,1)}), bf16[4,128,256]{2,1,0:T(8,128)(2,1)S(1)}, u32[]{:S(2)}, u32[]{:S(2)}) async-start(bf16[4,128,256]{2,1,0:T(8,128)(2,1)} %combine.1), calls=%async_computation.2 | async-start | bytes 524288 | tf_op jit(solution)/shard_map/all_to_all | solution.py:378
  99.9 6.8 %all-to-all-done.2.rows_ref = bf16[4,128,256]{2,1,0:T(8,128)(2,1)S(1)} async-done(((bf16[4,128,256]{2,1,0:T(8,128)(2,1)}), bf16[4,128,256]{2,1,0:T(8,128)(2,1)S(1)}, u32[]{:S(2)}, u32[]{:S(2)}) %all-to-all-start.2) | async-done | bytes 262176 | tf_op jit(solution)/shard_map/all_to_all | solution.py:378
  109.5 3.4 %collective-permute-start.11 = (f32[136,256]{1,0:T(8,128)S(1)}, f32[136,256]{1,0:T(8,128)S(1)}, u32[]{:S(2)}, u32[]{:S(2)}) collective-permute-start(f32[136,256]{1,0:T(8,128)S(1)} %get-tuple-element.10), channel_id=1, source_target_pairs={{0,64},{32,96},{64,128},{96,160},{128,192},{160,224},{192,256},{22... | collective-permute-start | bytes 417800 | tf_op jit(solution)/shard_map/ppermute | solution.py:33
  114.0 3.3 %collective-permute-done.11.refs_2_ = f32[136,256]{1,0:T(8,128)S(1)} collective-permute-done((f32[136,256]{1,0:T(8,128)S(1)}, f32[136,256]{1,0:T(8,128)S(1)}, u32[]{:S(2)}, u32[]{:S(2)}) %collective-permute-start.11) | collective-permute-done | bytes 139296 | tf_op jit(solution)/shard_map/ppermute | solution.py:33
  118.3 3.5 %all-to-all-start.3 = ((bf16[8,128,256]{2,1,0:T(8,128)(2,1)}), bf16[8,128,256]{2,1,0:T(8,128)(2,1)S(1)}, u32[]{:S(2)}, u32[]{:S(2)}) async-start(bf16[8,128,256]{2,1,0:T(8,128)(2,1)} %finish.1), calls=%async_computation.3 | async-start | bytes 1048576 | tf_op jit(solution)/shard_map/all_to_all | solution.py:378
  121.9 2.5 %collective-permute-start.12 = (bf16[128,256]{1,0:T(8,128)(2,1)S(1)}, bf16[128,256]{1,0:T(8,128)(2,1)S(1)}, u32[]{:S(2)}, u32[]{:S(2)}) collective-permute-start(bf16[128,256]{1,0:T(8,128)(2,1)S(1)} %get-tuple-element.16), channel_id=1, source_target_pairs={{0,8},{8,16},{16,24},{24,0},{1,9},{9,17},{17,25},{25,1},{2,10},{10... | collective-permute-start | bytes 196616 | tf_op jit(solution)/shard_map/ppermute | solution.py:27
  124.4 4.0 %collective-permute-start.13 = (bf16[128,256]{1,0:T(8,128)(2,1)S(1)}, bf16[128,256]{1,0:T(8,128)(2,1)S(1)}, u32[]{:S(2)}, u32[]{:S(2)}) collective-permute-start(bf16[128,256]{1,0:T(8,128)(2,1)S(1)} %get-tuple-element.18), channel_id=1, source_target_pairs={{0,16},{8,24},{16,0},{24,8},{1,17},{9,25},{17,1},{25,9},{2,18},{10... | collective-permute-start | bytes 196616 | tf_op jit(solution)/shard_map/ppermute | solution.py:27
  128.4 2.5 %collective-permute-start.14 = (bf16[128,256]{1,0:T(8,128)(2,1)S(1)}, bf16[128,256]{1,0:T(8,128)(2,1)S(1)}, u32[]{:S(2)}, u32[]{:S(2)}) collective-permute-start(bf16[128,256]{1,0:T(8,128)(2,1)S(1)} %get-tuple-element.15), channel_id=1, source_target_pairs={{0,24},{8,0},{16,8},{24,16},{1,25},{9,1},{17,9},{25,17},{2,26},{10... | collective-permute-start | bytes 196616 | tf_op jit(solution)/shard_map/ppermute | solution.py:27
  132.1 2.5 %collective-permute-done.14.refs_3_ = bf16[128,256]{1,0:T(8,128)(2,1)S(1)} collective-permute-done((bf16[128,256]{1,0:T(8,128)(2,1)S(1)}, bf16[128,256]{1,0:T(8,128)(2,1)S(1)}, u32[]{:S(2)}, u32[]{:S(2)}) %collective-permute-start.14) | collective-permute-done | bytes 65568 | tf_op jit(solution)/shard_map/ppermute | solution.py:27
  134.6 5.6 %all-to-all-done.3 = bf16[8,128,256]{2,1,0:T(8,128)(2,1)S(1)} async-done(((bf16[8,128,256]{2,1,0:T(8,128)(2,1)}), bf16[8,128,256]{2,1,0:T(8,128)(2,1)S(1)}, u32[]{:S(2)}, u32[]{:S(2)}) %all-to-all-start.3) | async-done | bytes 524320 | tf_op jit(solution)/shard_map/all_to_all | solution.py:378
  140.2 2.0 %decode.1 = f32[4,128,256]{2,1,0:T(8,128)S(1)} custom-call(s32[1]{0:T(128)} %bitcast.place_ref, bf16[1024,256]{1,0:T(8,128)(2,1)S(1)} %bitcast.36, bf16[128,256]{1,0:T(8,128)(2,1)S(1)} %get-tuple-element.17.refs_0_, bf16[128,256]{1,0:T(8,128)(2,1)S(1)} %collective-permute-done.12.refs_1_, bf16[128,256]{1,0:T(8,128)(2,1)S(1)} %collective-permute-done.13.refs_2_, ...), custom_call_target="tpu_custom_call" | custom-call | tf_op jit(solution)/shard_map/decode/pallas_call | solution.py:356
  142.2 12.4 %all_to_all.25 = f32[4,128,256]{2,1,0:T(8,128)S(1)} all-to-all(f32[4,128,256]{2,1,0:T(8,128)S(1)} %decode.1), channel_id=1, replica_groups=mesh['y'=8,'core'=2,'x'=4,'z'=8] {'x'}, dimensions={0} | all-to-all | bytes 1048576 | tf_op jit(solution)/shard_map/all_to_all | solution.py:378
  (43 shorter events, 21.0 us)
Async XLA Ops:
  0.0 6.7 %copy-start = (bf16[3072,32]{0,1:T(8,128)(2,1)S(1)}, bf16[3072,32]{0,1:T(8,128)(2,1)}, u32[]{:S(2)}) copy-start(bf16[3072,32]{0,1:T(8,128)(2,1)} %param.10) | copy-start | bytes 589828
  0.0 59.4 %copy-start.1 = (bf16[1,768,512]{2,1,0:T(8,128)(2,1)S(1)}, bf16[1,768,512]{2,1,0:T(8,128)(2,1)}, u32[]{:S(2)}) copy-start(bf16[1,768,512]{2,1,0:T(8,128)(2,1)} %param.6) | copy-start | bytes 2359300
  0.0 41.3 %collective-permute-start.1 = (bf16[768,512]{1,0:T(8,128)(2,1)}, bf16[768,512]{1,0:T(8,128)(2,1)S(1)}, u32[]{:S(2)}, u32[]{:S(2)}) collective-permute-start(bf16[768,512]{1,0:T(8,128)(2,1)} %bitcast.39), channel_id=1, source_target_pairs={{0,24},{8,0},{16,8},{24,16},{1,25},{9,1},{17,9},{25,17},{2,26},{10... | collective-permute-start | bytes 2359304 | tf_op jit(solution)/shard_map/ppermute | solution.py:27
  4.8 42.3 %collective-permute-start.2 = (bf16[768,512]{1,0:T(8,128)(2,1)}, bf16[768,512]{1,0:T(8,128)(2,1)S(1)}, u32[]{:S(2)}, u32[]{:S(2)}) collective-permute-start(bf16[768,512]{1,0:T(8,128)(2,1)} %bitcast.40), channel_id=1, source_target_pairs={{0,8},{8,16},{16,24},{24,0},{1,9},{9,17},{17,25},{25,1},{2,10},{10... | collective-permute-start | bytes 2359304 | tf_op jit(solution)/shard_map/ppermute | solution.py:27
  6.8 18.3 %collective-permute-start.5 = (bf16[32,1536]{1,0:T(8,128)(2,1)S(1)}, bf16[32,1536]{1,0:T(8,128)(2,1)S(1)}, u32[]{:S(2)}, u32[]{:S(2)}) collective-permute-start(bf16[32,1536]{1,0:T(8,128)(2,1)S(1)} %dynamic-slice_bitcast_fusion), channel_id=1, source_target_pairs={{0,0},{1,1},{2,2},{3,3},{4,4},{5,5},{6,6},{7,7},{65,64},{64,65},{6... | collective-permute-start | bytes 294920 | tf_op jit(solution)/shard_map/ppermute | solution.py:39
  19.2 30.6 %all-to-all-start = ((bf16[32,16,256]{2,1,0:T(8,128)(2,1)}), bf16[32,16,256]{2,1,0:T(8,128)(2,1)S(1)}, u32[]{:S(2)}, u32[]{:S(2)}) async-start(bf16[32,16,256]{2,1,0:T(8,128)(2,1)} %bitcast.6), calls=%async_computation | async-start | bytes 524288 | tf_op jit(solution)/shard_map/all_to_all | solution.py:378
  25.0 10.4 %collective-permute-start.6 = (bf16[32,1536]{1,0:T(8,128)(2,1)S(1)}, bf16[32,1536]{1,0:T(8,128)(2,1)S(1)}, u32[]{:S(2)}, u32[]{:S(2)}) collective-permute-start(bf16[32,1536]{1,0:T(8,128)(2,1)S(1)} %collective-permute-done.5), channel_id=1, source_target_pairs={{0,256},{64,320},{128,384},{192,448},{256,0},{320,64},{384,128},{4... | collective-permute-start | bytes 294920 | tf_op jit(solution)/shard_map/ppermute | solution.py:43
  35.5 16.3 %collective-permute-start.7 = (bf16[64,1536]{1,0:T(8,128)(2,1)S(1)}, bf16[64,1536]{1,0:T(8,128)(2,1)}, u32[]{:S(2)}, u32[]{:S(2)}) collective-permute-start(bf16[64,1536]{1,0:T(8,128)(2,1)S(1)} %pad_maximum_fusion), channel_id=1, source_target_pairs={{0,128},{64,192},{128,0},{192,64},{256,384},{320,448},{384,256},{4... | collective-permute-start | bytes 589832 | tf_op jit(solution)/shard_map/ppermute | solution.py:43
  42.1 13.1 %collective-permute-start.3 = (bf16[384,512]{1,0:T(8,128)(2,1)}, bf16[384,512]{1,0:T(8,128)(2,1)}, u32[]{:S(2)}, u32[]{:S(2)}) collective-permute-start(bf16[384,512]{1,0:T(8,128)(2,1)} %slice.40), channel_id=1, source_target_pairs={{0,24},{8,0},{16,8},{24,16},{1,25},{9,1},{17,9},{25,17},{2,26},{10... | collective-permute-start | bytes 1179656 | tf_op jit(solution)/shard_map/ppermute | solution.py:27
  47.9 11.5 %collective-permute-start.4 = (bf16[384,512]{1,0:T(8,128)(2,1)}, bf16[384,512]{1,0:T(8,128)(2,1)}, u32[]{:S(2)}, u32[]{:S(2)}) collective-permute-start(bf16[384,512]{1,0:T(8,128)(2,1)} %slice.41), channel_id=1, source_target_pairs={{0,8},{8,16},{16,24},{24,0},{1,9},{9,17},{17,25},{25,1},{2,10},{10... | collective-permute-start | bytes 1179656 | tf_op jit(solution)/shard_map/ppermute | solution.py:27
  49.8 5.4 %collective-permute-start = (bf16[512,256]{1,0:T(8,128)(2,1)S(1)}, bf16[512,256]{1,0:T(8,128)(2,1)S(1)}, u32[]{:S(2)}, u32[]{:S(2)}) collective-permute-start(bf16[512,256]{1,0:T(8,128)(2,1)S(1)} %bitcast.37), channel_id=1, source_target_pairs={{0,32},{32,0},{1,33},{33,1},{2,34},{34,2},{3,35},{35,3},{4,36},{36... | collective-permute-start | bytes 786440 | tf_op jit(solution)/shard_map/ppermute | solution.py:47
  52.7 26.8 %collective-permute-start.8 = (bf16[128,1536]{1,0:T(8,128)(2,1)S(1)}, bf16[128,1536]{1,0:T(8,128)(2,1)}, u32[]{:S(2)}, u32[]{:S(2)}) collective-permute-start(bf16[128,1536]{1,0:T(8,128)(2,1)S(1)} %constant_dynamic-update-slice_fusion.first_ref), channel_id=1, source_target_pairs={{0,64},{64,0},{128,192},{192,128},{256,320},{320,256},{384,448},{4... | collective-permute-start | bytes 1179656 | tf_op jit(solution)/shard_map/ppermute | solution.py:43
  72.9 33.8 %copy-start.2 = (f32[3072]{0:T(1024)S(1)}, f32[3072]{0:T(1024)}, u32[]{:S(2)}) copy-start(f32[3072]{0:T(1024)} %param.9) | copy-start | bytes 36868
  72.9 21.2 %all-to-all-start.1 = ((bf16[8,136,256]{2,1,0:T(8,128)(2,1)}), bf16[8,136,256]{2,1,0:T(8,128)(2,1)S(1)}, u32[]{:S(2)}, u32[]{:S(2)}) async-start(bf16[8,136,256]{2,1,0:T(8,128)(2,1)} %attend.1), calls=%async_computation.1 | async-start | bytes 1114112 | tf_op jit(solution)/shard_map/all_to_all | solution.py:378
  80.5 19.4 %collective-permute-start.9 = (bf16[256,1536]{1,0:T(8,128)(2,1)S(1)}, bf16[256,1536]{1,0:T(8,128)(2,1)S(1)}, u32[]{:S(2)}, u32[]{:S(2)}) collective-permute-start(bf16[256,1536]{1,0:T(8,128)(2,1)S(1)} %order.1.mine_ref), channel_id=1, source_target_pairs={{0,32},{32,0},{1,33},{33,1},{2,34},{34,2},{3,35},{35,3},{4,36},{36... | collective-permute-start | bytes 2359304 | tf_op jit(solution)/shard_map/ppermute | solution.py:47
  95.4 11.3 %all-to-all-start.2 = ((bf16[4,128,256]{2,1,0:T(8,128)(2,1)}), bf16[4,128,256]{2,1,0:T(8,128)(2,1)S(1)}, u32[]{:S(2)}, u32[]{:S(2)}) async-start(bf16[4,128,256]{2,1,0:T(8,128)(2,1)} %combine.1), calls=%async_computation.2 | async-start | bytes 524288 | tf_op jit(solution)/shard_map/all_to_all | solution.py:378
  99.9 21.9 %copy-start.3 = (bf16[1,128,1024]{2,1,0:T(8,128)(2,1)S(1)}, bf16[1,128,1024]{2,1,0:T(8,128)(2,1)}, u32[]{:S(2)}) copy-start(bf16[1,128,1024]{2,1,0:T(8,128)(2,1)} %param.11) | copy-start | bytes 786436
  107.6 6.4 %collective-permute-start.10 = (f32[136,256]{1,0:T(8,128)S(1)}, f32[136,256]{1,0:T(8,128)S(1)}, u32[]{:S(2)}, u32[]{:S(2)}) collective-permute-start(f32[136,256]{1,0:T(8,128)S(1)} %get-tuple-element.9), channel_id=1, source_target_pairs={{0,32},{32,64},{64,96},{96,128},{128,160},{160,192},{192,224},{224... | collective-permute-start | bytes 417800 | tf_op jit(solution)/shard_map/ppermute | solution.py:33
  109.5 7.8 %collective-permute-start.11 = (f32[136,256]{1,0:T(8,128)S(1)}, f32[136,256]{1,0:T(8,128)S(1)}, u32[]{:S(2)}, u32[]{:S(2)}) collective-permute-start(f32[136,256]{1,0:T(8,128)S(1)} %get-tuple-element.10), channel_id=1, source_target_pairs={{0,64},{32,96},{64,128},{96,160},{128,192},{160,224},{192,256},{22... | collective-permute-start | bytes 417800 | tf_op jit(solution)/shard_map/ppermute | solution.py:33
  118.3 21.9 %all-to-all-start.3 = ((bf16[8,128,256]{2,1,0:T(8,128)(2,1)}), bf16[8,128,256]{2,1,0:T(8,128)(2,1)S(1)}, u32[]{:S(2)}, u32[]{:S(2)}) async-start(bf16[8,128,256]{2,1,0:T(8,128)(2,1)} %finish.1), calls=%async_computation.3 | async-start | bytes 1048576 | tf_op jit(solution)/shard_map/all_to_all | solution.py:378
  121.9 9.0 %collective-permute-start.12 = (bf16[128,256]{1,0:T(8,128)(2,1)S(1)}, bf16[128,256]{1,0:T(8,128)(2,1)S(1)}, u32[]{:S(2)}, u32[]{:S(2)}) collective-permute-start(bf16[128,256]{1,0:T(8,128)(2,1)S(1)} %get-tuple-element.16), channel_id=1, source_target_pairs={{0,8},{8,16},{16,24},{24,0},{1,9},{9,17},{17,25},{25,1},{2,10},{10... | collective-permute-start | bytes 196616 | tf_op jit(solution)/shard_map/ppermute | solution.py:27
  124.4 7.7 %collective-permute-start.13 = (bf16[128,256]{1,0:T(8,128)(2,1)S(1)}, bf16[128,256]{1,0:T(8,128)(2,1)S(1)}, u32[]{:S(2)}, u32[]{:S(2)}) collective-permute-start(bf16[128,256]{1,0:T(8,128)(2,1)S(1)} %get-tuple-element.18), channel_id=1, source_target_pairs={{0,16},{8,24},{16,0},{24,8},{1,17},{9,25},{17,1},{25,9},{2,18},{10... | collective-permute-start | bytes 196616 | tf_op jit(solution)/shard_map/ppermute | solution.py:27
  128.4 6.2 %collective-permute-start.14 = (bf16[128,256]{1,0:T(8,128)(2,1)S(1)}, bf16[128,256]{1,0:T(8,128)(2,1)S(1)}, u32[]{:S(2)}, u32[]{:S(2)}) collective-permute-start(bf16[128,256]{1,0:T(8,128)(2,1)S(1)} %get-tuple-element.15), channel_id=1, source_target_pairs={{0,24},{8,0},{16,8},{24,16},{1,25},{9,1},{17,9},{25,17},{2,26},{10... | collective-permute-start | bytes 196616 | tf_op jit(solution)/shard_map/ppermute | solution.py:27

commit v5 on v4

--- a/solution.py
+++ b/solution.py
@@ -31,12 +31,6 @@
     devices = range(lax.axis_size(axis))
     route = [(i - distance, i) for i in devices if i - distance in devices]
     return lax.ppermute(block, axis, route)
-
-
-def skew(block):
-    ys, zs = lax.axis_size("y"), lax.axis_size("z")
-    route = [(y * zs + (z ^ y), y * zs + z) for y in range(ys) for z in range(zs)]
-    return lax.ppermute(block, ("y", "z"), route)
 
 
 def across(block, axis, mask):
@@ -333,10 +327,12 @@
     query_refs, out_ref = refs[:-1], refs[-1]
     groups, rows, width = out_ref.shape
     pair = 2
+    blocks = [(ref, low) for ref in query_refs for low in range(0, ref.shape[0], rows)]
     for k in range(0, groups, pair):
         for h in range(width // HEAD_DIM):
             cols = head_cols(h)
-            queries = jnp.concatenate([ref[:, cols] for ref in query_refs[k : k + pair]], axis=0)
+            queries = [ref[low : low + rows, cols] for ref, low in blocks[k : k + pair]]
+            queries = jnp.concatenate(queries, axis=0)
             scores = dot_nt(queries, mixed_ref[:, cols])
             peak = jnp.max(scores, axis=1, keepdims=True)
             weights = jnp.exp2((scores - peak) * EXP2_SCALE)
@@ -352,7 +348,7 @@
 
 def decode(place, mixed, queries):
     rows, width = queries[0].shape
-    shape = (len(queries), rows, width)
+    shape = (sum(block.shape[0] for block in queries) // rows, rows, width)
     return pl.pallas_call(
         decode_body,
         grid=(1,),
@@ -370,8 +366,8 @@
     return index.reshape(1).astype(jnp.int32)
 
 
-def join(first, second):
-    return jnp.concatenate([first, second], axis=0)
+def join(*blocks):
+    return jnp.concatenate(blocks, axis=0)
 
 
 def all_to_all(block, axis):
@@ -395,10 +391,9 @@
     mix_t = mix_weight.T
     mix_half = mix_t.shape[1] // 2
     held = lax.dynamic_slice_in_dim(mix_t, core_index * mix_half, mix_half, axis=1)
-    held = skew(held)
     for mask in XORS[:-1]:
-        held = join(held, across(held, "y", mask))
-    brought = across(held, "y", XORS[-1])
+        held = join(held, across(held, "z", mask))
+    brought = across(held, "z", XORS[-1])
 
     rows = latent_queries.shape[0] // 2
     asked = lax.dynamic_slice_in_dim(latent_queries, core_index * rows, rows, axis=0)
@@ -431,7 +426,9 @@
         to = (place + k) % groups
         sent = lax.dynamic_slice_in_dim(output_queries[0], to * width, width, axis=1)
         queries.append(shift(sent, "x", k) if k else sent)
-    mix_mine = order(scalar(lax.axis_index("z") ^ lax.axis_index("y")), held, brought)
+    early = lax.optimization_barrier(join(*queries[1:3]))
+    queries = [queries[0], early] + queries[3:]
+    mix_mine = order(scalar(lax.axis_index("z")), held, brought)
     mix_other = partner(mix_mine)
 
     window = all_to_all(combine(parts, groups), "x")

time: 157 us -> 147 us (0.936)
  the two profiles are of different devices: /device:TPU:48 before, /device:TPU:16 now
where the time goes in v5:
time: 147 us; the launch traced here: 146 us
  starting transfers between devices  68.3 us (46%)
  waiting for transfers between devices  40.1 us (27%)
  Pallas kernels  19.7 us (13%)
  blocking collectives  12.4 us (8%)
  local copies, waits for them, and re-layouts  3.16 us (2%)
  other arithmetic  1.91 us (1%)
    all_to_all x4, waiting for transfers between devices, all_to_all(): return lax.all_to_all(block, axis, 0, 0, tiled=True)  31.3 us
    ppermute x7, starting transfers between devices, shift(): lax.ppermute(block, axis, [(i, (i + distance) % size) for i in range(size)])  22.2 us
    all_to_all x4, starting transfers between devices, all_to_all(): return lax.all_to_all(block, axis, 0, 0, tiled=True)  19.4 us
    ppermute x3, starting transfers between devices, across(): lax.ppermute(block, axis, [(i, i ^ mask) for i in range(lax.axis_size(axi...  17.4 us
    pallas_call x1, Pallas kernels, attend(): pl.pallas_call(attend_body, grid_spec=pltpu.PrefetchScalarGridSpec(num_sc...  13.5 us
    all_to_all x1, blocking collectives, all_to_all(): return lax.all_to_all(block, axis, 0, 0, tiled=True)  12.4 us
    ppermute x2, starting transfers between devices, from_behind(): return lax.ppermute(block, axis, route)  5.4 us
    ppermute x2, waiting for transfers between devices, from_behind(): return lax.ppermute(block, axis, route)  4.45 us
  transfers between devices with their start and end apart: 18, of which 9 were waited for; matrix products, arithmetic and copies ran while one was open for 3% of the time, Pallas kernels for 11%

profile of v5, /device:TPU:16, one launch (start us, length us, event | category | flops | bytes accessed | tf_op | source)
XLA Modules:
  0.0 145.9 jit_solution(2148032527056249585)
XLA Ops:
  0.0 4.8 %collective-permute-start.1 = (bf16[768,512]{1,0:T(8,128)(2,1)}, bf16[768,512]{1,0:T(8,128)(2,1)S(1)}, u32[]{:S(2)}, u32[]{:S(2)}) collective-permute-start(bf16[768,512]{1,0:T(8,128)(2,1)} %bitcast.39), channel_id=1, source_target_pairs={{0,24},{8,0},{16,8},{24,16},{1,25},{9,1},{17,9},{25,17},{2,26},{10... | collective-permute-start | bytes 2359304 | tf_op jit(solution)/shard_map/ppermute | solution.py:27
  6.8 10.9 %collective-permute-start.5 = (bf16[32,1536]{1,0:T(8,128)(2,1)S(1)}, bf16[32,1536]{1,0:T(8,128)(2,1)S(1)}, u32[]{:S(2)}, u32[]{:S(2)}) collective-permute-start(bf16[32,1536]{1,0:T(8,128)(2,1)S(1)} %dynamic-slice_bitcast_fusion), channel_id=1, source_target_pairs={{0,4},{1,5},{2,6},{3,7},{4,0},{5,1},{6,2},{7,3},{8,12},{9,13},{10,... | collective-permute-start | bytes 294920 | tf_op jit(solution)/shard_map/ppermute | solution.py:37
  19.2 7.6 %all-to-all-start = ((bf16[32,16,256]{2,1,0:T(8,128)(2,1)}), bf16[32,16,256]{2,1,0:T(8,128)(2,1)S(1)}, u32[]{:S(2)}, u32[]{:S(2)}) async-start(bf16[32,16,256]{2,1,0:T(8,128)(2,1)} %bitcast.6), calls=%async_computation | async-start | bytes 524288 | tf_op jit(solution)/shard_map/all_to_all | solution.py:374
  26.9 4.6 %collective-permute-start.6 = (bf16[64,1536]{1,0:T(8,128)(2,1)S(1)}, bf16[64,1536]{1,0:T(8,128)(2,1)}, u32[]{:S(2)}, u32[]{:S(2)}) collective-permute-start(bf16[64,1536]{1,0:T(8,128)(2,1)S(1)} %pad_maximum_fusion.1), channel_id=1, source_target_pairs={{0,2},{1,3},{2,0},{3,1},{4,6},{5,7},{6,4},{7,5},{8,10},{9,11},{10,... | collective-permute-start | bytes 589832 | tf_op jit(solution)/shard_map/ppermute | solution.py:37
  32.2 4.6 %collective-permute-start.3 = (bf16[384,512]{1,0:T(8,128)(2,1)}, bf16[384,512]{1,0:T(8,128)(2,1)}, u32[]{:S(2)}, u32[]{:S(2)}) collective-permute-start(bf16[384,512]{1,0:T(8,128)(2,1)} %slice.40), channel_id=1, source_target_pairs={{0,24},{8,0},{16,8},{24,16},{1,25},{9,1},{17,9},{25,17},{2,26},{10... | collective-permute-start | bytes 1179656 | tf_op jit(solution)/shard_map/ppermute | solution.py:27
  39.6 4.9 %all-to-all-done = bf16[32,16,256]{2,1,0:T(8,128)(2,1)S(1)} async-done(((bf16[32,16,256]{2,1,0:T(8,128)(2,1)}), bf16[32,16,256]{2,1,0:T(8,128)(2,1)S(1)}, u32[]{:S(2)}, u32[]{:S(2)}) %all-to-all-start) | async-done | bytes 262176 | tf_op jit(solution)/shard_map/all_to_all | solution.py:374
  47.4 1.9 %collective-permute-start.7 = (bf16[128,1536]{1,0:T(8,128)(2,1)S(1)}, bf16[128,1536]{1,0:T(8,128)(2,1)}, u32[]{:S(2)}, u32[]{:S(2)}) collective-permute-start(bf16[128,1536]{1,0:T(8,128)(2,1)S(1)} %pad_maximum_fusion.first_ref), channel_id=1, source_target_pairs={{0,1},{1,0},{2,3},{3,2},{4,5},{5,4},{6,7},{7,6},{8,9},{9,8},{10,11... | collective-permute-start | bytes 1179656 | tf_op jit(solution)/shard_map/ppermute | solution.py:37
  50.1 13.5 %attend.1 = bf16[8,136,256]{2,1,0:T(8,128)(2,1)} custom-call(s32[2]{0:T(128)S(1)} %pad_add_fusion.spot_ref, bf16[512,256]{1,0:T(8,128)(2,1)S(1)} %bitcast.38, bf16[512,256]{1,0:T(8,128)(2,1)S(1)} %collective-permute-done.other_ref, bf16[512,2048]{1,0:T(8,128)(2,1)} %value_ref.1, bf16[512,2048]{1,0:T(8,128)(2,1)} %value_ref.1, bf16[768,512]{1,0:T(8,128)(2,1)S(1)} %bitcast.41, ...), custom_call_target="tpu_custom_call" | custom-call | tf_op jit(solution)/shard_map/attend/pallas_call | solution.py:151
  63.6 4.9 %all-to-all-start.1 = ((bf16[8,136,256]{2,1,0:T(8,128)(2,1)}), bf16[8,136,256]{2,1,0:T(8,128)(2,1)S(1)}, u32[]{:S(2)}, u32[]{:S(2)}) async-start(bf16[8,136,256]{2,1,0:T(8,128)(2,1)} %attend.1), calls=%async_computation.1 | async-start | bytes 1114112 | tf_op jit(solution)/shard_map/all_to_all | solution.py:374
  69.6 1.9 %collective-permute-start.8 = (bf16[256,1536]{1,0:T(8,128)(2,1)S(1)}, bf16[256,1536]{1,0:T(8,128)(2,1)S(1)}, u32[]{:S(2)}, u32[]{:S(2)}) collective-permute-start(bf16[256,1536]{1,0:T(8,128)(2,1)S(1)} %order.1.mine_ref), channel_id=1, source_target_pairs={{0,32},{32,0},{1,33},{33,1},{2,34},{34,2},{3,35},{35,3},{4,36},{36... | collective-permute-start | bytes 2359304 | tf_op jit(solution)/shard_map/ppermute | solution.py:41
  71.5 14.2 %all-to-all-done.1.part_ref = bf16[8,136,256]{2,1,0:T(8,128)(2,1)S(1)} async-done(((bf16[8,136,256]{2,1,0:T(8,128)(2,1)}), bf16[8,136,256]{2,1,0:T(8,128)(2,1)S(1)}, u32[]{:S(2)}, u32[]{:S(2)}) %all-to-all-start.1) | async-done | bytes 557088 | tf_op jit(solution)/shard_map/all_to_all | solution.py:374
  87.0 3.4 %all-to-all-start.2 = ((bf16[4,128,256]{2,1,0:T(8,128)(2,1)}), bf16[4,128,256]{2,1,0:T(8,128)(2,1)S(1)}, u32[]{:S(2)}, u32[]{:S(2)}) async-start(bf16[4,128,256]{2,1,0:T(8,128)(2,1)} %combine.1), calls=%async_computation.2 | async-start | bytes 524288 | tf_op jit(solution)/shard_map/all_to_all | solution.py:374
  90.5 6.6 %all-to-all-done.2.rows_ref = bf16[4,128,256]{2,1,0:T(8,128)(2,1)S(1)} async-done(((bf16[4,128,256]{2,1,0:T(8,128)(2,1)}), bf16[4,128,256]{2,1,0:T(8,128)(2,1)S(1)}, u32[]{:S(2)}, u32[]{:S(2)}) %all-to-all-start.2) | async-done | bytes 262176 | tf_op jit(solution)/shard_map/all_to_all | solution.py:374
  97.9 3.5 %collective-permute-start.10 = (f32[136,256]{1,0:T(8,128)S(1)}, f32[136,256]{1,0:T(8,128)S(1)}, u32[]{:S(2)}, u32[]{:S(2)}) collective-permute-start(f32[136,256]{1,0:T(8,128)S(1)} %get-tuple-element.10), channel_id=1, source_target_pairs={{0,64},{32,96},{64,128},{96,160},{128,192},{160,224},{192,256},{22... | collective-permute-start | bytes 417800 | tf_op jit(solution)/shard_map/ppermute | solution.py:33
  101.4 1.9 %collective-permute-start.9 = (f32[136,256]{1,0:T(8,128)S(1)}, f32[136,256]{1,0:T(8,128)S(1)}, u32[]{:S(2)}, u32[]{:S(2)}) collective-permute-start(f32[136,256]{1,0:T(8,128)S(1)} %get-tuple-element.9), channel_id=1, source_target_pairs={{0,32},{32,64},{64,96},{96,128},{128,160},{160,192},{192,224},{224... | collective-permute-start | bytes 417800 | tf_op jit(solution)/shard_map/ppermute | solution.py:33
  104.8 2.9 %collective-permute-done.9.refs_1_ = f32[136,256]{1,0:T(8,128)S(1)} collective-permute-done((f32[136,256]{1,0:T(8,128)S(1)}, f32[136,256]{1,0:T(8,128)S(1)}, u32[]{:S(2)}, u32[]{:S(2)}) %collective-permute-start.9) | collective-permute-done | bytes 139296 | tf_op jit(solution)/shard_map/ppermute | solution.py:33
  108.8 3.5 %all-to-all-start.3 = ((bf16[8,128,256]{2,1,0:T(8,128)(2,1)}), bf16[8,128,256]{2,1,0:T(8,128)(2,1)S(1)}, u32[]{:S(2)}, u32[]{:S(2)}) async-start(bf16[8,128,256]{2,1,0:T(8,128)(2,1)} %finish.1), calls=%async_computation.3 | async-start | bytes 1048576 | tf_op jit(solution)/shard_map/all_to_all | solution.py:374
  112.4 2.5 %collective-permute-start.11 = (bf16[128,256]{1,0:T(8,128)(2,1)S(1)}, bf16[128,256]{1,0:T(8,128)(2,1)S(1)}, u32[]{:S(2)}, u32[]{:S(2)}) collective-permute-start(bf16[128,256]{1,0:T(8,128)(2,1)S(1)} %get-tuple-element.16), channel_id=1, source_target_pairs={{0,8},{8,16},{16,24},{24,0},{1,9},{9,17},{17,25},{25,1},{2,10},{10... | collective-permute-start | bytes 196616 | tf_op jit(solution)/shard_map/ppermute | solution.py:27
  114.9 4.0 %collective-permute-start.12 = (bf16[128,256]{1,0:T(8,128)(2,1)S(1)}, bf16[128,256]{1,0:T(8,128)(2,1)S(1)}, u32[]{:S(2)}, u32[]{:S(2)}) collective-permute-start(bf16[128,256]{1,0:T(8,128)(2,1)S(1)} %get-tuple-element.18), channel_id=1, source_target_pairs={{0,16},{8,24},{16,0},{24,8},{1,17},{9,25},{17,1},{25,9},{2,18},{10... | collective-permute-start | bytes 196616 | tf_op jit(solution)/shard_map/ppermute | solution.py:27
  118.9 2.5 %collective-permute-start.13 = (bf16[128,256]{1,0:T(8,128)(2,1)S(1)}, bf16[128,256]{1,0:T(8,128)(2,1)S(1)}, u32[]{:S(2)}, u32[]{:S(2)}) collective-permute-start(bf16[128,256]{1,0:T(8,128)(2,1)S(1)} %get-tuple-element.15), channel_id=1, source_target_pairs={{0,24},{8,0},{16,8},{24,16},{1,25},{9,1},{17,9},{25,17},{2,26},{10... | collective-permute-start | bytes 196616 | tf_op jit(solution)/shard_map/ppermute | solution.py:27
  122.5 2.5 %collective-permute-done.13.refs_2_ = bf16[128,256]{1,0:T(8,128)(2,1)S(1)} collective-permute-done((bf16[128,256]{1,0:T(8,128)(2,1)S(1)}, bf16[128,256]{1,0:T(8,128)(2,1)S(1)}, u32[]{:S(2)}, u32[]{:S(2)}) %collective-permute-start.13) | collective-permute-done | bytes 65568 | tf_op jit(solution)/shard_map/ppermute | solution.py:27
  125.0 5.6 %all-to-all-done.3 = bf16[8,128,256]{2,1,0:T(8,128)(2,1)S(1)} async-done(((bf16[8,128,256]{2,1,0:T(8,128)(2,1)}), bf16[8,128,256]{2,1,0:T(8,128)(2,1)S(1)}, u32[]{:S(2)}, u32[]{:S(2)}) %all-to-all-start.3) | async-done | bytes 524320 | tf_op jit(solution)/shard_map/all_to_all | solution.py:374
  130.6 2.0 %decode.1 = f32[4,128,256]{2,1,0:T(8,128)S(1)} custom-call(s32[1]{0:T(128)} %bitcast.place_ref, bf16[1024,256]{1,0:T(8,128)(2,1)S(1)} %bitcast.36, bf16[128,256]{1,0:T(8,128)(2,1)S(1)} %get-tuple-element.17.refs_0_, bf16[256,256]{1,0:T(8,128)(2,1)S(1)} %pad_maximum_fusion.2.refs_1_, bf16[128,256]{1,0:T(8,128)(2,1)S(1)} %collective-permute-done.13.refs_2_), custom_call_target="tpu_custom_call" | custom-call | tf_op jit(solution)/shard_map/decode/pallas_call | solution.py:352
  132.7 12.4 %all_to_all.25 = f32[4,128,256]{2,1,0:T(8,128)S(1)} all-to-all(f32[4,128,256]{2,1,0:T(8,128)S(1)} %decode.1), channel_id=1, replica_groups=mesh['y'=8,'core'=2,'x'=4,'z'=8] {'x'}, dimensions={0} | all-to-all | bytes 1048576 | tf_op jit(solution)/shard_map/all_to_all | solution.py:374
  (40 shorter events, 18.3 us)
Async XLA Ops:
  0.0 6.7 %copy-start = (bf16[3072,32]{0,1:T(8,128)(2,1)S(1)}, bf16[3072,32]{0,1:T(8,128)(2,1)}, u32[]{:S(2)}) copy-start(bf16[3072,32]{0,1:T(8,128)(2,1)} %param.10) | copy-start | bytes 589828
  0.0 50.1 %copy-start.1 = (bf16[1,768,512]{2,1,0:T(8,128)(2,1)S(1)}, bf16[1,768,512]{2,1,0:T(8,128)(2,1)}, u32[]{:S(2)}) copy-start(bf16[1,768,512]{2,1,0:T(8,128)(2,1)} %param.6) | copy-start | bytes 2359300
  0.0 31.5 %collective-permute-start.1 = (bf16[768,512]{1,0:T(8,128)(2,1)}, bf16[768,512]{1,0:T(8,128)(2,1)S(1)}, u32[]{:S(2)}, u32[]{:S(2)}) collective-permute-start(bf16[768,512]{1,0:T(8,128)(2,1)} %bitcast.39), channel_id=1, source_target_pairs={{0,24},{8,0},{16,8},{24,16},{1,25},{9,1},{17,9},{25,17},{2,26},{10... | collective-permute-start | bytes 2359304 | tf_op jit(solution)/shard_map/ppermute | solution.py:27
  4.8 32.1 %collective-permute-start.2 = (bf16[768,512]{1,0:T(8,128)(2,1)}, bf16[768,512]{1,0:T(8,128)(2,1)S(1)}, u32[]{:S(2)}, u32[]{:S(2)}) collective-permute-start(bf16[768,512]{1,0:T(8,128)(2,1)} %bitcast.40), channel_id=1, source_target_pairs={{0,8},{8,16},{16,24},{24,0},{1,9},{9,17},{17,25},{25,1},{2,10},{10... | collective-permute-start | bytes 2359304 | tf_op jit(solution)/shard_map/ppermute | solution.py:27
  6.8 20.1 %collective-permute-start.5 = (bf16[32,1536]{1,0:T(8,128)(2,1)S(1)}, bf16[32,1536]{1,0:T(8,128)(2,1)S(1)}, u32[]{:S(2)}, u32[]{:S(2)}) collective-permute-start(bf16[32,1536]{1,0:T(8,128)(2,1)S(1)} %dynamic-slice_bitcast_fusion), channel_id=1, source_target_pairs={{0,4},{1,5},{2,6},{3,7},{4,0},{5,1},{6,2},{7,3},{8,12},{9,13},{10,... | collective-permute-start | bytes 294920 | tf_op jit(solution)/shard_map/ppermute | solution.py:37
  19.2 25.3 %all-to-all-start = ((bf16[32,16,256]{2,1,0:T(8,128)(2,1)}), bf16[32,16,256]{2,1,0:T(8,128)(2,1)S(1)}, u32[]{:S(2)}, u32[]{:S(2)}) async-start(bf16[32,16,256]{2,1,0:T(8,128)(2,1)} %bitcast.6), calls=%async_computation | async-start | bytes 524288 | tf_op jit(solution)/shard_map/all_to_all | solution.py:374
  26.9 19.6 %collective-permute-start.6 = (bf16[64,1536]{1,0:T(8,128)(2,1)S(1)}, bf16[64,1536]{1,0:T(8,128)(2,1)}, u32[]{:S(2)}, u32[]{:S(2)}) collective-permute-start(bf16[64,1536]{1,0:T(8,128)(2,1)S(1)} %pad_maximum_fusion.1), channel_id=1, source_target_pairs={{0,2},{1,3},{2,0},{3,1},{4,6},{5,7},{6,4},{7,5},{8,10},{9,11},{10,... | collective-permute-start | bytes 589832 | tf_op jit(solution)/shard_map/ppermute | solution.py:37
  32.2 17.2 %collective-permute-start.3 = (bf16[384,512]{1,0:T(8,128)(2,1)}, bf16[384,512]{1,0:T(8,128)(2,1)}, u32[]{:S(2)}, u32[]{:S(2)}) collective-permute-start(bf16[384,512]{1,0:T(8,128)(2,1)} %slice.40), channel_id=1, source_target_pairs={{0,24},{8,0},{16,8},{24,16},{1,25},{9,1},{17,9},{25,17},{2,26},{10... | collective-permute-start | bytes 1179656 | tf_op jit(solution)/shard_map/ppermute | solution.py:27
  37.7 12.4 %collective-permute-start.4 = (bf16[384,512]{1,0:T(8,128)(2,1)}, bf16[384,512]{1,0:T(8,128)(2,1)}, u32[]{:S(2)}, u32[]{:S(2)}) collective-permute-start(bf16[384,512]{1,0:T(8,128)(2,1)} %slice.41), channel_id=1, source_target_pairs={{0,8},{8,16},{16,24},{24,0},{1,9},{9,17},{17,25},{25,1},{2,10},{10... | collective-permute-start | bytes 1179656 | tf_op jit(solution)/shard_map/ppermute | solution.py:27
  44.5 4.9 %collective-permute-start = (bf16[512,256]{1,0:T(8,128)(2,1)S(1)}, bf16[512,256]{1,0:T(8,128)(2,1)S(1)}, u32[]{:S(2)}, u32[]{:S(2)}) collective-permute-start(bf16[512,256]{1,0:T(8,128)(2,1)S(1)} %bitcast.37), channel_id=1, source_target_pairs={{0,32},{32,0},{1,33},{33,1},{2,34},{34,2},{3,35},{35,3},{4,36},{36... | collective-permute-start | bytes 786440 | tf_op jit(solution)/shard_map/ppermute | solution.py:41
  47.4 21.1 %collective-permute-start.7 = (bf16[128,1536]{1,0:T(8,128)(2,1)S(1)}, bf16[128,1536]{1,0:T(8,128)(2,1)}, u32[]{:S(2)}, u32[]{:S(2)}) collective-permute-start(bf16[128,1536]{1,0:T(8,128)(2,1)S(1)} %pad_maximum_fusion.first_ref), channel_id=1, source_target_pairs={{0,1},{1,0},{2,3},{3,2},{4,5},{5,4},{6,7},{7,6},{8,9},{9,8},{10,11... | collective-permute-start | bytes 1179656 | tf_op jit(solution)/shard_map/ppermute | solution.py:37
  63.6 33.5 %copy-start.2 = (f32[3072]{0:T(1024)S(1)}, f32[3072]{0:T(1024)}, u32[]{:S(2)}) copy-start(f32[3072]{0:T(1024)} %param.9) | copy-start | bytes 36868
  63.6 22.1 %all-to-all-start.1 = ((bf16[8,136,256]{2,1,0:T(8,128)(2,1)}), bf16[8,136,256]{2,1,0:T(8,128)(2,1)S(1)}, u32[]{:S(2)}, u32[]{:S(2)}) async-start(bf16[8,136,256]{2,1,0:T(8,128)(2,1)} %attend.1), calls=%async_computation.1 | async-start | bytes 1114112 | tf_op jit(solution)/shard_map/all_to_all | solution.py:374
  69.6 20.9 %collective-permute-start.8 = (bf16[256,1536]{1,0:T(8,128)(2,1)S(1)}, bf16[256,1536]{1,0:T(8,128)(2,1)S(1)}, u32[]{:S(2)}, u32[]{:S(2)}) collective-permute-start(bf16[256,1536]{1,0:T(8,128)(2,1)S(1)} %order.1.mine_ref), channel_id=1, source_target_pairs={{0,32},{32,0},{1,33},{33,1},{2,34},{34,2},{3,35},{35,3},{4,36},{36... | collective-permute-start | bytes 2359304 | tf_op jit(solution)/shard_map/ppermute | solution.py:41
  87.0 10.1 %all-to-all-start.2 = ((bf16[4,128,256]{2,1,0:T(8,128)(2,1)}), bf16[4,128,256]{2,1,0:T(8,128)(2,1)S(1)}, u32[]{:S(2)}, u32[]{:S(2)}) async-start(bf16[4,128,256]{2,1,0:T(8,128)(2,1)} %combine.1), calls=%async_computation.2 | async-start | bytes 524288 | tf_op jit(solution)/shard_map/all_to_all | solution.py:374
  90.4 21.9 %copy-start.3 = (bf16[1,128,1024]{2,1,0:T(8,128)(2,1)S(1)}, bf16[1,128,1024]{2,1,0:T(8,128)(2,1)}, u32[]{:S(2)}) copy-start(bf16[1,128,1024]{2,1,0:T(8,128)(2,1)} %param.11) | copy-start | bytes 786436
  97.9 6.9 %collective-permute-start.10 = (f32[136,256]{1,0:T(8,128)S(1)}, f32[136,256]{1,0:T(8,128)S(1)}, u32[]{:S(2)}, u32[]{:S(2)}) collective-permute-start(f32[136,256]{1,0:T(8,128)S(1)} %get-tuple-element.10), channel_id=1, source_target_pairs={{0,64},{32,96},{64,128},{96,160},{128,192},{160,224},{192,256},{22... | collective-permute-start | bytes 417800 | tf_op jit(solution)/shard_map/ppermute | solution.py:33
  101.4 6.4 %collective-permute-start.9 = (f32[136,256]{1,0:T(8,128)S(1)}, f32[136,256]{1,0:T(8,128)S(1)}, u32[]{:S(2)}, u32[]{:S(2)}) collective-permute-start(f32[136,256]{1,0:T(8,128)S(1)} %get-tuple-element.9), channel_id=1, source_target_pairs={{0,32},{32,64},{64,96},{96,128},{128,160},{160,192},{192,224},{224... | collective-permute-start | bytes 417800 | tf_op jit(solution)/shard_map/ppermute | solution.py:33
  108.8 21.8 %all-to-all-start.3 = ((bf16[8,128,256]{2,1,0:T(8,128)(2,1)}), bf16[8,128,256]{2,1,0:T(8,128)(2,1)S(1)}, u32[]{:S(2)}, u32[]{:S(2)}) async-start(bf16[8,128,256]{2,1,0:T(8,128)(2,1)} %finish.1), calls=%async_computation.3 | async-start | bytes 1048576 | tf_op jit(solution)/shard_map/all_to_all | solution.py:374
  112.4 9.0 %collective-permute-start.11 = (bf16[128,256]{1,0:T(8,128)(2,1)S(1)}, bf16[128,256]{1,0:T(8,128)(2,1)S(1)}, u32[]{:S(2)}, u32[]{:S(2)}) collective-permute-start(bf16[128,256]{1,0:T(8,128)(2,1)S(1)} %get-tuple-element.16), channel_id=1, source_target_pairs={{0,8},{8,16},{16,24},{24,0},{1,9},{9,17},{17,25},{25,1},{2,10},{10... | collective-permute-start | bytes 196616 | tf_op jit(solution)/shard_map/ppermute | solution.py:27
  114.9 7.7 %collective-permute-start.12 = (bf16[128,256]{1,0:T(8,128)(2,1)S(1)}, bf16[128,256]{1,0:T(8,128)(2,1)S(1)}, u32[]{:S(2)}, u32[]{:S(2)}) collective-permute-start(bf16[128,256]{1,0:T(8,128)(2,1)S(1)} %get-tuple-element.18), channel_id=1, source_target_pairs={{0,16},{8,24},{16,0},{24,8},{1,17},{9,25},{17,1},{25,9},{2,18},{10... | collective-permute-start | bytes 196616 | tf_op jit(solution)/shard_map/ppermute | solution.py:27
  118.9 6.2 %collective-permute-start.13 = (bf16[128,256]{1,0:T(8,128)(2,1)S(1)}, bf16[128,256]{1,0:T(8,128)(2,1)S(1)}, u32[]{:S(2)}, u32[]{:S(2)}) collective-permute-start(bf16[128,256]{1,0:T(8,128)(2,1)S(1)} %get-tuple-element.15), channel_id=1, source_target_pairs={{0,24},{8,0},{16,8},{24,16},{1,25},{9,1},{17,9},{25,17},{2,26},{10... | collective-permute-start | bytes 196616 | tf_op jit(solution)/shard_map/ppermute | solution.py:27
